TPU v7x, 32 devices: a whole 2x2x4 slice. The times are simulated.
32 devices in a mesh: dp: 2 (over core), head: 4 (over y, x), seq: 4 (over z).
Axes of the slice: x: 2, y: 2, z: 4, core: 2. Of those that a mesh axis runs over, the one named last changes fastest.
Arguments:
- layer_input: bfloat16 [2, 2048, 2048], P('dp', 'seq'), may hold values from -6 to 6
- head_values: bfloat16 [2, 2048, 2048], P('dp', 'seq', 'head'), may hold values from -6 to 6
- dt_raw: float32 [2, 32, 2048], P('dp', 'head', 'seq'), may hold values from -2 to 40
- w_bc: bfloat16 [2048, 128], replicated, may hold values from -0.015625 to 0.015625
- decay_rate: float32 [32], P('head'), may hold values from 0.0068359375 to 2
- dt_bias: float32 [32], P('head'), may hold values from -4.5 to -3.5
- skip_gain: float32 [32], P('head'), may hold values from 0.5 to 1.5
- grad_y: bfloat16 [2, 2048, 2048], P('dp', 'seq', 'head'), may hold values from -6 to 6
Outputs:
- y_out: bfloat16 [2, 2048, 2048], P('dp', 'seq', 'head')
- grad_values: bfloat16 [2, 2048, 2048], P('dp', 'seq', 'head')
- grad_input: bfloat16 [2, 2048, 2048], P('dp', 'seq')
- grad_w_bc: float32 [2048, 128], P(('dp', 'seq'))
All inputs are finite; a program needn't handle non-finite values.
Results may differ from a plain program's by a relative error of at most 0.013.
Values may be sent and summed in bfloat16 or wider, within the bound.
No kernel may reach another device: no remote copies, remote signals or barrier semaphores. Data moves between devices by JAX's collectives and lax.ppermute only.
A program may use at most 320 MiB of HBM per device.

v0:
```python
import jax
import jax.numpy as jnp
from jax import lax
from jax.sharding import PartitionSpec as P

maximum_level = lax.Precision.HIGHEST


def carried_in(x, axis, combine, identity, reverse):
    size, here = (lax.axis_size(axis), lax.axis_index(axis))
    everything = jax.tree.map(
        lambda part, kind: lax.all_gather(part.astype(kind), axis), x, (jnp.bfloat16, jnp.bfloat16)
    )
    start = jax.tree.map(
        lambda part, zero: jnp.broadcast_to(jnp.asarray(zero, part.dtype), part.shape), x, identity
    )

    def step(k, before):
        at = size - 1 - k if reverse else k
        reached = at > here if reverse else at < here
        new = combine(
            before, jax.tree.map(lambda part, own: part[at].astype(own.dtype), everything, x)
        )
        return jax.tree.map(lambda a, b: jnp.where(reached, a, b), new, before)

    return lax.fori_loop(0, size, step, start)


def spread_heads(vector):
    return vector[None, :, None, None]


def combine_states(earlier, later_part):
    factor_vec = later_part[0]
    return (earlier[0] * factor_vec, spread_heads(factor_vec) * earlier[1] + later_part[1])


def head_state(scaled_keys, value_matrix):
    return jnp.einsum("qgz,qgn->gzn", scaled_keys, value_matrix, precision=maximum_level)


def spread_state(value_scaled, key_rows):
    return jnp.einsum("shp,sn->hnp", value_scaled, key_rows, precision=maximum_level)


def shared_query(query_rows, state):
    return jnp.einsum("tn,hnp->thp", query_rows, state, precision=maximum_level)


def head_query(query_rows, state):
    return jnp.einsum("thp,hnp->tn", query_rows, state, precision=maximum_level)


def per_device(layer_input, head_values, dt_raw, w_bc, decay_rate, dt_bias, skip_gain, grad_y):
    tokens = layer_input[0]
    head_count = decay_rate.shape[0]
    length = tokens.shape[0]
    state_dim = w_bc.shape[1] // 2
    head_dim = head_values.shape[2] // head_count
    values_x = head_values[0].reshape(length, head_count, head_dim)
    cotangent = grad_y[0].reshape(length, head_count, head_dim)
    log_step = -decay_rate[:, None] * jax.nn.softplus(dt_raw[0] + dt_bias[:, None])
    cum_log = jnp.cumsum(log_step, axis=1)
    prev_log = cum_log - log_step
    final_logarithm = cum_log[:, -1]
    projected = jnp.dot(tokens, w_bc, preferred_element_type=jnp.float32).astype(jnp.bfloat16)
    b_mat = projected[:, :state_dim]
    c_mat = projected[:, state_dim:]
    row_index = jnp.arange(length)[:, None]
    col_index = jnp.arange(length)[None, :]
    state_scores = jnp.einsum("tn,sn->ts", c_mat, b_mat, preferred_element_type=jnp.float32)

    def head_block(totals, inputs):
        cum_head, prev_head, x_head, g_head = inputs
        diff_fwd = cum_head[:, None] - cum_head[None, :]
        diff_bwd = prev_head[None, :] - prev_head[:, None]
        exponent = jnp.minimum(jnp.where(col_index < row_index, diff_fwd, diff_bwd), 0.0)
        kernel = jnp.where(col_index == row_index, 0.0, jnp.exp(exponent))
        weights_main = (state_scores * kernel).astype(jnp.bfloat16)
        value_scores = jnp.dot(g_head, x_head.T, preferred_element_type=jnp.float32)
        weights_grad = (value_scores * kernel).astype(jnp.bfloat16)
        y_head = jnp.dot(weights_main, x_head, preferred_element_type=jnp.float32)
        gv_head = jnp.dot(weights_main.T, g_head, preferred_element_type=jnp.float32)
        gc_total = totals[0] + jnp.dot(weights_grad, b_mat, preferred_element_type=jnp.float32)
        gb_total = totals[1] + jnp.dot(weights_grad.T, c_mat, preferred_element_type=jnp.float32)
        return ((gc_total, gb_total), (y_head, gv_head))

    zero_rows = jnp.zeros((length, state_dim), jnp.float32)
    head_inputs = (cum_log, prev_log, values_x.transpose(1, 0, 2), cotangent.transpose(1, 0, 2))
    (local_gc, local_gb), (heads_y, heads_gv) = lax.scan(
        head_block, (zero_rows, zero_rows), head_inputs
    )
    local_y = heads_y.transpose(1, 0, 2)
    local_gv = heads_gv.transpose(1, 0, 2)
    b_float = b_mat.astype(jnp.float32)
    c_float = c_mat.astype(jnp.float32)
    x_float = values_x.astype(jnp.float32)
    g_float = cotangent.astype(jnp.float32)
    up_cum = jnp.exp(cum_log).T
    up_prev = jnp.exp(prev_log).T
    down_cum = jnp.exp(final_logarithm[:, None] - cum_log).T
    down_prev = jnp.exp(final_logarithm[:, None] - prev_log).T
    next_main = head_state(b_float[:, None, :] * down_cum[:, :, None], x_float)
    prior_main = head_state(b_float[:, None, :] * up_prev[:, :, None], x_float)
    next_back = head_state(c_float[:, None, :] * down_prev[:, :, None], g_float)
    prior_back = head_state(c_float[:, None, :] * up_cum[:, :, None], g_float)
    next_gc = spread_state(x_float * down_cum[:, :, None], b_float)
    prior_gc = spread_state(x_float * up_prev[:, :, None], b_float)
    next_gb = spread_state(g_float * down_prev[:, :, None], c_float)
    prior_gb = spread_state(g_float * up_cum[:, :, None], c_float)
    stacked_next = jnp.stack([next_main, next_back, next_gc, next_gb])
    stacked_prior = jnp.stack([prior_main, prior_back, prior_gc, prior_gb])
    state_pick = (0, 1, 2, 3)
    decay_total = jnp.exp(final_logarithm)
    unit_decay = jnp.ones_like(decay_total)
    zero_stack = jnp.zeros_like(stacked_next)
    scanned_next = carried_in(
        (decay_total, stacked_next), "seq", combine_states, (unit_decay, zero_stack), False
    )
    scanned_prior = carried_in(
        (decay_total, stacked_prior), "seq", combine_states, (unit_decay, zero_stack), True
    )
    contribution_earlier = scanned_next[1]
    contribution_later = scanned_prior[1]
    before_list = [contribution_earlier[slot_index] for slot_index in state_pick]
    after_list = [contribution_later[slot_index] for slot_index in state_pick]
    carry_y = (
        shared_query(c_float, before_list[0]) * up_cum[:, :, None]
        + shared_query(c_float, after_list[0]) * down_prev[:, :, None]
    )
    carry_gv = (
        shared_query(b_float, before_list[1]) * up_prev[:, :, None]
        + shared_query(b_float, after_list[1]) * down_cum[:, :, None]
    )
    carry_gc = head_query(g_float * up_cum[:, :, None], before_list[2]) + head_query(
        g_float * down_prev[:, :, None], after_list[2]
    )
    carry_gb = head_query(x_float * up_prev[:, :, None], before_list[3]) + head_query(
        x_float * down_cum[:, :, None], after_list[3]
    )
    y_out = (local_y + carry_y + skip_gain[None, :, None] * x_float).astype(jnp.bfloat16)
    grad_values = (local_gv + carry_gv + skip_gain[None, :, None] * g_float).astype(jnp.bfloat16)
    partial_bc = jnp.concatenate([local_gb + carry_gb, local_gc + carry_gc], axis=1)
    summed_bc = lax.psum(partial_bc.astype(jnp.bfloat16), "head")
    grad_input = jnp.einsum(
        "tk,dk->td", summed_bc, w_bc, preferred_element_type=jnp.float32
    ).astype(jnp.bfloat16)
    group_count = lax.axis_size("dp") * lax.axis_size("seq")
    total_tokens = group_count * length
    weight_part = lax.psum_scatter(
        jnp.einsum("td,tk->dk", tokens, summed_bc, preferred_element_type=jnp.float32),
        ("dp", "seq"),
        scatter_dimension=0,
        tiled=True,
    )
    grad_w_bc = weight_part / total_tokens
    return (
        y_out.reshape(1, length, head_count * head_dim),
        grad_values.reshape(1, length, head_count * head_dim),
        grad_input[None],
        grad_w_bc,
    )


def solution(mesh):
    in_specs = (
        P("dp", "seq", None),
        P("dp", "seq", "head"),
        P("dp", "head", "seq"),
        P(),
        P("head"),
        P("head"),
        P("head"),
        P("dp", "seq", "head"),
    )
    out_specs = (
        P("dp", "seq", "head"),
        P("dp", "seq", "head"),
        P("dp", "seq", None),
        P(("dp", "seq"), None),
    )
    return jax.shard_map(
        per_device, mesh=mesh, in_specs=in_specs, out_specs=out_specs, check_vma=False
    )
```

profile of v0, /device:TPU:0, one launch (start us, length us, event | category | flops | bytes accessed | tf_op | source)
XLA Modules:
  0.0 231.7 jit_solution(15547888984841466233)
XLA Ops:
  16.3 2.2 fusion.33
  30.8 56.7 %while.50 = (s32[]{:T(128)}, f32[512,64]{0,1:T(8,128)S(1)}, f32[512,64]{0,1:T(8,128)S(1)}, f32[8,512,64]{1,2,0:T(8,128)}, f32[8,512,64]{1,2,0:T(8,128)}, /*index...) while((s32[]{:T(128)}, f32[512,64]{0,1:T(8,128)S(1)}, ...), condition=%wide.region_3.4_spmd.clone.clone, body=%wide.region_2.3_spmd.clone.clone.sunk | while | flops 174981120 | bytes 13274344 | solution.py:90
  33.5 2.4 %fusion.139 = f32[8,512,64]{1,2,0:T(8,128)} fusion(f32[8,512,64]{1,2,0:T(8,128)} %get-tuple-element.700, s32[]{:T(128)} %get-tuple-element.697, bf16[8,512,64]{1,2,0:T(8,128)(2,1)} %copy-done.1, f32[512,512]{1,0:T(8,128)} %get-tuple-element.722, f32[512]{0:T(512)S(1)} %bitcast.267, f32[512]{0:T(512)S(1)} %bitcast.270), kind=kOutput, calls=%fused_computation.15.clone.1 | convolution fusion | flops 35913728 | bytes 1254400 | tf_op jit(solution)/shard_map/while/body/eval_jaxpr/dot_general | solution.py:82
  40.6 2.4 %fusion.139 = f32[8,512,64]{1,2,0:T(8,128)} fusion(f32[8,512,64]{1,2,0:T(8,128)} %get-tuple-element.700, s32[]{:T(128)} %get-tuple-element.697, bf16[8,512,64]{1,2,0:T(8,128)(2,1)} %copy-done.1, f32[512,512]{1,0:T(8,128)} %get-tuple-element.722, f32[512]{0:T(512)S(1)} %bitcast.267, f32[512]{0:T(512)S(1)} %bitcast.270), kind=kOutput, calls=%fused_computation.15.clone.1 | convolution fusion | flops 35913728 | bytes 1254400 | tf_op jit(solution)/shard_map/while/body/eval_jaxpr/dot_general | solution.py:82
  43.0 2.0 fusion.140
  47.7 2.4 %fusion.139 = f32[8,512,64]{1,2,0:T(8,128)} fusion(f32[8,512,64]{1,2,0:T(8,128)} %get-tuple-element.700, s32[]{:T(128)} %get-tuple-element.697, bf16[8,512,64]{1,2,0:T(8,128)(2,1)} %copy-done.1, f32[512,512]{1,0:T(8,128)} %get-tuple-element.722, f32[512]{0:T(512)S(1)} %bitcast.267, f32[512]{0:T(512)S(1)} %bitcast.270), kind=kOutput, calls=%fused_computation.15.clone.1 | convolution fusion | flops 35913728 | bytes 1254400 | tf_op jit(solution)/shard_map/while/body/eval_jaxpr/dot_general | solution.py:82
  50.1 2.0 fusion.140
  54.8 2.4 %fusion.139 = f32[8,512,64]{1,2,0:T(8,128)} fusion(f32[8,512,64]{1,2,0:T(8,128)} %get-tuple-element.700, s32[]{:T(128)} %get-tuple-element.697, bf16[8,512,64]{1,2,0:T(8,128)(2,1)} %copy-done.1, f32[512,512]{1,0:T(8,128)} %get-tuple-element.722, f32[512]{0:T(512)S(1)} %bitcast.267, f32[512]{0:T(512)S(1)} %bitcast.270), kind=kOutput, calls=%fused_computation.15.clone.1 | convolution fusion | flops 35913728 | bytes 1254400 | tf_op jit(solution)/shard_map/while/body/eval_jaxpr/dot_general | solution.py:82
  57.2 2.0 fusion.140
  61.9 2.4 %fusion.139 = f32[8,512,64]{1,2,0:T(8,128)} fusion(f32[8,512,64]{1,2,0:T(8,128)} %get-tuple-element.700, s32[]{:T(128)} %get-tuple-element.697, bf16[8,512,64]{1,2,0:T(8,128)(2,1)} %copy-done.1, f32[512,512]{1,0:T(8,128)} %get-tuple-element.722, f32[512]{0:T(512)S(1)} %bitcast.267, f32[512]{0:T(512)S(1)} %bitcast.270), kind=kOutput, calls=%fused_computation.15.clone.1 | convolution fusion | flops 35913728 | bytes 1254400 | tf_op jit(solution)/shard_map/while/body/eval_jaxpr/dot_general | solution.py:82
  64.3 2.0 fusion.140
  69.0 2.4 %fusion.139 = f32[8,512,64]{1,2,0:T(8,128)} fusion(f32[8,512,64]{1,2,0:T(8,128)} %get-tuple-element.700, s32[]{:T(128)} %get-tuple-element.697, bf16[8,512,64]{1,2,0:T(8,128)(2,1)} %copy-done.1, f32[512,512]{1,0:T(8,128)} %get-tuple-element.722, f32[512]{0:T(512)S(1)} %bitcast.267, f32[512]{0:T(512)S(1)} %bitcast.270), kind=kOutput, calls=%fused_computation.15.clone.1 | convolution fusion | flops 35913728 | bytes 1254400 | tf_op jit(solution)/shard_map/while/body/eval_jaxpr/dot_general | solution.py:82
  71.3 2.0 fusion.140
  76.0 2.4 %fusion.139 = f32[8,512,64]{1,2,0:T(8,128)} fusion(f32[8,512,64]{1,2,0:T(8,128)} %get-tuple-element.700, s32[]{:T(128)} %get-tuple-element.697, bf16[8,512,64]{1,2,0:T(8,128)(2,1)} %copy-done.1, f32[512,512]{1,0:T(8,128)} %get-tuple-element.722, f32[512]{0:T(512)S(1)} %bitcast.267, f32[512]{0:T(512)S(1)} %bitcast.270), kind=kOutput, calls=%fused_computation.15.clone.1 | convolution fusion | flops 35913728 | bytes 1254400 | tf_op jit(solution)/shard_map/while/body/eval_jaxpr/dot_general | solution.py:82
  78.4 2.0 fusion.140
  83.1 2.4 %fusion.139 = f32[8,512,64]{1,2,0:T(8,128)} fusion(f32[8,512,64]{1,2,0:T(8,128)} %get-tuple-element.700, s32[]{:T(128)} %get-tuple-element.697, bf16[8,512,64]{1,2,0:T(8,128)(2,1)} %copy-done.1, f32[512,512]{1,0:T(8,128)} %get-tuple-element.722, f32[512]{0:T(512)S(1)} %bitcast.267, f32[512]{0:T(512)S(1)} %bitcast.270), kind=kOutput, calls=%fused_computation.15.clone.1 | convolution fusion | flops 35913728 | bytes 1254400 | tf_op jit(solution)/shard_map/while/body/eval_jaxpr/dot_general | solution.py:82
  85.5 2.0 fusion.140
  90.0 2.7 %convert_multiply_fusion.7 = (f32[1,512,512]{1,2,0:T(8,128)}, f32[1,512,512]{1,2,0:T(8,128)}) fusion(bf16[1,512,512]{1,2,0:T(8,128)(2,1)} %bitcast.250, f32[512,8]{0,1:T(8,128)S(1)} %copy-done.15, f32[512,8]{0,1:T(8,128)} %copy-done.19), kind=kLoop, calls=%fused_computation.46 | loop fusion | flops 786432 | bytes 2654208 | tf_op jit(solution)/shard_map/mul | solution.py:110
  96.4 14.6 %all-reduce = bf16[32]{0:T(256)(128)(2,1)} all-reduce(bf16[32]{0:T(256)(128)(2,1)} %dynamic-update-slice), channel_id=2, replica_groups=mesh['dp'=2,'head'=4,'seq'=4] {'seq'}, use_global_device_ids=true, to_apply=%add | all-reduce | flops 32 | bytes 128
  112.4 15.4 %while.49 = (s32[]{:T(128)}, f32[4,8,64,64]{3,2,1,0:T(8,128)}, s32[]{:T(128)}, bf16[4,8]{1,0:T(4,128)(2,1)}, bf16[4,4,8,64,64]{4,3,2,1,0:T(8,128)(2,1)}, /*index=5*/s32[]{:T(128)}, s32[]{:T(128)}, s32[]{:T(128)}, s32[]{:T(128)}) while((s32[]{:T(128)}, f32[4,8,64,64]{3,2,1,0:T(8,128)}, s32[]{:T(128)}, bf16[4,8]{1,0:T(4,128)(2,1)}, ...), condition=%wide.region_7.8_spmd.clone, body=%wide.region_6.7_spmd.clone.sunk | while | flops 655376 | bytes 1310967 | solution.py:26
  113.6 2.4 %fusion.129 = f32[4,8,64,64]{3,2,1,0:T(8,128)} fusion(f32[4,8,64,64]{3,2,1,0:T(8,128)} %get-tuple-element.735, bf16[4,4,8,64,64]{4,3,2,1,0:T(8,128)(2,1)} %get-tuple-element.747, s32[]{:T(128)S(6)} %select_n.121, f32[8]{0:T(128)} %bitcast_convert_fusion.5, pred[]{:T(512)S(6)} %compare.10, pred[]{:T(512)S(6)} %gt.12), kind=kLoop, calls=%fused_computation.6.clone.1 | loop fusion | flops 655360 | bytes 1310758 | tf_op jit(solution)/shard_map/while/body/eval_jaxpr/jit(_where)/select_n | solution.py:24
  117.1 2.7 %fusion.129 = f32[4,8,64,64]{3,2,1,0:T(8,128)} fusion(f32[4,8,64,64]{3,2,1,0:T(8,128)} %get-tuple-element.735, bf16[4,4,8,64,64]{4,3,2,1,0:T(8,128)(2,1)} %get-tuple-element.747, s32[]{:T(128)S(6)} %select_n.121, f32[8]{0:T(128)} %bitcast_convert_fusion.5, pred[]{:T(512)S(6)} %compare.10, pred[]{:T(512)S(6)} %gt.12), kind=kLoop, calls=%fused_computation.6.clone.1 | loop fusion | flops 655360 | bytes 1310758 | tf_op jit(solution)/shard_map/while/body/eval_jaxpr/jit(_where)/select_n | solution.py:24
  121.1 2.7 %fusion.129 = f32[4,8,64,64]{3,2,1,0:T(8,128)} fusion(f32[4,8,64,64]{3,2,1,0:T(8,128)} %get-tuple-element.735, bf16[4,4,8,64,64]{4,3,2,1,0:T(8,128)(2,1)} %get-tuple-element.747, s32[]{:T(128)S(6)} %select_n.121, f32[8]{0:T(128)} %bitcast_convert_fusion.5, pred[]{:T(512)S(6)} %compare.10, pred[]{:T(512)S(6)} %gt.12), kind=kLoop, calls=%fused_computation.6.clone.1 | loop fusion | flops 655360 | bytes 1310758 | tf_op jit(solution)/shard_map/while/body/eval_jaxpr/jit(_where)/select_n | solution.py:24
  125.0 2.7 %fusion.129 = f32[4,8,64,64]{3,2,1,0:T(8,128)} fusion(f32[4,8,64,64]{3,2,1,0:T(8,128)} %get-tuple-element.735, bf16[4,4,8,64,64]{4,3,2,1,0:T(8,128)(2,1)} %get-tuple-element.747, s32[]{:T(128)S(6)} %select_n.121, f32[8]{0:T(128)} %bitcast_convert_fusion.5, pred[]{:T(512)S(6)} %compare.10, pred[]{:T(512)S(6)} %gt.12), kind=kLoop, calls=%fused_computation.6.clone.1 | loop fusion | flops 655360 | bytes 1310758 | tf_op jit(solution)/shard_map/while/body/eval_jaxpr/jit(_where)/select_n | solution.py:24
  127.7 10.7 %while.48 = (s32[]{:T(128)}, f32[4,8,64,64]{3,2,1,0:T(8,128)S(1)}, s32[]{:T(128)}, bf16[4,8]{1,0:T(4,128)(2,1)}, bf16[4,4,8,64,64]{4,3,2,1,0:T(8,128)(2,1)}, /*index=5*/s32[]{:T(128)}, s32[]{:T(128)}) while((s32[]{:T(128)}, f32[4,8,64,64]{3,2,1,0:T(8,128)S(1)}, s32[]{:T(128)}, bf16[4,8]{1,0:T(4,128)(2,1)}, ...), condition=%wide.region_5.6_spmd.clone, body=%wide.region_4.5_spmd.clone.sunk | while | flops 655372 | bytes 1310905 | solution.py:26
  138.4 2.2 convolution_bitcast_fusion.5
  140.6 2.1 convolution_bitcast_fusion.3
  148.0 37.3 %all-reduce.3.cloned.1.call-done = bf16[512,128]{0,1:T(8,128)(2,1)} async-done(((bf16[512,128]{0,1:T(8,128)(2,1)}), bf16[512,128]{0,1:T(8,128)(2,1)}) %all-reduce.3.cloned.1.call-update) | async-done | bytes 131088 | tf_op jit(solution)/shard_map/psum | solution.py:144
  185.3 2.4 %convolution_bitcast_fusion.2 = f32[2048,128]{0,1:T(8,128)} fusion(bf16[512,128]{0,1:T(8,128)(2,1)} %all-reduce.3.cloned.1.call-done, bf16[1,512,2048]{2,1,0:T(8,128)(2,1)S(1)} %copy-done), kind=kOutput, calls=%fused_computation.35 | convolution fusion | flops 268435456 | bytes 3276800 | tf_op jit(solution)/shard_map/td,tk->dk/dot_general | solution.py:151
  191.2 2.3 fusion.44
  195.6 3.1 %fusion.20 = bf16[1,512,2048]{2,1,0:T(8,128)(2,1)} fusion(bf16[512,128]{0,1:T(8,128)(2,1)S(1)} %copy-done.12, bf16[2048,128]{1,0:T(8,128)(2,1)} %param.17), kind=kOutput, calls=%fused_computation.34 | convolution fusion | flops 269484032 | bytes 2752512 | tf_op jit(solution)/shard_map/tk,dk->td/dot_general | solution.py:145
  198.6 24.9 %reduce-scatter.2.cloned.1.call-done = f32[256,128]{0,1:T(8,128)} async-done(((f32[2048,128]{0,1:T(8,128)}), f32[256,128]{0,1:T(8,128)}) %reduce-scatter.2.cloned.1.call-update) | async-done | bytes 131088 | tf_op jit(solution)/shard_map/reduce_scatter | solution.py:150
  (202 shorter events, 79.0 us)
Async XLA Ops:
  7.2 4.8 %copy-start = (bf16[1,512,2048]{2,1,0:T(8,128)(2,1)S(1)}, bf16[1,512,2048]{2,1,0:T(8,128)(2,1)}, u32[]{:S(2)}) copy-start(bf16[1,512,2048]{2,1,0:T(8,128)(2,1)} %param.14) | copy-start | bytes 6291460
  7.2 7.3 %copy-start.11 = (bf16[1,512,512]{2,1,0:T(8,128)(2,1)S(1)}, bf16[1,512,512]{2,1,0:T(8,128)(2,1)}, u32[]{:S(2)}) copy-start(bf16[1,512,512]{2,1,0:T(8,128)(2,1)} %param.15) | copy-start | bytes 1572868
  7.2 105.2 %all-gather.6.cloned.1.call-start = ((), (), s32[]{:S(2)}) async-start(), calls=%async_computation.2 | async-start | bytes 2621440 | tf_op jit(solution)/shard_map/all_gather | solution.py:12
  10.3 10.4 %copy-start.14 = (f32[512,8]{0,1:T(8,128)}, f32[512,8]{0,1:T(8,128)S(1)}, u32[]{:S(2)}) copy-start(f32[512,8]{0,1:T(8,128)S(1)} %get-tuple-element.525) | copy-start | bytes 49156
  11.3 13.8 %copy-start.21 = (f32[512,8]{0,1:T(8,128)}, f32[512,8]{0,1:T(8,128)S(1)}, u32[]{:S(2)}) copy-start(f32[512,8]{0,1:T(8,128)S(1)} %get-tuple-element.541) | copy-start | bytes 49156
  11.3 15.4 %copy-start.19 = (f32[512,8]{0,1:T(8,128)}, f32[512,8]{0,1:T(8,128)S(1)}, u32[]{:S(2)}) copy-start(f32[512,8]{0,1:T(8,128)S(1)} %get-tuple-element.523) | copy-start | bytes 49156
  11.9 4.4 %copy-start.16 = (f32[512,8]{0,1:T(8,128)}, f32[512,8]{0,1:T(8,128)S(1)}, u32[]{:S(2)}) copy-start(f32[512,8]{0,1:T(8,128)S(1)} %exponential_bitcast_fusion) | copy-start | bytes 49156
  19.8 7.0 %copy-start.5 = (bf16[1,512,512]{1,2,0:T(8,128)(2,1)}, bf16[1,512,512]{1,2,0:T(8,128)(2,1)S(1)}, u32[]{:S(2)}) copy-start(bf16[1,512,512]{1,2,0:T(8,128)(2,1)S(1)} %copy.48) | copy-start | bytes 1572868
  23.3 104.5 %all-gather.4.cloned.1.call-start = ((), (), s32[]{:S(2)}) async-start(), calls=%async_computation.1 | async-start | bytes 2621440 | tf_op jit(solution)/shard_map/all_gather | solution.py:12
  27.4 3.3 %copy-start.13 = (bf16[512,64]{0,1:T(8,128)(2,1)S(1)}, bf16[512,64]{0,1:T(8,128)(2,1)}, u32[]{:S(2)}) copy-start(bf16[512,64]{0,1:T(8,128)(2,1)} %get-tuple-element.539) | copy-start | bytes 196612
  28.3 157.0 %all-reduce.3.cloned.1.call-start = ((), (), s32[]{:S(2)}) async-start(), calls=%async_computation.3 | async-start | bytes 262144 | tf_op jit(solution)/shard_map/psum | solution.py:144
  30.8 57.5 %copy-start.17 = (f32[512,8]{0,1:T(8,128)S(1)}, f32[512,8]{0,1:T(8,128)}, u32[]{:S(2)}) copy-start(f32[512,8]{0,1:T(8,128)} %copy-done.16) | copy-start | bytes 49156
  30.8 57.5 %copy-start.22 = (f32[512,8]{0,1:T(8,128)S(1)}, f32[512,8]{0,1:T(8,128)}, u32[]{:S(2)}) copy-start(f32[512,8]{0,1:T(8,128)} %copy-done.21) | copy-start | bytes 49156
  33.2 2.8 %copy-start.10 = (f32[512,512]{1,0:T(8,128)S(1)}, f32[512,512]{1,0:T(8,128)}, u32[]{:S(2)}) copy-start(f32[512,512]{1,0:T(8,128)} %get-tuple-element.722) | copy-start | bytes 3145732 | tf_op jit(solution)/shard_map/while
  40.3 2.7 %copy-start.10 = (f32[512,512]{1,0:T(8,128)S(1)}, f32[512,512]{1,0:T(8,128)}, u32[]{:S(2)}) copy-start(f32[512,512]{1,0:T(8,128)} %get-tuple-element.722) | copy-start | bytes 3145732 | tf_op jit(solution)/shard_map/while
  43.0 2.0 copy-start.2
  47.4 2.7 %copy-start.10 = (f32[512,512]{1,0:T(8,128)S(1)}, f32[512,512]{1,0:T(8,128)}, u32[]{:S(2)}) copy-start(f32[512,512]{1,0:T(8,128)} %get-tuple-element.722) | copy-start | bytes 3145732 | tf_op jit(solution)/shard_map/while
  50.1 2.0 copy-start.2
  54.5 2.7 %copy-start.10 = (f32[512,512]{1,0:T(8,128)S(1)}, f32[512,512]{1,0:T(8,128)}, u32[]{:S(2)}) copy-start(f32[512,512]{1,0:T(8,128)} %get-tuple-element.722) | copy-start | bytes 3145732 | tf_op jit(solution)/shard_map/while
  57.2 2.0 copy-start.2
  61.6 2.7 %copy-start.10 = (f32[512,512]{1,0:T(8,128)S(1)}, f32[512,512]{1,0:T(8,128)}, u32[]{:S(2)}) copy-start(f32[512,512]{1,0:T(8,128)} %get-tuple-element.722) | copy-start | bytes 3145732 | tf_op jit(solution)/shard_map/while
  64.3 2.0 copy-start.2
  68.6 2.7 %copy-start.10 = (f32[512,512]{1,0:T(8,128)S(1)}, f32[512,512]{1,0:T(8,128)}, u32[]{:S(2)}) copy-start(f32[512,512]{1,0:T(8,128)} %get-tuple-element.722) | copy-start | bytes 3145732 | tf_op jit(solution)/shard_map/while
  71.3 2.0 copy-start.2
  75.7 2.7 %copy-start.10 = (f32[512,512]{1,0:T(8,128)S(1)}, f32[512,512]{1,0:T(8,128)}, u32[]{:S(2)}) copy-start(f32[512,512]{1,0:T(8,128)} %get-tuple-element.722) | copy-start | bytes 3145732 | tf_op jit(solution)/shard_map/while
  78.4 2.0 copy-start.2
  82.8 2.7 %copy-start.10 = (f32[512,512]{1,0:T(8,128)S(1)}, f32[512,512]{1,0:T(8,128)}, u32[]{:S(2)}) copy-start(f32[512,512]{1,0:T(8,128)} %get-tuple-element.722) | copy-start | bytes 3145732 | tf_op jit(solution)/shard_map/while
  85.5 2.0 copy-start.2
  138.4 4.3 %copy-start.7 = (f32[1,512,512]{1,2,0:T(8,128)S(1)}, f32[1,512,512]{1,2,0:T(8,128)}, u32[]{:S(2)}) copy-start(f32[1,512,512]{1,2,0:T(8,128)} %get-tuple-element.533) | copy-start | bytes 3145732
  138.4 5.2 %copy-start.8 = (f32[1,512,512]{1,2,0:T(8,128)S(1)}, f32[1,512,512]{1,2,0:T(8,128)}, u32[]{:S(2)}) copy-start(f32[1,512,512]{1,2,0:T(8,128)} %get-tuple-element.535) | copy-start | bytes 3145732
  145.1 78.4 %reduce-scatter.2.cloned.1.call-start = ((), (), s32[]{:S(2)}) async-start(), calls=%async_computation.4 | async-start | bytes 1179648 | tf_op jit(solution)/shard_map/reduce_scatter | solution.py:150
  193.5 2.0 copy-start.12
  (19 other events, 24.1 us)
Sparse Core Ops, SparseCore 0:
  23.4 48.6 all-gather.5
  73.6 44.9 all-gather.3
  145.2 40.0 all-reduce.2
  187.8 35.6 reduce-scatter.1
where the time goes:
time: 234 us; the launch traced here: 232 us
  matrix products  75.9 us (32%)
  waiting for transfers between devices  62.2 us (27%)
  other arithmetic  42.2 us (18%)
  local copies, waits for them, and re-layouts  21.3 us (9%)
  between operations  14.9 us (6%)
  blocking collectives  14.6 us (6%)
    psum x1, waiting for transfers between devices, per_device(): summed_bc = lax.psum(partial_bc.astype(jnp.bfloat16), 'head')  37.3 us
    reduce_scatter x1, waiting for transfers between devices, per_device(): lax.psum_scatter(jnp.einsum('td,tk->dk', tokens, summed_bc, preferred_ele...  24.9 us
    dot_general x8, matrix products, head_block(): y_head = jnp.dot(weights_main, x_head, preferred_element_type=jnp.float32)  19 us
    select_n x8, other arithmetic, step(): return jax.tree.map(lambda a, b: jnp.where(reached, a, b), new, before)  16.4 us
    dot_general x8, matrix products, head_block(): jnp.dot(weights_main.T, g_head, preferred_element_type=jnp.float32)  16.1 us
    unnamed x1, blocking collectives  14.6 us
    dot_general x8, matrix products, head_block(): value_scores = jnp.dot(g_head, x_head.T, preferred_element_type=jnp.float32)  10.2 us
    convert_element_type x8, other arithmetic, step(): part[at].astype(own.dtype)  9.56 us
  transfers between devices with their start and end apart: 4, of which 2 were waited for; matrix products, arithmetic and copies ran while one was open for 44% of the time, Pallas kernels for 0%

commit v1 on v0

v1 whole, which is shorter than its diff:
```python
import functools

import jax
import jax.numpy as jnp
from jax import lax
from jax.experimental import pallas as pl
from jax.experimental.pallas import tpu as pltpu
from jax.sharding import PartitionSpec as P

F32 = jnp.float32
BF16 = jnp.bfloat16
VMEM_SPEC = pl.BlockSpec(memory_space=pltpu.VMEM)
SMEM_SPEC = pl.BlockSpec(memory_space=pltpu.SMEM)
EXTRA = 16


def mm(a, b):
    return jnp.dot(a, b, preferred_element_type=F32)


def mm_t(a, b):
    return lax.dot_general(a, b, (((1,), (1,)), ((), ())), preferred_element_type=F32)


def split2(v):
    high = v.astype(BF16)
    return high, (v - high.astype(F32)).astype(BF16)


def spread_matrix(heads, width):
    rows = 8 * heads
    row = lax.broadcasted_iota(jnp.int32, (rows, 4 * width), 0)
    col = lax.broadcasted_iota(jnp.int32, (rows, 4 * width), 1)
    per_head = width // heads
    kind_ok = (row // (2 * heads)) == (col // width)
    head_ok = (row % heads) == ((col % width) // per_head)
    return jnp.where(kind_ok & head_ok, 1.0, 0.0).astype(BF16)


def states_kernel(
    n_seq, steps, tokens_ref, x_ref, g_ref, dt_ref, w_ref, rate_ref, bias_ref,
    bc_ref, cb_ref, rows_ref, cols_ref, decs_ref, pay1_ref, pay2_ref, pay3_ref, acc_ref, spread_ref, last_ref,
):
    step = pl.program_id(0)
    heads, length = dt_ref.shape
    chunk = tokens_ref.shape[0]
    width = x_ref.shape[1]

    @pl.when(step == 0)
    def _():
        sub = lax.broadcasted_iota(jnp.int32, (heads, 1), 0)
        rate = jnp.zeros((heads, 1), F32)
        bias = jnp.zeros((heads, 1), F32)
        for h in range(heads):
            rate = jnp.where(sub == h, rate_ref[h], rate)
            bias = jnp.where(sub == h, bias_ref[h], bias)
        v = dt_ref[...] + bias
        log_step = -rate * (jnp.maximum(v, 0.0) + jnp.log1p(jnp.exp(-jnp.abs(v))))
        lane = lax.broadcasted_iota(jnp.int32, (heads, length), 1)
        cum = log_step
        shift = 1
        while shift < length:
            cum = cum + jnp.where(lane >= shift, pltpu.roll(cum, shift, 1), 0.0)
            shift *= 2
        prev = cum - log_step
        final = cum[:, length - 1 : length]
        kinds = (jnp.exp(cum), jnp.exp(final - prev), jnp.exp(prev), jnp.exp(final - cum))
        parts = []
        for k in kinds:
            high = k.astype(BF16).astype(F32)
            parts += [high, k - high]
        decs_ref[...] = jnp.concatenate(parts, axis=0).astype(BF16)
        for p in range(heads // 2):
            block = jnp.concatenate(
                [cum[2 * p : 2 * p + 1], prev[2 * p : 2 * p + 1], cum[2 * p + 1 : 2 * p + 2], prev[2 * p + 1 : 2 * p + 2]]
                + [jnp.zeros((4, length), F32)],
                axis=0,
            )
            rows_ref[p] = block
            cols_ref[p] = block.T
        spread_ref[...] = spread_matrix(heads, width)
        head_of = lax.broadcasted_iota(jnp.int32, (heads, width), 1) // (width // heads)
        head_row = lax.broadcasted_iota(jnp.int32, (heads, width), 0)
        decay = jnp.sum(jnp.where(head_of == head_row, jnp.exp(final), 0.0), axis=0, keepdims=True)
        high = decay.astype(BF16).astype(F32)
        row16 = lax.broadcasted_iota(jnp.int32, (EXTRA, width), 0)
        last_ref[...] = jnp.where(row16 == 0, high, jnp.where(row16 == 1, decay - high, 0.0))
        acc_ref[...] = jnp.zeros_like(acc_ref)

    projected = mm(tokens_ref[...], w_ref[...])
    half = projected.shape[1] // 2
    bc = projected.astype(BF16)
    bc_ref[...] = bc
    turned = pltpu.roll(projected, half, 1)
    cb = turned.astype(BF16)
    cb_ref[...] = cb
    cb_t = turned.T.astype(BF16)
    start = pl.multiple_of(step * chunk, chunk)
    decs = decs_ref[:, pl.ds(start, chunk)].astype(F32).T.astype(BF16)
    e = mm(decs, spread_ref[...])
    x = x_ref[...].astype(F32)
    g = g_ref[...].astype(F32)
    g_up = (g * e[:, :width]).astype(BF16)
    g_down = (g * e[:, width : 2 * width]).astype(BF16)
    x_up = (x * e[:, 2 * width : 3 * width]).astype(BF16)
    x_down = (x * e[:, 3 * width :]).astype(BF16)
    acc_ref[0, :half] += mm(cb_t[:half], g_down)
    acc_ref[0, half:] += mm(cb_t[half:], x_down)
    acc_ref[1, :half] += mm(cb_t[:half], g_up)
    acc_ref[1, half:] += mm(cb_t[half:], x_up)

    @pl.when(step == steps - 1)
    def _():
        onward = acc_ref[0].astype(BF16)
        backward = acc_ref[1].astype(BF16)
        last = last_ref[...].astype(BF16)
        for k, ref in ((1, pay1_ref), (2, pay2_ref), (3, pay3_ref)):
            ref[2 * half :] = last
            if n_seq == 4:
                here = lax.axis_index("seq")
                up = (here ^ k) > here

                @pl.when(up)
                def _():
                    ref[: 2 * half] = onward

                @pl.when(jnp.logical_not(up))
                def _():
                    ref[: 2 * half] = backward
            else:
                ref[: 2 * half] = onward if k == 1 else backward


def block_states(n_seq, tokens, x, g, dt, w, rate, bias):
    _, length, depth = tokens.shape
    width = x.shape[2]
    heads = dt.shape[1]
    two_n = w.shape[1]
    steps = 2
    chunk = length // steps
    pay = jax.ShapeDtypeStruct((two_n + EXTRA, width), BF16)
    whole = lambda *shape: pl.BlockSpec(shape, lambda i: (0,) * len(shape))
    return pl.pallas_call(
        functools.partial(states_kernel, n_seq, steps),
        name="block_states",
        grid=(steps,),
        in_specs=[
            pl.BlockSpec((None, chunk, depth), lambda i: (0, i, 0)),
            pl.BlockSpec((None, chunk, width), lambda i: (0, i, 0)),
            pl.BlockSpec((None, chunk, width), lambda i: (0, i, 0)),
            pl.BlockSpec((None, heads, length), lambda i: (0, 0, 0)),
            whole(depth, two_n),
            SMEM_SPEC,
            SMEM_SPEC,
        ],
        out_specs=[
            pl.BlockSpec((chunk, two_n), lambda i: (i, 0)),
            pl.BlockSpec((chunk, two_n), lambda i: (i, 0)),
            whole(heads // 2, 8, length),
            whole(heads // 2, length, 8),
            whole(8 * heads, length),
            whole(two_n + EXTRA, width),
            whole(two_n + EXTRA, width),
            whole(two_n + EXTRA, width),
        ],
        out_shape=[
            jax.ShapeDtypeStruct((length, two_n), BF16),
            jax.ShapeDtypeStruct((length, two_n), BF16),
            jax.ShapeDtypeStruct((heads // 2, 8, length), F32),
            jax.ShapeDtypeStruct((heads // 2, length, 8), F32),
            jax.ShapeDtypeStruct((8 * heads, length), BF16),
            pay,
            pay,
            pay,
        ],
        scratch_shapes=[
            pltpu.VMEM((2, two_n, width), F32),
            pltpu.VMEM((8 * heads, 4 * width), BF16),
            pltpu.VMEM((EXTRA, width), F32),
        ],
        cost_estimate=pl.CostEstimate(flops=2 * length * depth * two_n, bytes_accessed=5 << 20, transcendentals=0),
    )(tokens, x, g, dt, w, rate, bias)


def local_kernel(
    n_t, n_pair, x_ref, g_ref, bc_ref, cb_ref, rows_ref, cols_ref, skip_ref,
    y_ref, gv_ref, gbc_ref, xm_ref, scores_ref, total_ref, gvt_ref, gbt_ref, gc_ref,
):
    tb = pl.program_id(0)
    pair = pl.program_id(1)
    length = x_ref.shape[0]
    tile = length // n_t
    lanes = 128
    t0 = pl.multiple_of(tb * tile, tile)
    p0 = pl.multiple_of(pair * lanes, lanes)
    first_half = lax.broadcasted_iota(jnp.int32, (1, lanes), 1) < lanes // 2
    zero = jnp.zeros((), BF16)

    @pl.when(tb == 0)
    def _():
        xp = x_ref[:, pl.ds(p0, lanes)]
        xm_ref[pair, :length] = jnp.where(first_half, xp, zero)
        xm_ref[pair, length:] = jnp.where(first_half, zero, xp)
        gvt_ref[pair] = jnp.zeros((lanes, length), F32)

    cb_t = cb_ref[pl.ds(t0, tile), :]

    @pl.when(pair == 0)
    def _():
        scores_ref[...] = mm_t(jnp.where(first_half, cb_t, zero), bc_ref[...])

    g_t = g_ref[pl.ds(t0, tile), pl.ds(p0, lanes)]
    g_s = g_t.astype(F32)
    row = t0 + lax.broadcasted_iota(jnp.int32, (tile, length), 0)
    col = lax.broadcasted_iota(jnp.int32, (tile, length), 1)
    below = col < row
    same = col == row
    xm = xm_ref[pair]
    grams = mm_t(g_t, xm)
    cols = cols_ref[pair, pl.ds(t0, tile), :]
    scores = scores_ref[...]
    mains = []
    grad = None
    for k in range(2):
        cum_t, prev_t = cols[:, 2 * k : 2 * k + 1], cols[:, 2 * k + 1 : 2 * k + 2]
        cum_s, prev_s = rows_ref[pair, 2 * k : 2 * k + 1], rows_ref[pair, 2 * k + 1 : 2 * k + 2]
        diff = jnp.minimum(jnp.where(below, cum_t - cum_s, prev_s - prev_t), 0.0)
        kern = jnp.where(same, 0.0, jnp.exp(diff))
        mains.append((scores * kern).astype(BF16))
        term = grams[:, k * length : (k + 1) * length] * kern
        grad = term if grad is None else grad + term

    y = mm(mains[0], xm[:length]) + mm(mains[1], xm[length:])
    sk = jnp.where(first_half, skip_ref[2 * pair], skip_ref[2 * pair + 1])
    y_ref[...] = y + sk * x_ref[pl.ds(t0, tile), pl.ds(p0, lanes)].astype(F32)
    gt = g_s.T.astype(BF16)
    upper = lax.broadcasted_iota(jnp.int32, (lanes, 1), 0) < lanes // 2
    gvt_ref[pair] += mm(jnp.where(upper, gt, zero), mains[0]) + mm(jnp.where(upper, zero, gt), mains[1])

    @pl.when(pair == 0)
    def _():
        total_ref[...] = grad

    @pl.when(pair > 0)
    def _():
        total_ref[...] += grad

    @pl.when(pair == n_pair - 1)
    def _():
        total = total_ref[...].astype(BF16)
        gc_ref[pl.ds(t0, tile), :] = mm(total, cb_ref[...])
        gbt = mm(cb_t.astype(F32).T.astype(BF16), total)

        @pl.when(tb == 0)
        def _():
            gbt_ref[...] = gbt

        @pl.when(tb > 0)
        def _():
            gbt_ref[...] += gbt

    @pl.when(tb == n_t - 1)
    def _():
        gv_ref[:, pl.ds(p0, lanes)] = gvt_ref[pair].T + sk * g_ref[:, pl.ds(p0, lanes)].astype(F32)

        @pl.when(pair == n_pair - 1)
        def _():
            gbc_ref[...] = jnp.where(first_half, gbt_ref[...].T, gc_ref[...])


def inside_block(x, g, bc, cb, rows, cols, skip):
    _, length, width = x.shape
    n_pair = width // 128
    n_t = 4
    tile = length // n_t
    full = lambda *shape: pl.BlockSpec(shape, lambda t, p: (0,) * len(shape))
    return pl.pallas_call(
        functools.partial(local_kernel, n_t, n_pair),
        name="inside_block",
        grid=(n_t, n_pair),
        in_specs=[
            pl.BlockSpec((None, length, width), lambda t, p: (0, 0, 0)),
            pl.BlockSpec((None, length, width), lambda t, p: (0, 0, 0)),
            full(length, 128),
            full(length, 128),
            full(n_pair, 8, length),
            full(n_pair, length, 8),
            SMEM_SPEC,
        ],
        out_specs=[
            pl.BlockSpec((tile, 128), lambda t, p: (t, p)),
            full(length, width),
            full(length, 128),
        ],
        out_shape=[
            jax.ShapeDtypeStruct((length, width), F32),
            jax.ShapeDtypeStruct((length, width), F32),
            jax.ShapeDtypeStruct((length, 128), F32),
        ],
        scratch_shapes=[
            pltpu.VMEM((n_pair, 2 * length, 128), BF16),
            pltpu.VMEM((tile, length), F32),
            pltpu.VMEM((tile, length), F32),
            pltpu.VMEM((n_pair, 128, length), F32),
            pltpu.VMEM((128, length), F32),
            pltpu.VMEM((length, 128), F32),
        ],
        cost_estimate=pl.CostEstimate(
            flops=6 * length * length * width, bytes_accessed=4 << 20, transcendentals=2 * n_pair * length * length
        ),
    )(x, g, bc, cb, rows, cols, skip)


def carry_kernel(
    direct, r1_ref, r2_ref, r3_ref, x_ref, g_ref, bc_ref, decs_ref, y_ref, gv_ref, gbc_ref,
    yo_ref, gvo_ref, group_ref, before_ref, after_ref, spread_ref,
):
    step = pl.program_id(0)
    two_n, width = before_ref.shape
    heads = decs_ref.shape[0] // 8
    chunk = x_ref.shape[0]

    @pl.when(step == 0)
    def _():
        spread_ref[...] = spread_matrix(heads, width)
        if direct:
            here = lax.axis_index("seq")
            refs = (r1_ref, r2_ref, r3_ref)
            decays = [r[two_n : two_n + 1].astype(F32) + r[two_n + 1 : two_n + 2].astype(F32) for r in refs]
            before = jnp.zeros((two_n, width), F32)
            after = jnp.zeros((two_n, width), F32)
            for k in (1, 2, 3):
                there = here ^ k
                low, high = jnp.minimum(here, there), jnp.maximum(here, there)
                factor = jnp.ones((1, width), F32)
                for m in (1, 2, 3):
                    if m != k:
                        mid = here ^ m
                        inside = jnp.logical_and(mid > low, mid < high)
                        factor = factor * jnp.where(inside, decays[m - 1], 1.0)
                part = refs[k - 1][:two_n].astype(F32)
                earlier = there < here
                before = before + part * jnp.where(earlier, factor, 0.0)
                after = after + part * jnp.where(earlier, 0.0, factor)
            before_ref[...] = before.astype(BF16)
            after_ref[...] = after.astype(BF16)
        else:
            before_ref[...] = r1_ref[:two_n]
            after_ref[...] = r2_ref[:two_n]

    before = before_ref[...]
    after = after_ref[...]
    half = two_n // 2
    top = lax.broadcasted_iota(jnp.int32, (two_n, 1), 0) < half
    zero = jnp.zeros((), BF16)
    start = pl.multiple_of(step * chunk, chunk)
    decs = decs_ref[:, pl.ds(start, chunk)].astype(F32).T.astype(BF16)
    e = mm(decs, spread_ref[...])
    g_up, g_down = e[:, :width], e[:, width : 2 * width]
    x_up, x_down = e[:, 2 * width : 3 * width], e[:, 3 * width :]
    bc = bc_ref[...]
    lower_b, lower_a = jnp.where(top, zero, before), jnp.where(top, zero, after)
    upper_b, upper_a = jnp.where(top, before, zero), jnp.where(top, after, zero)
    yo_ref[...] = (y_ref[...] + g_up * mm(bc, lower_b) + g_down * mm(bc, lower_a)).astype(BF16)
    gvo_ref[...] = (gv_ref[...] + x_up * mm(bc, upper_b) + x_down * mm(bc, upper_a)).astype(BF16)
    x = x_ref[...].astype(F32)
    g = g_ref[...].astype(F32)
    from_x = mm_t((x * x_up).astype(BF16), before) + mm_t((x * x_down).astype(BF16), after)
    from_g = mm_t((g * g_up).astype(BF16), before) + mm_t((g * g_down).astype(BF16), after)
    left = lax.broadcasted_iota(jnp.int32, (1, two_n), 1) < half
    group_ref[...] = (gbc_ref[...] + jnp.where(left, from_x, from_g)).astype(BF16)


def add_carries(direct, r1, r2, r3, x, g, bc, decs, y, gv, gbc):
    _, length, width = x.shape
    two_n = bc.shape[1]
    steps = 2
    chunk = length // steps
    whole = lambda a: pl.BlockSpec(a.shape, lambda i: (0, 0))
    part = lambda w: pl.BlockSpec((chunk, w), lambda i: (i, 0))
    part3 = lambda w: pl.BlockSpec((None, chunk, w), lambda i: (0, i, 0))
    return pl.pallas_call(
        functools.partial(carry_kernel, direct),
        name="add_carries",
        grid=(steps,),
        in_specs=[
            whole(r1), whole(r2), whole(r3), part3(width), part3(width), part(two_n), whole(decs),
            part(width), part(width), part(two_n),
        ],
        out_specs=[part3(width), part3(width), part(two_n)],
        out_shape=[
            jax.ShapeDtypeStruct((1, length, width), BF16),
            jax.ShapeDtypeStruct((1, length, width), BF16),
            jax.ShapeDtypeStruct((length, two_n), BF16),
        ],
        scratch_shapes=[
            pltpu.VMEM((two_n, width), BF16),
            pltpu.VMEM((two_n, width), BF16),
            pltpu.VMEM((decs.shape[0], 4 * width), BF16),
        ],
        cost_estimate=pl.CostEstimate(flops=16 * length * two_n * width, bytes_accessed=5 << 20, transcendentals=0),
    )(r1, r2, r3, x, g, bc, decs, y, gv, gbc)


def scanned_generic(onward, backward, two_n):
    size, here = lax.axis_size("seq"), lax.axis_index("seq")

    def total(payload, reverse):
        every = lax.all_gather(payload, "seq")

        def step(k, before):
            at = size - 1 - k if reverse else k
            one = every[at].astype(F32)
            new = before * (one[two_n : two_n + 1] + one[two_n + 1 : two_n + 2]) + one[:two_n]
            return jnp.where(at > here if reverse else at < here, new, before)

        return lax.fori_loop(0, size, step, jnp.zeros((two_n, payload.shape[1]), F32))

    pad = lambda v: jnp.pad(v.astype(BF16), ((0, EXTRA), (0, 0)))
    return pad(total(onward, False)), pad(total(backward, True))


def weight_kernel(a0_ref, a1_ref, a2_ref, a3_ref, tokens_ref, grad_ref, send_ref, keep_ref):
    total = a0_ref[...].astype(F32) + a1_ref[...].astype(F32) + a2_ref[...].astype(F32) + a3_ref[...].astype(F32)
    grad = total.astype(BF16)
    grad_ref[...] = grad
    grad_t = grad.astype(F32).T.astype(BF16)
    here = lax.axis_index("dp")
    n_seq, _, cols = keep_ref.shape
    for s in range(n_seq):
        away = pl.multiple_of(((1 - here) * n_seq + s) * cols, cols)
        send_ref[s] = mm(grad_t, tokens_ref[:, pl.ds(away, cols)]).astype(BF16)
    for s in range(n_seq):
        home = pl.multiple_of((here * n_seq + s) * cols, cols)
        keep_ref[s] = mm(grad_t, tokens_ref[:, pl.ds(home, cols)])


def weight_parts(n_seq, groups, tokens):
    _, length, depth = tokens.shape
    two_n = groups[0].shape[1]
    cols = depth // (2 * n_seq)
    return pl.pallas_call(
        weight_kernel,
        name="weight_parts",
        grid=(1,),
        in_specs=[pl.BlockSpec((length, two_n), lambda i: (0, 0))] * 4
        + [pl.BlockSpec((None, length, depth), lambda i: (0, 0, 0))],
        out_specs=[
            pl.BlockSpec((length, two_n), lambda i: (0, 0)),
            pl.BlockSpec((n_seq, two_n, cols), lambda i: (0, 0, 0)),
            pl.BlockSpec((n_seq, two_n, cols), lambda i: (0, 0, 0)),
        ],
        out_shape=[
            jax.ShapeDtypeStruct((length, two_n), BF16),
            jax.ShapeDtypeStruct((n_seq, two_n, cols), BF16),
            jax.ShapeDtypeStruct((n_seq, two_n, cols), F32),
        ],
        cost_estimate=pl.CostEstimate(flops=2 * length * two_n * depth, bytes_accessed=4 << 20, transcendentals=0),
    )(*groups, tokens)


def pair_kernel(keep_ref, got_ref, own_ref, s1_ref, s2_ref, s3_ref):
    here = lax.axis_index("seq")
    own_ref[...] = keep_ref[here] + got_ref[here].astype(F32)
    for k, ref in ((1, s1_ref), (2, s2_ref), (3, s3_ref)):
        at = here ^ k
        ref[...] = (keep_ref[at] + got_ref[at].astype(F32)).astype(BF16)


def pair_sum(keep, got):
    _, two_n, cols = keep.shape
    small = jax.ShapeDtypeStruct((two_n, cols), BF16)
    return pl.pallas_call(
        pair_kernel,
        name="pair_sum",
        in_specs=[VMEM_SPEC, VMEM_SPEC],
        out_specs=[VMEM_SPEC] * 4,
        out_shape=[jax.ShapeDtypeStruct((two_n, cols), F32), small, small, small],
    )(keep, got)


def final_kernel(scale, own_ref, r1_ref, r2_ref, r3_ref, out_ref):
    total = own_ref[...] + r1_ref[...].astype(F32) + r2_ref[...].astype(F32) + r3_ref[...].astype(F32)
    out_ref[...] = total.T * scale


def final_sum(scale, own, r1, r2, r3):
    two_n, cols = own.shape
    return pl.pallas_call(
        functools.partial(final_kernel, scale),
        name="final_sum",
        in_specs=[VMEM_SPEC] * 4,
        out_specs=VMEM_SPEC,
        out_shape=jax.ShapeDtypeStruct((cols, two_n), F32),
    )(own, r1, r2, r3)


def input_kernel(grad_ref, w_ref, out_ref):
    out_ref[...] = mm_t(grad_ref[...], w_ref[...]).astype(BF16)


def input_grad(grad, w):
    length, two_n = grad.shape
    depth = w.shape[0]
    steps = 4
    chunk = length // steps
    return pl.pallas_call(
        input_kernel,
        name="input_grad",
        grid=(steps,),
        in_specs=[pl.BlockSpec((chunk, two_n), lambda i: (i, 0)), pl.BlockSpec((depth, two_n), lambda i: (0, 0))],
        out_specs=pl.BlockSpec((None, chunk, depth), lambda i: (0, i, 0)),
        out_shape=jax.ShapeDtypeStruct((1, length, depth), BF16),
        cost_estimate=pl.CostEstimate(flops=2 * length * two_n * depth, bytes_accessed=3 << 20, transcendentals=0),
    )(grad, w)


def swap(value, axis, k):
    return lax.ppermute(value, axis, [(i, i ^ k) for i in range(lax.axis_size(axis))])


def per_device(layer_input, head_values, dt_raw, w_bc, decay_rate, dt_bias, skip_gain, grad_y):
    n_seq, n_head, n_dp = lax.axis_size("seq"), lax.axis_size("head"), lax.axis_size("dp")
    length = layer_input.shape[1]
    two_n = w_bc.shape[1]
    bc, cb, rows, cols, decs, pay1, pay2, pay3 = block_states(
        n_seq, layer_input, head_values, grad_y, dt_raw, w_bc, decay_rate, dt_bias
    )
    direct = n_seq == 4
    if direct:
        r1, r2, r3 = swap(pay1, "seq", 1), swap(pay2, "seq", 2), swap(pay3, "seq", 3)
    else:
        r1, r2 = scanned_generic(pay1, pay2, two_n)
        r3 = r2
    y_local, gv_local, gbc_local = inside_block(head_values, grad_y, bc, cb, rows, cols, skip_gain)
    y_out, grad_values, group = add_carries(
        direct, r1, r2, r3, head_values, grad_y, bc, decs, y_local, gv_local, gbc_local
    )
    total_tokens = n_dp * n_seq * length
    if direct and n_dp == 2 and n_head == 4:
        groups = [group] + [swap(group, "head", k) for k in (1, 2, 3)]
        grad_bc, send, keep = weight_parts(n_seq, groups, layer_input)
        got = swap(send, "dp", 1)
        own, s1, s2, s3 = pair_sum(keep, got)
        grad_w_bc = final_sum(1.0 / total_tokens, own, swap(s1, "seq", 1), swap(s2, "seq", 2), swap(s3, "seq", 3))
    else:
        grad_bc = lax.psum(group.astype(F32), "head").astype(BF16)
        part = jnp.einsum("td,tk->dk", layer_input[0], grad_bc, preferred_element_type=F32)
        grad_w_bc = lax.psum_scatter(part, ("dp", "seq"), scatter_dimension=0, tiled=True) / total_tokens
    grad_input = input_grad(grad_bc, w_bc)
    return y_out, grad_values, grad_input, grad_w_bc


def solution(mesh):
    in_specs = (
        P("dp", "seq", None),
        P("dp", "seq", "head"),
        P("dp", "head", "seq"),
        P(),
        P("head"),
        P("head"),
        P("head"),
        P("dp", "seq", "head"),
    )
    out_specs = (
        P("dp", "seq", "head"),
        P("dp", "seq", "head"),
        P("dp", "seq", None),
        P(("dp", "seq"), None),
    )
    return jax.shard_map(per_device, mesh=mesh, in_specs=in_specs, out_specs=out_specs, check_vma=False)
```

time: 234 us -> 64.1 us (0.27)
  matrix products: 75.9 us -> 0 us
  waiting for transfers between devices: 62.2 us -> 8.99 us
  other arithmetic: 42.2 us -> 0 us
  Pallas kernels: 0 us -> 37.1 us
  local copies, waits for them, and re-layouts: 21.3 us -> 3.31 us
  blocking collectives: 14.6 us -> 0 us
  between operations: 14.9 us -> 0.7 us
  starting transfers between devices: 0.16 us -> 13.6 us
    dot_general x56 -> x0, matrix products: 73.7 us -> none  [the longest x8 19 us: head_block(): y_head = jnp.dot(weights_main, x_head, preferred_element_type=jnp.float32)]
    psum x1 -> x0, waiting for transfers between devices: 37.3 us -> none  [per_device(): summed_bc = lax.psum(partial_bc.astype(jnp.bfloat16), 'head')]
    pallas_call x0 -> x7, Pallas kernels: none -> 37.1 us  [the longest x1 15.6 us: inside_block(): pl.pallas_call(functools.partial(local_kernel, n_t, n_pair), name='inside...]
    reduce_scatter x1 -> x0, waiting for transfers between devices: 24.9 us -> none  [per_device(): lax.psum_scatter(jnp.einsum('td,tk->dk', tokens, summed_bc, preferred_ele...]
    select_n x8 -> x0, other arithmetic: 16.4 us -> none  [step(): return jax.tree.map(lambda a, b: jnp.where(reached, a, b), new, before)]
    unnamed x1 -> x0, blocking collectives: 14.6 us -> none
    ppermute x0 -> x10, starting transfers between devices: none -> 13.6 us  [swap(): lax.ppermute(value, axis, [(i, i ^ k) for i in range(lax.axis_size(axis))])]
    convert_element_type x11 -> x0, other arithmetic: 13.3 us -> none  [the longest x8 9.56 us: step(): part[at].astype(own.dtype)]
  transfers between devices with their start and end apart: 4 -> 10, of which waited for: 2 -> 6; matrix products, arithmetic and copies ran while one was open for 44% -> 0% of each run, Pallas kernels for 0% -> 31%
where the time goes in v1:
time: 64.1 us; the launch traced here: 63.6 us
  Pallas kernels  37.1 us (58%)
  starting transfers between devices  13.6 us (21%)
  waiting for transfers between devices  8.99 us (14%)
  local copies, waits for them, and re-layouts  3.31 us (5%)
  between operations  0.7 us (1%)
    pallas_call x1, Pallas kernels, inside_block(): pl.pallas_call(functools.partial(local_kernel, n_t, n_pair), name='inside...  15.6 us
    ppermute x10, starting transfers between devices, swap(): lax.ppermute(value, axis, [(i, i ^ k) for i in range(lax.axis_size(axis))])  13.6 us
    ppermute x10, waiting for transfers between devices, swap(): lax.ppermute(value, axis, [(i, i ^ k) for i in range(lax.axis_size(axis))])  8.99 us
    pallas_call x1, Pallas kernels, block_states(): pl.pallas_call(functools.partial(states_kernel, n_seq, steps), name='bloc...  5.79 us
    pallas_call x1, Pallas kernels, add_carries(): pl.pallas_call(functools.partial(carry_kernel, direct), name='add_carries...  4.87 us
    pallas_call x1, Pallas kernels, input_grad(): pl.pallas_call(input_kernel, name='input_grad', grid=(steps,), in_specs=[...  4 us
    unnamed x20, local copies, waits for them, and re-layouts  3.31 us
    pallas_call x1, Pallas kernels, weight_parts(): pl.pallas_call(weight_kernel, name='weight_parts', grid=(1,), in_specs=[p...  3.19 us
  transfers between devices with their start and end apart: 10, of which 6 were waited for; matrix products, arithmetic and copies ran while one was open for 0% of the time, Pallas kernels for 31%

profile of v1, /device:TPU:0, one launch (start us, length us, event | category | flops | bytes accessed | tf_op | source)
XLA Modules:
  0.0 63.6 jit_solution(8759249982645199075)
XLA Ops:
  0.6 5.8 %block_states.1 = (bf16[512,128]{1,0:T(8,128)(2,1)}, bf16[512,128]{1,0:T(8,128)(2,1)}, f32[4,8,512]{2,1,0:T(8,128)}, f32[4,512,8]{2,1,0:T(8,128)}, bf16[64,512]{...) custom-call(bf16[1,512,2048]{2,1,0:T(8,128)(2,1)} %tokens_ref.3, ...), custom_call_target="tpu_custom_call" | custom-call | flops 268435456 | bytes 5242880 | tf_op jit(solution)/shard_map/block_states/pallas_call | solution.py:143
  6.4 3.1 %collective-permute-start = (bf16[144,512]{1,0:T(8,128)(2,1)}, bf16[144,512]{1,0:T(8,128)(2,1)S(1)}, u32[]{:S(2)}, u32[]{:S(2)}) collective-permute-start(bf16[144,512]{1,0:T(8,128)(2,1)} %get-tuple-element.25), channel_id=1, source_target_pairs={{0,1},{1,0},{2,3},{3,2},{4,5},{5,4},{6,7},{7,6},{8,9},{9,8},{10,11... | collective-permute-start | bytes 442376 | tf_op jit(solution)/shard_map/ppermute | solution.py:519
  9.5 2.6 %collective-permute-start.1 = (bf16[144,512]{1,0:T(8,128)(2,1)}, bf16[144,512]{1,0:T(8,128)(2,1)S(1)}, u32[]{:S(2)}, u32[]{:S(2)}) collective-permute-start(bf16[144,512]{1,0:T(8,128)(2,1)} %get-tuple-element.26), channel_id=1, source_target_pairs={{0,2},{1,3},{2,0},{3,1},{4,6},{5,7},{6,4},{7,5},{8,10},{9,11},{10,... | collective-permute-start | bytes 442376 | tf_op jit(solution)/shard_map/ppermute | solution.py:519
  12.1 0.0 collective-permute-start.2
  12.1 15.6 %inside_block.1 = (f32[512,512]{1,0:T(8,128)}, f32[512,512]{1,0:T(8,128)}, f32[512,128]{1,0:T(8,128)}) custom-call(bf16[1,512,512]{2,1,0:T(8,128)(2,1)} %x_ref.5, bf16[1,512,512]{2,1,0:T(8,128)(2,1)} %g_ref.5, bf16[512,128]{1,0:T(8,128)(2,1)} %get-tuple-element.28.bc_ref, bf16[512,128]{1,0:T(8,128)(2,1)} %get-tuple-element.30.cb_ref, ...), custom_call_target="tpu_custom_call" | custom-call | flops 805306368 | bytes 4194304 | tf_op jit(solution)/shard_map/inside_block/pallas_call | solution.py:277
  27.8 0.0 copy-start.1
  27.8 0.0 collective-permute-done.2.r3_ref
  27.8 0.6 copy-done.1
  28.4 0.1 copy-done.2
  28.5 0.0 copy-done.3
  28.5 4.9 %add_carries.1 = (bf16[1,512,512]{2,1,0:T(8,128)(2,1)}, bf16[1,512,512]{2,1,0:T(8,128)(2,1)}, bf16[512,128]{1,0:T(8,128)(2,1)}) custom-call(bf16[144,512]{1,0:T(8,128)(2,1)} %copy-done.1, bf16[144,512]{1,0:T(8,128)(2,1)} %copy-done.2, bf16[144,512]{1,0:T(8,128)(2,1)} %copy-done.3, bf16[1,512,512]{2,1,0:T(8,128)(2,1)} %x_ref.5, bf16[1,512,512]{2,1,0:T(8,128)(2,1)} %g_ref.5, ...), custom_call_target="tpu_custom_call" | custom-call | flops 536870912 | bytes 5242880 | tf_op jit(solution)/shard_map/add_carries/pallas_call | solution.py:382
  33.4 2.6 %collective-permute-start.5 = (bf16[512,128]{1,0:T(8,128)(2,1)}, bf16[512,128]{1,0:T(8,128)(2,1)S(1)}, u32[]{:S(2)}, u32[]{:S(2)}) collective-permute-start(bf16[512,128]{1,0:T(8,128)(2,1)} %get-tuple-element.38.a0_ref), channel_id=1, source_target_pairs={{0,12},{4,8},{8,4},{12,0},{1,13},{5,9},{9,5},{13,1},{2,14},{6,10},... | collective-permute-start | bytes 393224 | tf_op jit(solution)/shard_map/ppermute | solution.py:519
  36.0 0.5 collective-permute-start.4
  36.5 0.4 collective-permute-start.3
  36.9 3.2 %collective-permute-done.5.a3_ref = bf16[512,128]{1,0:T(8,128)(2,1)S(1)} collective-permute-done((bf16[512,128]{1,0:T(8,128)(2,1)}, bf16[512,128]{1,0:T(8,128)(2,1)S(1)}, u32[]{:S(2)}, u32[]{:S(2)}) %collective-permute-start.5) | collective-permute-done | bytes 131104 | tf_op jit(solution)/shard_map/ppermute | solution.py:519
  40.1 1.9 %collective-permute-done.4.a2_ref = bf16[512,128]{1,0:T(8,128)(2,1)S(1)} collective-permute-done((bf16[512,128]{1,0:T(8,128)(2,1)}, bf16[512,128]{1,0:T(8,128)(2,1)S(1)}, u32[]{:S(2)}, u32[]{:S(2)}) %collective-permute-start.4) | collective-permute-done | bytes 131104 | tf_op jit(solution)/shard_map/ppermute | solution.py:519
  42.0 0.1 collective-permute-done.3.a1_ref
  42.1 0.6 copy-done.5
  42.7 0.7 %copy-done.6 = bf16[512,128]{1,0:T(8,128)(2,1)} copy-done((bf16[512,128]{1,0:T(8,128)(2,1)}, bf16[512,128]{1,0:T(8,128)(2,1)S(1)}, u32[]{:S(2)}) %copy-start.6) | copy-done | bytes 131096
  43.3 3.2 %weight_parts.1 = (bf16[512,128]{1,0:T(8,128)(2,1)}, bf16[4,128,256]{2,1,0:T(8,128)(2,1)}, f32[4,128,256]{2,1,0:T(8,128)}) custom-call(bf16[512,128]{1,0:T(8,128)(2,1)} %get-tuple-element.38.a0_ref, bf16[512,128]{1,0:T(8,128)(2,1)} %copy-done.6, bf16[512,128]{1,0:T(8,128)(2,1)} %copy-done.5, bf16[512,128]{1,0:T(8,128)(2,1)} %copy-done.4, ...), custom_call_target="tpu_custom_call" | custom-call | flops 268435456 | bytes 4194304 | tf_op jit(solution)/shard_map/weight_parts/pallas_call | solution.py:442
  46.5 1.7 %collective-permute-done.6.got_ref = bf16[4,128,256]{2,1,0:T(8,128)(2,1)S(1)} collective-permute-done((bf16[4,128,256]{2,1,0:T(8,128)(2,1)}, bf16[4,128,256]{2,1,0:T(8,128)(2,1)S(1)}, u32[]{:S(2)}, u32[]{:S(2)}) %collective-permute-start.6) | collective-permute-done | bytes 262176 | tf_op jit(solution)/shard_map/ppermute | solution.py:519
  48.3 0.7 %copy-done = bf16[4,128,256]{2,1,0:T(8,128)(2,1)} copy-done((bf16[4,128,256]{2,1,0:T(8,128)(2,1)}, bf16[4,128,256]{2,1,0:T(8,128)(2,1)S(1)}, u32[]{:S(2)}) %copy-start) | copy-done | bytes 262168
  49.0 1.9 %pair_sum.1 = (f32[128,256]{1,0:T(8,128)}, bf16[128,256]{1,0:T(8,128)(2,1)}, bf16[128,256]{1,0:T(8,128)(2,1)}, bf16[128,256]{1,0:T(8,128)(2,1)}) custom-call(f32[4,128,256]{2,1,0:T(8,128)} %get-tuple-element.40.keep_ref, bf16[4,128,256]{2,1,0:T(8,128)(2,1)} %copy-done), custom_call_target="tpu_custom_call" | custom-call | tf_op jit(solution)/shard_map/pair_sum/pallas_call | solution.py:473
  50.8 0.6 collective-permute-start.7
  51.4 3.5 %collective-permute-start.8 = (bf16[128,256]{1,0:T(8,128)(2,1)}, bf16[128,256]{1,0:T(8,128)(2,1)S(1)}, u32[]{:S(2)}, u32[]{:S(2)}) collective-permute-start(bf16[128,256]{1,0:T(8,128)(2,1)} %get-tuple-element.44), channel_id=1, source_target_pairs={{0,2},{1,3},{2,0},{3,1},{4,6},{5,7},{6,4},{7,5},{8,10},{9,11},{10,... | collective-permute-start | bytes 196616 | tf_op jit(solution)/shard_map/ppermute | solution.py:519
  54.9 0.3 collective-permute-start.9
  55.2 4.0 %input_grad.1 = bf16[1,512,2048]{2,1,0:T(8,128)(2,1)} custom-call(bf16[512,128]{1,0:T(8,128)(2,1)} %get-tuple-element.39.grad_ref, bf16[2048,128]{1,0:T(8,128)(2,1)} %w_ref.3), custom_call_target="tpu_custom_call" | custom-call | flops 268435456 | bytes 3145728 | tf_op jit(solution)/shard_map/input_grad/pallas_call | solution.py:507
  59.2 0.0 collective-permute-done.7.r1_ref
  59.2 0.6 %collective-permute-done.8.r2_ref = bf16[128,256]{1,0:T(8,128)(2,1)S(1)} collective-permute-done((bf16[128,256]{1,0:T(8,128)(2,1)}, bf16[128,256]{1,0:T(8,128)(2,1)S(1)}, u32[]{:S(2)}, u32[]{:S(2)}) %collective-permute-start.8) | collective-permute-done | bytes 65568 | tf_op jit(solution)/shard_map/ppermute | solution.py:519
  59.9 1.4 %collective-permute-done.9.r3_ref = bf16[128,256]{1,0:T(8,128)(2,1)S(1)} collective-permute-done((bf16[128,256]{1,0:T(8,128)(2,1)}, bf16[128,256]{1,0:T(8,128)(2,1)S(1)}, u32[]{:S(2)}, u32[]{:S(2)}) %collective-permute-start.9) | collective-permute-done | bytes 65568 | tf_op jit(solution)/shard_map/ppermute | solution.py:519
  61.3 0.6 copy-done.9
  61.9 1.7 %final_sum.1 = f32[256,128]{1,0:T(8,128)} custom-call(f32[128,256]{1,0:T(8,128)} %get-tuple-element.42.own_ref, bf16[128,256]{1,0:T(8,128)(2,1)} %copy-done.7, bf16[128,256]{1,0:T(8,128)(2,1)} %copy-done.8, bf16[128,256]{1,0:T(8,128)(2,1)} %copy-done.9), custom_call_target="tpu_custom_call" | custom-call | tf_op jit(solution)/shard_map/final_sum/pallas_call | solution.py:489
  (15 shorter events, 0.0 us)
Async XLA Ops:
  6.4 21.3 %collective-permute-start = (bf16[144,512]{1,0:T(8,128)(2,1)}, bf16[144,512]{1,0:T(8,128)(2,1)S(1)}, u32[]{:S(2)}, u32[]{:S(2)}) collective-permute-start(bf16[144,512]{1,0:T(8,128)(2,1)} %get-tuple-element.25), channel_id=1, source_target_pairs={{0,1},{1,0},{2,3},{3,2},{4,5},{5,4},{6,7},{7,6},{8,9},{9,8},{10,11... | collective-permute-start | bytes 442376 | tf_op jit(solution)/shard_map/ppermute | solution.py:519
  9.5 18.3 %collective-permute-start.1 = (bf16[144,512]{1,0:T(8,128)(2,1)}, bf16[144,512]{1,0:T(8,128)(2,1)S(1)}, u32[]{:S(2)}, u32[]{:S(2)}) collective-permute-start(bf16[144,512]{1,0:T(8,128)(2,1)} %get-tuple-element.26), channel_id=1, source_target_pairs={{0,2},{1,3},{2,0},{3,1},{4,6},{5,7},{6,4},{7,5},{8,10},{9,11},{10,... | collective-permute-start | bytes 442376 | tf_op jit(solution)/shard_map/ppermute | solution.py:519
  12.1 15.7 %collective-permute-start.2 = (bf16[144,512]{1,0:T(8,128)(2,1)}, bf16[144,512]{1,0:T(8,128)(2,1)S(1)}, u32[]{:S(2)}, u32[]{:S(2)}) collective-permute-start(bf16[144,512]{1,0:T(8,128)(2,1)} %get-tuple-element.27), channel_id=1, source_target_pairs={{0,3},{1,2},{2,1},{3,0},{4,7},{5,6},{6,5},{7,4},{8,11},{9,10},{10,... | collective-permute-start | bytes 442376 | tf_op jit(solution)/shard_map/ppermute | solution.py:519
  27.8 0.7 %copy-start.1 = (bf16[144,512]{1,0:T(8,128)(2,1)}, bf16[144,512]{1,0:T(8,128)(2,1)S(1)}, u32[]{:S(2)}) copy-start(bf16[144,512]{1,0:T(8,128)(2,1)S(1)} %collective-permute-done.r1_ref) | copy-start | bytes 442372
  27.8 0.7 %copy-start.2 = (bf16[144,512]{1,0:T(8,128)(2,1)}, bf16[144,512]{1,0:T(8,128)(2,1)S(1)}, u32[]{:S(2)}) copy-start(bf16[144,512]{1,0:T(8,128)(2,1)S(1)} %collective-permute-done.1.r2_ref) | copy-start | bytes 442372
  27.8 0.7 %copy-start.3 = (bf16[144,512]{1,0:T(8,128)(2,1)}, bf16[144,512]{1,0:T(8,128)(2,1)S(1)}, u32[]{:S(2)}) copy-start(bf16[144,512]{1,0:T(8,128)(2,1)S(1)} %collective-permute-done.2.r3_ref) | copy-start | bytes 442372
  33.4 6.8 %collective-permute-start.5 = (bf16[512,128]{1,0:T(8,128)(2,1)}, bf16[512,128]{1,0:T(8,128)(2,1)S(1)}, u32[]{:S(2)}, u32[]{:S(2)}) collective-permute-start(bf16[512,128]{1,0:T(8,128)(2,1)} %get-tuple-element.38.a0_ref), channel_id=1, source_target_pairs={{0,12},{4,8},{8,4},{12,0},{1,13},{5,9},{9,5},{13,1},{2,14},{6,10},... | collective-permute-start | bytes 393224 | tf_op jit(solution)/shard_map/ppermute | solution.py:519
  36.0 6.0 %collective-permute-start.4 = (bf16[512,128]{1,0:T(8,128)(2,1)}, bf16[512,128]{1,0:T(8,128)(2,1)S(1)}, u32[]{:S(2)}, u32[]{:S(2)}) collective-permute-start(bf16[512,128]{1,0:T(8,128)(2,1)} %get-tuple-element.38.a0_ref), channel_id=1, source_target_pairs={{0,8},{4,12},{8,0},{12,4},{1,9},{5,13},{9,1},{13,5},{2,10},{6,14},... | collective-permute-start | bytes 393224 | tf_op jit(solution)/shard_map/ppermute | solution.py:519
  36.5 5.6 %collective-permute-start.3 = (bf16[512,128]{1,0:T(8,128)(2,1)}, bf16[512,128]{1,0:T(8,128)(2,1)S(1)}, u32[]{:S(2)}, u32[]{:S(2)}) collective-permute-start(bf16[512,128]{1,0:T(8,128)(2,1)} %get-tuple-element.38.a0_ref), channel_id=1, source_target_pairs={{0,4},{4,0},{8,12},{12,8},{1,5},{5,1},{9,13},{13,9},{2,6},{6,2},{1... | collective-permute-start | bytes 393224 | tf_op jit(solution)/shard_map/ppermute | solution.py:519
  40.1 2.0 %copy-start.4 = (bf16[512,128]{1,0:T(8,128)(2,1)}, bf16[512,128]{1,0:T(8,128)(2,1)S(1)}, u32[]{:S(2)}) copy-start(bf16[512,128]{1,0:T(8,128)(2,1)S(1)} %collective-permute-done.5.a3_ref) | copy-start | bytes 393220
  42.0 0.7 %copy-start.5 = (bf16[512,128]{1,0:T(8,128)(2,1)}, bf16[512,128]{1,0:T(8,128)(2,1)S(1)}, u32[]{:S(2)}) copy-start(bf16[512,128]{1,0:T(8,128)(2,1)S(1)} %collective-permute-done.4.a2_ref) | copy-start | bytes 393220
  42.7 0.7 %copy-start.6 = (bf16[512,128]{1,0:T(8,128)(2,1)}, bf16[512,128]{1,0:T(8,128)(2,1)S(1)}, u32[]{:S(2)}) copy-start(bf16[512,128]{1,0:T(8,128)(2,1)S(1)} %collective-permute-done.3.a1_ref) | copy-start | bytes 393220
  46.5 1.7 %collective-permute-start.6 = (bf16[4,128,256]{2,1,0:T(8,128)(2,1)}, bf16[4,128,256]{2,1,0:T(8,128)(2,1)S(1)}, u32[]{:S(2)}, u32[]{:S(2)}) collective-permute-start(bf16[4,128,256]{2,1,0:T(8,128)(2,1)} %get-tuple-element.41), channel_id=1, source_target_pairs={{0,16},{16,0},{1,17},{17,1},{2,18},{18,2},{3,19},{19,3},{4,20},{20... | collective-permute-start | bytes 786440 | tf_op jit(solution)/shard_map/ppermute | solution.py:519
  48.3 0.7 %copy-start = (bf16[4,128,256]{2,1,0:T(8,128)(2,1)}, bf16[4,128,256]{2,1,0:T(8,128)(2,1)S(1)}, u32[]{:S(2)}) copy-start(bf16[4,128,256]{2,1,0:T(8,128)(2,1)S(1)} %collective-permute-done.6.got_ref) | copy-start | bytes 786436
  50.8 8.4 %collective-permute-start.7 = (bf16[128,256]{1,0:T(8,128)(2,1)}, bf16[128,256]{1,0:T(8,128)(2,1)S(1)}, u32[]{:S(2)}, u32[]{:S(2)}) collective-permute-start(bf16[128,256]{1,0:T(8,128)(2,1)} %get-tuple-element.43), channel_id=1, source_target_pairs={{0,1},{1,0},{2,3},{3,2},{4,5},{5,4},{6,7},{7,6},{8,9},{9,8},{10,11... | collective-permute-start | bytes 196616 | tf_op jit(solution)/shard_map/ppermute | solution.py:519
  51.4 8.5 %collective-permute-start.8 = (bf16[128,256]{1,0:T(8,128)(2,1)}, bf16[128,256]{1,0:T(8,128)(2,1)S(1)}, u32[]{:S(2)}, u32[]{:S(2)}) collective-permute-start(bf16[128,256]{1,0:T(8,128)(2,1)} %get-tuple-element.44), channel_id=1, source_target_pairs={{0,2},{1,3},{2,0},{3,1},{4,6},{5,7},{6,4},{7,5},{8,10},{9,11},{10,... | collective-permute-start | bytes 196616 | tf_op jit(solution)/shard_map/ppermute | solution.py:519
  54.9 6.4 %collective-permute-start.9 = (bf16[128,256]{1,0:T(8,128)(2,1)}, bf16[128,256]{1,0:T(8,128)(2,1)S(1)}, u32[]{:S(2)}, u32[]{:S(2)}) collective-permute-start(bf16[128,256]{1,0:T(8,128)(2,1)} %get-tuple-element.45), channel_id=1, source_target_pairs={{0,3},{1,2},{2,1},{3,0},{4,7},{5,6},{6,5},{7,4},{8,11},{9,10},{10,... | collective-permute-start | bytes 196616 | tf_op jit(solution)/shard_map/ppermute | solution.py:519
  59.2 2.0 %copy-start.7 = (bf16[128,256]{1,0:T(8,128)(2,1)}, bf16[128,256]{1,0:T(8,128)(2,1)S(1)}, u32[]{:S(2)}) copy-start(bf16[128,256]{1,0:T(8,128)(2,1)S(1)} %collective-permute-done.7.r1_ref) | copy-start | bytes 196612
  59.9 1.4 %copy-start.8 = (bf16[128,256]{1,0:T(8,128)(2,1)}, bf16[128,256]{1,0:T(8,128)(2,1)S(1)}, u32[]{:S(2)}) copy-start(bf16[128,256]{1,0:T(8,128)(2,1)S(1)} %collective-permute-done.8.r2_ref) | copy-start | bytes 196612
  61.3 0.6 %copy-start.9 = (bf16[128,256]{1,0:T(8,128)(2,1)}, bf16[128,256]{1,0:T(8,128)(2,1)S(1)}, u32[]{:S(2)}) copy-start(bf16[128,256]{1,0:T(8,128)(2,1)S(1)} %collective-permute-done.9.r3_ref) | copy-start | bytes 196612

commit v2 on v1

v2 whole, which is shorter than its diff:
```python
import functools

import jax
import jax.numpy as jnp
from jax import lax
from jax.experimental import pallas as pl
from jax.experimental.pallas import tpu as pltpu
from jax.sharding import PartitionSpec as P

F32 = jnp.float32
BF16 = jnp.bfloat16
VMEM_SPEC = pl.BlockSpec(memory_space=pltpu.VMEM)
SMEM_SPEC = pl.BlockSpec(memory_space=pltpu.SMEM)
EXTRA = 16


def mm(a, b):
    return jnp.dot(a, b, preferred_element_type=F32)


def mm_t(a, b):
    return lax.dot_general(a, b, (((1,), (1,)), ((), ())), preferred_element_type=F32)


LIMIT = pltpu.CompilerParams(vmem_limit_bytes=20 << 20)
HBM_SPEC = pl.BlockSpec(memory_space=pltpu.HBM)
CHUNKS = 2


def log2(n):
    return n.bit_length() - 1


def spread_matrix(heads, width):
    rows = 8 * heads
    row = lax.broadcasted_iota(jnp.int32, (rows, 4 * width), 0)
    col = lax.broadcasted_iota(jnp.int32, (rows, 4 * width), 1)
    kind_ok = (row >> log2(2 * heads)) == (col >> log2(width))
    head_ok = (row & (heads - 1)) == ((col & (width - 1)) >> log2(width // heads))
    return jnp.where(kind_ok & head_ok, 1.0, 0.0).astype(BF16)


def states_kernel(
    n_seq, tokens_hbm, x_hbm, g_hbm, dt_hbm, w_hbm, rate_hbm, bias_hbm,
    bc_ref, cb_ref, rows_ref, decs_ref, spread_ref, scaled_ref, near_ref, coef_ref, pay1_ref, pay2_ref, pay3_ref,
    tok_ref, x_ref, g_ref, dt_ref, w_ref, rate_ref, bias_ref, sems,
):
    heads, length = dt_ref.shape
    chunk = length // CHUNKS
    width = x_ref.shape[1]
    copies = [
        pltpu.make_async_copy(dt_hbm.at[0], dt_ref, sems.at[0]),
        pltpu.make_async_copy(rate_hbm, rate_ref, sems.at[1]),
        pltpu.make_async_copy(bias_hbm, bias_ref, sems.at[2]),
        pltpu.make_async_copy(w_hbm, w_ref, sems.at[3]),
        pltpu.make_async_copy(tokens_hbm.at[0, :chunk], tok_ref.at[:chunk], sems.at[4]),
        pltpu.make_async_copy(x_hbm.at[0], x_ref, sems.at[5]),
        pltpu.make_async_copy(g_hbm.at[0], g_ref, sems.at[6]),
        pltpu.make_async_copy(tokens_hbm.at[0, chunk:], tok_ref.at[chunk:], sems.at[7]),
    ]
    for c in copies:
        c.start()
    spread = spread_matrix(heads, width)
    spread_ref[...] = spread
    for c in copies[:3]:
        c.wait()
    sub = lax.broadcasted_iota(jnp.int32, (heads, 1), 0)
    rate = jnp.zeros((heads, 1), F32)
    bias = jnp.zeros((heads, 1), F32)
    for h in range(heads):
        rate = jnp.where(sub == h, rate_ref[h], rate)
        bias = jnp.where(sub == h, bias_ref[h], bias)
    v = dt_ref[...] + bias
    log_step = -rate * (jnp.maximum(v, 0.0) + jnp.log1p(jnp.exp(-jnp.abs(v))))
    lane = lax.broadcasted_iota(jnp.int32, (heads, length), 1)
    cum = log_step
    shift = 1
    while shift < length:
        cum = cum + jnp.where(lane >= shift, pltpu.roll(cum, shift, 1), 0.0)
        shift *= 2
    prev = cum - log_step
    middle = cum[:, chunk - 1 : chunk]
    final = cum[:, length - 1 : length]
    second = lane >= chunk
    begin = jnp.where(second, middle, 0.0)
    end = jnp.where(second, final, middle)
    kinds = (jnp.exp(cum - begin), jnp.exp(end - prev), jnp.exp(jnp.minimum(prev - begin, 0.0)), jnp.exp(end - cum))
    parts = []
    for k in kinds:
        high = k.astype(BF16).astype(F32)
        parts += [high, k - high]
    decs = jnp.concatenate(parts, axis=0)
    decs_ref[...] = decs.astype(BF16)
    for p in range(heads // 2):
        rows_ref[p] = jnp.concatenate(
            [cum[2 * p : 2 * p + 1], prev[2 * p : 2 * p + 1], cum[2 * p + 1 : 2 * p + 2], prev[2 * p + 1 : 2 * p + 2]]
            + [jnp.zeros((4, length), F32)],
            axis=0,
        )
    head_of = lax.broadcasted_iota(jnp.int32, (heads, width), 1) >> log2(width // heads)
    mine = head_of == lax.broadcasted_iota(jnp.int32, (heads, width), 0)
    to_lanes = lambda col: jnp.sum(jnp.where(mine, col, 0.0), axis=0, keepdims=True)
    decay = to_lanes(jnp.exp(final))
    first_decay = to_lanes(jnp.exp(middle))
    second_decay = to_lanes(jnp.exp(final - middle))
    row8 = lax.broadcasted_iota(jnp.int32, (8, width), 0)
    coef_ref[...] = jnp.where(row8 == 0, first_decay, jnp.where(row8 == 1, second_decay, 0.0))
    high = decay.astype(BF16).astype(F32)
    row16 = lax.broadcasted_iota(jnp.int32, (EXTRA, width), 0)
    last = jnp.where(row16 == 0, high, jnp.where(row16 == 1, decay - high, 0.0)).astype(BF16)

    onward, backward = [], []
    for q in range(CHUNKS):
        at = slice(q * chunk, (q + 1) * chunk)
        e = mm(decs[:, at].T.astype(BF16), spread)
        if q == 0:
            copies[3].wait()
            copies[4].wait()
        else:
            copies[7].wait()
        projected = mm(tok_ref[at], w_ref[...])
        half = projected.shape[1] // 2
        bc_ref[at] = projected.astype(BF16)
        turned = pltpu.roll(projected, half, 1)
        cb_ref[at] = turned.astype(BF16)
        cb_t = turned.T.astype(BF16)
        if q == 0:
            copies[5].wait()
            copies[6].wait()
        x = x_ref[at].astype(F32)
        g = g_ref[at].astype(F32)
        g_up = (g * e[:, :width]).astype(BF16)
        g_down = (g * e[:, width : 2 * width]).astype(BF16)
        x_up = (x * e[:, 2 * width : 3 * width]).astype(BF16)
        x_down = (x * e[:, 3 * width :]).astype(BF16)
        scaled_ref[at, :width] = g_up
        scaled_ref[at, width : 2 * width] = g_down
        scaled_ref[at, 2 * width : 3 * width] = x_up
        scaled_ref[at, 3 * width :] = x_down
        onward.append(jnp.concatenate([mm(cb_t[:half], g_down), mm(cb_t[half:], x_down)], axis=0))
        backward.append(jnp.concatenate([mm(cb_t[:half], g_up), mm(cb_t[half:], x_up)], axis=0))

    near_ref[0] = onward[0]
    near_ref[1] = backward[1]
    next_total = (onward[0] * second_decay + onward[1]).astype(BF16)
    prior_total = (backward[0] + first_decay * backward[1]).astype(BF16)
    rows = next_total.shape[0]
    for k, ref in ((1, pay1_ref), (2, pay2_ref), (3, pay3_ref)):
        ref[rows:] = last
        if n_seq == 4:
            here = lax.axis_index("seq")
            up = (here ^ k) > here

            @pl.when(up)
            def _():
                ref[:rows] = next_total

            @pl.when(jnp.logical_not(up))
            def _():
                ref[:rows] = prior_total
        else:
            ref[:rows] = next_total if k == 1 else prior_total


def block_states(n_seq, tokens, x, g, dt, w, rate, bias):
    _, length, depth = tokens.shape
    width = x.shape[2]
    heads = dt.shape[1]
    two_n = w.shape[1]
    pay = jax.ShapeDtypeStruct((two_n + EXTRA, width), BF16)
    return pl.pallas_call(
        functools.partial(states_kernel, n_seq),
        name="block_states",
        in_specs=[HBM_SPEC] * 7,
        out_specs=[VMEM_SPEC] * 11,
        out_shape=[
            jax.ShapeDtypeStruct((length, two_n), BF16),
            jax.ShapeDtypeStruct((length, two_n), BF16),
            jax.ShapeDtypeStruct((heads // 2, 8, length), F32),
            jax.ShapeDtypeStruct((8 * heads, length), BF16),
            jax.ShapeDtypeStruct((8 * heads, 4 * width), BF16),
            jax.ShapeDtypeStruct((length, 4 * width), BF16),
            jax.ShapeDtypeStruct((2, two_n, width), F32),
            jax.ShapeDtypeStruct((8, width), F32),
            pay,
            pay,
            pay,
        ],
        scratch_shapes=[
            pltpu.VMEM((length, depth), BF16),
            pltpu.VMEM((length, width), BF16),
            pltpu.VMEM((length, width), BF16),
            pltpu.VMEM((heads, length), F32),
            pltpu.VMEM((depth, two_n), BF16),
            pltpu.SMEM((heads,), F32),
            pltpu.SMEM((heads,), F32),
            pltpu.SemaphoreType.DMA((8,)),
        ],
        compiler_params=LIMIT,
        cost_estimate=pl.CostEstimate(flops=2 * length * depth * two_n, bytes_accessed=5 << 20, transcendentals=0),
    )(*[pltpu.with_memory_space_constraint(a, pltpu.HBM) for a in (tokens, x, g, dt, w, rate, bias)])


def local_kernel(
    x_ref, g_ref, bc_ref, cb_ref, rows_ref, decs_ref, spread_ref, skip_ref,
    y_ref, gv_ref, gbc_ref, queries_ref, gvt_ref, gbt_ref, gc_ref,
):
    length, width = x_ref.shape[1:]
    lanes = 128
    n_pair = width // lanes
    chunk = length // CHUNKS
    tile = 128
    first_half = lax.broadcasted_iota(jnp.int32, (1, lanes), 1) < lanes // 2
    upper = lax.broadcasted_iota(jnp.int32, (lanes, 1), 0) < lanes // 2
    zero = jnp.zeros((), BF16)

    @pl.loop(0, CHUNKS)
    def _(q):
        s0 = pl.multiple_of(q * chunk, chunk)
        bc_s = bc_ref[pl.ds(s0, chunk), :]
        for tb in range(chunk // tile):
            t0 = pl.multiple_of(s0 + tb * tile, tile)
            cb_t = cb_ref[pl.ds(t0, tile), :]
            scores = mm_t(jnp.where(first_half, cb_t, zero), bc_s)
            row = tb * tile + lax.broadcasted_iota(jnp.int32, (tile, chunk), 0)
            col = lax.broadcasted_iota(jnp.int32, (tile, chunk), 1)
            below = col < row
            same = col == row
            total = None
            for p in range(n_pair):
                at = slice(p * lanes, (p + 1) * lanes)
                xp = x_ref[0, pl.ds(s0, chunk), at]
                x1, x2 = jnp.where(first_half, xp, zero), jnp.where(first_half, zero, xp)
                g_t = g_ref[0, pl.ds(t0, tile), at]
                gt = g_t.astype(F32).T.astype(BF16)
                cols = rows_ref[p, :, pl.ds(t0, tile)].T
                mains = []
                for k, xk in ((0, x1), (1, x2)):
                    gram = mm_t(g_t, xk)
                    cum_t, prev_t = cols[:, 2 * k : 2 * k + 1], cols[:, 2 * k + 1 : 2 * k + 2]
                    cum_s = rows_ref[p, 2 * k : 2 * k + 1, pl.ds(s0, chunk)]
                    prev_s = rows_ref[p, 2 * k + 1 : 2 * k + 2, pl.ds(s0, chunk)]
                    diff = jnp.minimum(jnp.where(below, cum_t - cum_s, prev_s - prev_t), 0.0)
                    kern = jnp.where(same, 0.0, jnp.exp(diff))
                    mains.append((scores * kern).astype(BF16))
                    term = gram * kern
                    total = term if total is None else total + term
                sk = jnp.where(first_half, skip_ref[2 * p], skip_ref[2 * p + 1])
                y = mm(mains[0], x1) + mm(mains[1], x2)
                y_ref[pl.ds(t0, tile), at] = y + sk * x_ref[0, pl.ds(t0, tile), at].astype(F32)
                gvt = mm(jnp.where(upper, gt, zero), mains[0]) + mm(jnp.where(upper, zero, gt), mains[1])
                if tb == 0:
                    gvt_ref[p] = gvt
                elif tb < chunk // tile - 1:
                    gvt_ref[p] += gvt
                else:
                    gs = g_ref[0, pl.ds(s0, chunk), at].astype(F32)
                    gv_ref[pl.ds(s0, chunk), at] = (gvt_ref[p] + gvt).T + sk * gs
            total = total.astype(BF16)
            gc_ref[tb * tile : (tb + 1) * tile] = mm(total, cb_ref[pl.ds(s0, chunk), :])
            gbt = mm(cb_t.astype(F32).T.astype(BF16), total)
            if tb == 0:
                gbt_ref[...] = gbt
            else:
                gbt_ref[...] += gbt
        gbc_ref[pl.ds(s0, chunk), :] = jnp.where(first_half, gbt_ref[...].T, gc_ref[...])

        e = mm(decs_ref[:, pl.ds(s0, chunk)].astype(F32).T.astype(BF16), spread_ref[...])
        bc = bc_s.astype(F32)
        cb = cb_ref[pl.ds(s0, chunk), :].astype(F32)
        cc, bb = jnp.where(first_half, cb, bc), jnp.where(first_half, bc, cb)
        for j, (query, kind) in enumerate(((cc, 0), (cc, 1), (bb, 2), (bb, 3))):
            for p in range(n_pair):
                value = query * e[:, kind * width + p * lanes : kind * width + (p + 1) * lanes]
                to = (j // 2) * 2 * width + p * 2 * lanes + (j % 2) * lanes
                queries_ref[pl.ds(s0, chunk), to : to + lanes] = value.astype(BF16)


def inside_chunks(x, g, bc, cb, rows, decs, spread, skip):
    _, length, width = x.shape
    n_pair = width // 128
    chunk = length // CHUNKS
    return pl.pallas_call(
        local_kernel,
        name="inside_chunks",
        in_specs=[VMEM_SPEC] * 7 + [SMEM_SPEC],
        out_specs=[VMEM_SPEC] * 4,
        out_shape=[
            jax.ShapeDtypeStruct((length, width), F32),
            jax.ShapeDtypeStruct((length, width), F32),
            jax.ShapeDtypeStruct((length, 128), F32),
            jax.ShapeDtypeStruct((length, 4 * width), BF16),
        ],
        scratch_shapes=[
            pltpu.VMEM((n_pair, 128, chunk), F32),
            pltpu.VMEM((128, chunk), F32),
            pltpu.VMEM((chunk, 128), F32),
        ],
        compiler_params=LIMIT,
        cost_estimate=pl.CostEstimate(
            flops=6 * length * length * width, bytes_accessed=4 << 20, transcendentals=2 * n_pair * length * length
        ),
    )(x, g, bc, cb, rows, decs, spread, skip)


def carry_kernel(
    direct, r1_ref, r2_ref, r3_ref, near_ref, coef_ref, queries_ref, scaled_ref, y_ref, gv_ref, gbc_ref,
    yo_ref, gvo_ref, group_ref, before_ref, after_ref,
):
    step = pl.program_id(0)
    _, two_n, width = before_ref.shape
    chunk = group_ref.shape[0]
    lanes = 128
    half = two_n // 2

    @pl.when(step == 0)
    def _():
        if direct:
            here = lax.axis_index("seq")
            refs = (r1_ref, r2_ref, r3_ref)
            decays = [r[two_n : two_n + 1].astype(F32) + r[two_n + 1 : two_n + 2].astype(F32) for r in refs]
            before = jnp.zeros((two_n, width), F32)
            after = jnp.zeros((two_n, width), F32)
            for k in (1, 2, 3):
                there = here ^ k
                low, high = jnp.minimum(here, there), jnp.maximum(here, there)
                factor = jnp.ones((1, width), F32)
                for m in (1, 2, 3):
                    if m != k:
                        mid = here ^ m
                        inside = jnp.logical_and(mid > low, mid < high)
                        factor = factor * jnp.where(inside, decays[m - 1], 1.0)
                part = refs[k - 1][:two_n].astype(F32)
                earlier = there < here
                before = before + part * jnp.where(earlier, factor, 0.0)
                after = after + part * jnp.where(earlier, 0.0, factor)
        else:
            before = r1_ref[:two_n].astype(F32)
            after = r2_ref[:two_n].astype(F32)
        before_ref[0] = before.astype(BF16)
        before_ref[1] = (near_ref[0] + coef_ref[0:1] * before).astype(BF16)
        after_ref[0] = (near_ref[1] + coef_ref[1:2] * after).astype(BF16)
        after_ref[1] = after.astype(BF16)

    before = before_ref[step]
    after = after_ref[step]
    first_half = lax.broadcasted_iota(jnp.int32, (1, lanes), 1) < lanes // 2
    zero = jnp.zeros((), BF16)
    s0 = pl.multiple_of(step * chunk, chunk)

    def apart(v):
        return [jnp.where(first_half, v, zero), jnp.where(first_half, zero, v)]

    for p in range(width // lanes):
        at = slice(p * lanes, (p + 1) * lanes)
        main = jnp.concatenate(apart(before[half:, at]) + apart(after[half:, at]), axis=0)
        back = jnp.concatenate(apart(before[:half, at]) + apart(after[:half, at]), axis=0)
        wide = slice(2 * p * lanes, 2 * (p + 1) * lanes)
        wide2 = slice(2 * width + 2 * p * lanes, 2 * width + 2 * (p + 1) * lanes)
        yo_ref[:, at] = (y_ref[pl.ds(s0, chunk), at] + mm(queries_ref[pl.ds(s0, chunk), wide], main)).astype(BF16)
        gvo_ref[:, at] = (gv_ref[pl.ds(s0, chunk), at] + mm(queries_ref[pl.ds(s0, chunk), wide2], back)).astype(BF16)
    both = jnp.concatenate([before, after], axis=1)
    from_g = mm_t(scaled_ref[pl.ds(s0, chunk), : 2 * width], both)
    from_x = mm_t(scaled_ref[pl.ds(s0, chunk), 2 * width :], both)
    group_ref[...] = (gbc_ref[pl.ds(s0, chunk), :] + jnp.where(first_half, from_x, from_g)).astype(BF16)


def add_carries(direct, r1, r2, r3, near, coef, queries, scaled, y, gv, gbc):
    length, width = y.shape
    two_n = gbc.shape[1]
    chunk = length // CHUNKS
    part3 = pl.BlockSpec((None, chunk, width), lambda i: (0, i, 0))
    return pl.pallas_call(
        functools.partial(carry_kernel, direct),
        name="add_carries",
        grid=(CHUNKS,),
        in_specs=[VMEM_SPEC] * 10,
        out_specs=[part3, part3, pl.BlockSpec((chunk, two_n), lambda i: (i, 0))],
        out_shape=[
            jax.ShapeDtypeStruct((1, length, width), BF16),
            jax.ShapeDtypeStruct((1, length, width), BF16),
            jax.ShapeDtypeStruct((length, two_n), BF16),
        ],
        scratch_shapes=[
            pltpu.VMEM((CHUNKS, two_n, width), BF16),
            pltpu.VMEM((CHUNKS, two_n, width), BF16),
        ],
        compiler_params=LIMIT,
        cost_estimate=pl.CostEstimate(flops=16 * length * two_n * width, bytes_accessed=5 << 20, transcendentals=0),
    )(r1, r2, r3, near, coef, queries, scaled, y, gv, gbc)


def scanned_generic(onward, backward, two_n):
    size, here = lax.axis_size("seq"), lax.axis_index("seq")

    def total(payload, reverse):
        every = lax.all_gather(payload, "seq")

        def step(k, before):
            at = size - 1 - k if reverse else k
            one = every[at].astype(F32)
            new = before * (one[two_n : two_n + 1] + one[two_n + 1 : two_n + 2]) + one[:two_n]
            return jnp.where(at > here if reverse else at < here, new, before)

        return lax.fori_loop(0, size, step, jnp.zeros((two_n, payload.shape[1]), F32))

    pad = lambda v: jnp.pad(v.astype(BF16), ((0, EXTRA), (0, 0)))
    return pad(total(onward, False)), pad(total(backward, True))


def weight_kernel(a0_ref, a1_ref, a2_ref, a3_ref, tokens_ref, grad_ref, send_ref, keep_ref):
    total = a0_ref[...].astype(F32) + a1_ref[...].astype(F32) + a2_ref[...].astype(F32) + a3_ref[...].astype(F32)
    grad = total.astype(BF16)
    grad_ref[...] = grad
    grad_t = grad.astype(F32).T.astype(BF16)
    here = lax.axis_index("dp")
    n_seq, _, cols = keep_ref.shape
    for s in range(n_seq):
        away = pl.multiple_of(((1 - here) * n_seq + s) * cols, cols)
        send_ref[s] = mm(grad_t, tokens_ref[:, pl.ds(away, cols)]).astype(BF16)
    for s in range(n_seq):
        home = pl.multiple_of((here * n_seq + s) * cols, cols)
        keep_ref[s] = mm(grad_t, tokens_ref[:, pl.ds(home, cols)])


def weight_parts(n_seq, groups, tokens):
    _, length, depth = tokens.shape
    two_n = groups[0].shape[1]
    cols = depth // (2 * n_seq)
    return pl.pallas_call(
        weight_kernel,
        name="weight_parts",
        grid=(1,),
        in_specs=[pl.BlockSpec((length, two_n), lambda i: (0, 0))] * 4
        + [pl.BlockSpec((None, length, depth), lambda i: (0, 0, 0))],
        out_specs=[
            pl.BlockSpec((length, two_n), lambda i: (0, 0)),
            pl.BlockSpec((n_seq, two_n, cols), lambda i: (0, 0, 0)),
            pl.BlockSpec((n_seq, two_n, cols), lambda i: (0, 0, 0)),
        ],
        out_shape=[
            jax.ShapeDtypeStruct((length, two_n), BF16),
            jax.ShapeDtypeStruct((n_seq, two_n, cols), BF16),
            jax.ShapeDtypeStruct((n_seq, two_n, cols), F32),
        ],
        compiler_params=LIMIT,
        cost_estimate=pl.CostEstimate(flops=2 * length * two_n * depth, bytes_accessed=4 << 20, transcendentals=0),
    )(*groups, tokens)


def pair_kernel(keep_ref, got_ref, own_ref, s1_ref, s2_ref, s3_ref):
    here = lax.axis_index("seq")
    own_ref[...] = keep_ref[here] + got_ref[here].astype(F32)
    for k, ref in ((1, s1_ref), (2, s2_ref), (3, s3_ref)):
        at = here ^ k
        ref[...] = (keep_ref[at] + got_ref[at].astype(F32)).astype(BF16)


def pair_sum(keep, got):
    _, two_n, cols = keep.shape
    small = jax.ShapeDtypeStruct((two_n, cols), BF16)
    return pl.pallas_call(
        pair_kernel,
        name="pair_sum",
        compiler_params=LIMIT,
        in_specs=[VMEM_SPEC, VMEM_SPEC],
        out_specs=[VMEM_SPEC] * 4,
        out_shape=[jax.ShapeDtypeStruct((two_n, cols), F32), small, small, small],
    )(keep, got)


def final_kernel(scale, own_ref, r1_ref, r2_ref, r3_ref, out_ref):
    total = own_ref[...] + r1_ref[...].astype(F32) + r2_ref[...].astype(F32) + r3_ref[...].astype(F32)
    out_ref[...] = total.T * scale


def final_sum(scale, own, r1, r2, r3):
    two_n, cols = own.shape
    return pl.pallas_call(
        functools.partial(final_kernel, scale),
        name="final_sum",
        compiler_params=LIMIT,
        in_specs=[VMEM_SPEC] * 4,
        out_specs=VMEM_SPEC,
        out_shape=jax.ShapeDtypeStruct((cols, two_n), F32),
    )(own, r1, r2, r3)


def input_kernel(grad_ref, w_ref, out_ref):
    out_ref[...] = mm_t(grad_ref[...], w_ref[...]).astype(BF16)


def input_grad(grad, w):
    length, two_n = grad.shape
    depth = w.shape[0]
    steps = 4
    chunk = length // steps
    return pl.pallas_call(
        input_kernel,
        name="input_grad",
        grid=(steps,),
        in_specs=[pl.BlockSpec((chunk, two_n), lambda i: (i, 0)), pl.BlockSpec((depth, two_n), lambda i: (0, 0))],
        out_specs=pl.BlockSpec((None, chunk, depth), lambda i: (0, i, 0)),
        out_shape=jax.ShapeDtypeStruct((1, length, depth), BF16),
        compiler_params=LIMIT,
        cost_estimate=pl.CostEstimate(flops=2 * length * two_n * depth, bytes_accessed=3 << 20, transcendentals=0),
    )(grad, w)


def swap(value, axis, k):
    return lax.ppermute(value, axis, [(i, i ^ k) for i in range(lax.axis_size(axis))])


def per_device(layer_input, head_values, dt_raw, w_bc, decay_rate, dt_bias, skip_gain, grad_y):
    n_seq, n_head, n_dp = lax.axis_size("seq"), lax.axis_size("head"), lax.axis_size("dp")
    length = layer_input.shape[1]
    two_n = w_bc.shape[1]
    bc, cb, rows, decs, spread, scaled, near, coef, pay1, pay2, pay3 = block_states(
        n_seq, layer_input, head_values, grad_y, dt_raw, w_bc, decay_rate, dt_bias
    )
    direct = n_seq == 4
    if direct:
        r1, r2, r3 = swap(pay1, "seq", 1), swap(pay2, "seq", 2), swap(pay3, "seq", 3)
    else:
        r1, r2 = scanned_generic(pay1, pay2, two_n)
        r3 = r2
    y_local, gv_local, gbc_local, queries = inside_chunks(
        head_values, grad_y, bc, cb, rows, decs, spread, skip_gain
    )
    y_out, grad_values, group = add_carries(
        direct, r1, r2, r3, near, coef, queries, scaled, y_local, gv_local, gbc_local
    )
    total_tokens = n_dp * n_seq * length
    if direct and n_dp == 2 and n_head == 4:
        groups = [group] + [swap(group, "head", k) for k in (1, 2, 3)]
        grad_bc, send, keep = weight_parts(n_seq, groups, layer_input)
        got = swap(send, "dp", 1)
        own, s1, s2, s3 = pair_sum(keep, got)
        grad_w_bc = final_sum(1.0 / total_tokens, own, swap(s1, "seq", 1), swap(s2, "seq", 2), swap(s3, "seq", 3))
    else:
        grad_bc = lax.psum(group.astype(F32), "head").astype(BF16)
        part = jnp.einsum("td,tk->dk", layer_input[0], grad_bc, preferred_element_type=F32)
        grad_w_bc = lax.psum_scatter(part, ("dp", "seq"), scatter_dimension=0, tiled=True) / total_tokens
    grad_input = input_grad(grad_bc, w_bc)
    return y_out, grad_values, grad_input, grad_w_bc


def solution(mesh):
    in_specs = (
        P("dp", "seq", None),
        P("dp", "seq", "head"),
        P("dp", "head", "seq"),
        P(),
        P("head"),
        P("head"),
        P("head"),
        P("dp", "seq", "head"),
    )
    out_specs = (
        P("dp", "seq", "head"),
        P("dp", "seq", "head"),
        P("dp", "seq", None),
        P(("dp", "seq"), None),
    )
    return jax.shard_map(per_device, mesh=mesh, in_specs=in_specs, out_specs=out_specs, check_vma=False)
```

time: 64.1 us -> 45.7 us (0.71)
  Pallas kernels: 37.1 us -> 15.3 us
  waiting for transfers between devices: 8.99 us -> 15.3 us
  local copies, waits for them, and re-layouts: 3.31 us -> 0.02 us
    pallas_call x3, Pallas kernels: 23.3 us -> 9.3 us  [the longest x1 5.13 us: inside_chunks(): pl.pallas_call(local_kernel, name='inside_chunks', in_specs=[VMEM_SPEC] *...]
    ppermute x10, waiting for transfers between devices: 8.99 us -> 15.3 us  [swap(): lax.ppermute(value, axis, [(i, i ^ k) for i in range(lax.axis_size(axis))])]
    unnamed x20 -> x10, local copies, waits for them, and re-layouts: 3.31 us -> 0.02 us
    pallas_call x1, Pallas kernels: 3.19 us -> 0.51 us  [weight_parts(): pl.pallas_call(weight_kernel, name='weight_parts', grid=(1,), in_specs=[p...]
    pallas_call x1, Pallas kernels: 4.87 us -> 2.21 us  [add_carries(): pl.pallas_call(functools.partial(carry_kernel, direct), name='add_carries...]
    pallas_call x1, Pallas kernels: 4 us -> 2.49 us  [input_grad(): pl.pallas_call(input_kernel, name='input_grad', grid=(steps,), in_specs=[...]
    pallas_call x1, Pallas kernels: 1.73 us -> 0.76 us  [final_sum(): pl.pallas_call(functools.partial(final_kernel, scale), name='final_sum',...]
    ppermute x10, starting transfers between devices: 13.6 us -> 14.2 us  [swap(): lax.ppermute(value, axis, [(i, i ^ k) for i in range(lax.axis_size(axis))])]
  transfers between devices with their start and end apart: 10 -> 10, of which waited for: 6 -> 6; matrix products, arithmetic and copies ran while one was open for 0% -> 0% of each run, Pallas kernels for 31% -> 17%
where the time goes in v2:
time: 45.7 us; the launch traced here: 45.6 us
  Pallas kernels  15.3 us (33%)
  waiting for transfers between devices  15.3 us (33%)
  starting transfers between devices  14.2 us (31%)
  between operations  0.72 us (2%)
    ppermute x10, waiting for transfers between devices, swap(): lax.ppermute(value, axis, [(i, i ^ k) for i in range(lax.axis_size(axis))])  15.3 us
    ppermute x10, starting transfers between devices, swap(): lax.ppermute(value, axis, [(i, i ^ k) for i in range(lax.axis_size(axis))])  14.2 us
    pallas_call x1, Pallas kernels, inside_chunks(): pl.pallas_call(local_kernel, name='inside_chunks', in_specs=[VMEM_SPEC] *...  5.13 us
    pallas_call x1, Pallas kernels, block_states(): pl.pallas_call(functools.partial(states_kernel, n_seq), name='block_state...  4.12 us
    pallas_call x1, Pallas kernels, input_grad(): pl.pallas_call(input_kernel, name='input_grad', grid=(steps,), in_specs=[...  2.49 us
    pallas_call x1, Pallas kernels, add_carries(): pl.pallas_call(functools.partial(carry_kernel, direct), name='add_carries...  2.21 us
  transfers between devices with their start and end apart: 10, of which 6 were waited for; matrix products, arithmetic and copies ran while one was open for 0% of the time, Pallas kernels for 17%

profile of v2, /device:TPU:0, one launch (start us, length us, event | category | flops | bytes accessed | tf_op | source)
XLA Modules:
  0.0 45.6 jit_solution(5026636139737927582)
XLA Ops:
  0.6 0.0 copy-start.3
  0.6 0.0 copy-start.2
  0.7 0.0 copy-start.4
  0.7 4.1 %block_states.1 = (bf16[512,128]{1,0:T(8,128)(2,1)S(1)}, bf16[512,128]{1,0:T(8,128)(2,1)S(1)}, f32[4,8,512]{2,1,0:T(8,128)S(1)}, bf16[64,512]{1,0:T(8,128)(2,1)S...) custom-call(bf16[1,512,2048]{2,1,0:T(8,128)(2,1)} %tokens_ref.1, ...), custom_call_target="tpu_custom_call" | custom-call | flops 268435456 | bytes 5242880 | tf_op jit(solution)/shard_map/block_states/pallas_call | solution.py:171
  4.8 3.1 %collective-permute-start = (bf16[144,512]{1,0:T(8,128)(2,1)S(1)}, bf16[144,512]{1,0:T(8,128)(2,1)S(1)}, u32[]{:S(2)}, u32[]{:S(2)}) collective-permute-start(bf16[144,512]{1,0:T(8,128)(2,1)S(1)} %get-tuple-element.29), channel_id=1, source_target_pairs={{0,1},{1,0},{2,3},{3,2},{4,5},{5,4},{6,7},{7,6},{8,9},{9,8},{10,11... | collective-permute-start | bytes 442376 | tf_op jit(solution)/shard_map/ppermute | solution.py:511
  7.9 2.6 %collective-permute-start.1 = (bf16[144,512]{1,0:T(8,128)(2,1)S(1)}, bf16[144,512]{1,0:T(8,128)(2,1)S(1)}, u32[]{:S(2)}, u32[]{:S(2)}) collective-permute-start(bf16[144,512]{1,0:T(8,128)(2,1)S(1)} %get-tuple-element.30), channel_id=1, source_target_pairs={{0,2},{1,3},{2,0},{3,1},{4,6},{5,7},{6,4},{7,5},{8,10},{9,11},{10,... | collective-permute-start | bytes 442376 | tf_op jit(solution)/shard_map/ppermute | solution.py:511
  10.5 0.0 collective-permute-start.2
  10.5 0.0 copy-done.3
  10.5 0.0 copy-done.2
  10.5 0.0 copy-done.4
  10.5 5.1 %inside_chunks.1 = (f32[512,512]{1,0:T(8,128)S(1)}, f32[512,512]{1,0:T(8,128)S(1)}, f32[512,128]{1,0:T(8,128)S(1)}, bf16[512,2048]{1,0:T(8,128)(2,1)S(1)}) custom-call(bf16[1,512,512]{2,1,0:T(8,128)(2,1)S(1)} %copy-done.2, bf16[1,512,512]{2,1,0:T(8,128)(2,1)S(1)} %copy-done.3, bf16[512,128]{1,0:T(8,128)(2,1)S(1)} %get-tuple-element.34.bc_ref, ...), custom_call_target="tpu_custom_call" | custom-call | flops 805306368 | bytes 4194304 | tf_op jit(solution)/shard_map/inside_chunks/pallas_call | solution.py:283
  15.6 0.0 collective-permute-done.r1_ref
  15.6 6.2 %collective-permute-done.1.r2_ref = bf16[144,512]{1,0:T(8,128)(2,1)S(1)} collective-permute-done((bf16[144,512]{1,0:T(8,128)(2,1)S(1)}, bf16[144,512]{1,0:T(8,128)(2,1)S(1)}, u32[]{:S(2)}, u32[]{:S(2)}) %collective-permute-start.1) | collective-permute-done | bytes 147488 | tf_op jit(solution)/shard_map/ppermute | solution.py:511
  21.9 0.0 collective-permute-done.2.r3_ref
  21.9 2.2 %add_carries.1 = (bf16[1,512,512]{2,1,0:T(8,128)(2,1)}, bf16[1,512,512]{2,1,0:T(8,128)(2,1)}, bf16[512,128]{1,0:T(8,128)(2,1)S(1)}) custom-call(bf16[144,512]{1,0:T(8,128)(2,1)S(1)} %collective-permute-done.r1_ref, bf16[144,512]{1,0:T(8,128)(2,1)S(1)} %collective-permute-done.1.r2_ref, bf16[144,512]{1,0:T(8,128)(2,1)S(1)} %collective-permute-done.2.r3_ref, ...), custom_call_target="tpu_custom_call" | custom-call | flops 536870912 | bytes 5242880 | tf_op jit(solution)/shard_map/add_carries/pallas_call | solution.py:373
  24.1 2.4 %collective-permute-start.5 = (bf16[512,128]{1,0:T(8,128)(2,1)S(1)}, bf16[512,128]{1,0:T(8,128)(2,1)S(1)}, u32[]{:S(2)}, u32[]{:S(2)}) collective-permute-start(bf16[512,128]{1,0:T(8,128)(2,1)S(1)} %get-tuple-element.46.a0_ref), channel_id=1, source_target_pairs={{0,12},{4,8},{8,4},{12,0},{1,13},{5,9},{9,5},{13,1},{2,14},{6,10},... | collective-permute-start | bytes 393224 | tf_op jit(solution)/shard_map/ppermute | solution.py:511
  26.5 0.5 %collective-permute-start.4 = (bf16[512,128]{1,0:T(8,128)(2,1)S(1)}, bf16[512,128]{1,0:T(8,128)(2,1)S(1)}, u32[]{:S(2)}, u32[]{:S(2)}) collective-permute-start(bf16[512,128]{1,0:T(8,128)(2,1)S(1)} %get-tuple-element.46.a0_ref), channel_id=1, source_target_pairs={{0,8},{4,12},{8,0},{12,4},{1,9},{5,13},{9,1},{13,5},{2,10},{6,14},... | collective-permute-start | bytes 393224 | tf_op jit(solution)/shard_map/ppermute | solution.py:511
  27.0 0.5 %collective-permute-start.3 = (bf16[512,128]{1,0:T(8,128)(2,1)S(1)}, bf16[512,128]{1,0:T(8,128)(2,1)S(1)}, u32[]{:S(2)}, u32[]{:S(2)}) collective-permute-start(bf16[512,128]{1,0:T(8,128)(2,1)S(1)} %get-tuple-element.46.a0_ref), channel_id=1, source_target_pairs={{0,4},{4,0},{8,12},{12,8},{1,5},{5,1},{9,13},{13,9},{2,6},{6,2},{1... | collective-permute-start | bytes 393224 | tf_op jit(solution)/shard_map/ppermute | solution.py:511
  27.6 2.6 %collective-permute-done.5.a3_ref = bf16[512,128]{1,0:T(8,128)(2,1)S(1)} collective-permute-done((bf16[512,128]{1,0:T(8,128)(2,1)S(1)}, bf16[512,128]{1,0:T(8,128)(2,1)S(1)}, u32[]{:S(2)}, u32[]{:S(2)}) %collective-permute-start.5) | collective-permute-done | bytes 131104 | tf_op jit(solution)/shard_map/ppermute | solution.py:511
  30.2 1.4 %collective-permute-done.4.a2_ref = bf16[512,128]{1,0:T(8,128)(2,1)S(1)} collective-permute-done((bf16[512,128]{1,0:T(8,128)(2,1)S(1)}, bf16[512,128]{1,0:T(8,128)(2,1)S(1)}, u32[]{:S(2)}, u32[]{:S(2)}) %collective-permute-start.4) | collective-permute-done | bytes 131104 | tf_op jit(solution)/shard_map/ppermute | solution.py:511
  31.6 0.4 collective-permute-done.3.a1_ref
  32.0 0.5 %weight_parts.1 = (bf16[512,128]{1,0:T(8,128)(2,1)S(1)}, bf16[4,128,256]{2,1,0:T(8,128)(2,1)S(1)}, f32[4,128,256]{2,1,0:T(8,128)S(1)}) custom-call(bf16[512,128]{1,0:T(8,128)(2,1)S(1)} %get-tuple-element.46.a0_ref, bf16[512,128]{1,0:T(8,128)(2,1)S(1)} %collective-permute-done.3.a1_ref, bf16[512,128]{1,0:T(8,128)(2,1)S(1)} %collective-permute-done.4.a2_ref, ...), custom_call_target="tpu_custom_call" | custom-call | flops 268435456 | bytes 4194304 | tf_op jit(solution)/shard_map/weight_parts/pallas_call | solution.py:430
  32.5 0.1 collective-permute-start.6
  32.6 1.5 %collective-permute-done.6.got_ref = bf16[4,128,256]{2,1,0:T(8,128)(2,1)S(1)} collective-permute-done((bf16[4,128,256]{2,1,0:T(8,128)(2,1)S(1)}, bf16[4,128,256]{2,1,0:T(8,128)(2,1)S(1)}, u32[]{:S(2)}, u32[]{:S(2)}) %collective-permute-start.6) | collective-permute-done | bytes 262176 | tf_op jit(solution)/shard_map/ppermute | solution.py:511
  34.2 2.4 %collective-permute-start.7 = (bf16[128,256]{1,0:T(8,128)(2,1)S(1)}, bf16[128,256]{1,0:T(8,128)(2,1)S(1)}, u32[]{:S(2)}, u32[]{:S(2)}) collective-permute-start(bf16[128,256]{1,0:T(8,128)(2,1)S(1)} %get-tuple-element.51), channel_id=1, source_target_pairs={{0,1},{1,0},{2,3},{3,2},{4,5},{5,4},{6,7},{7,6},{8,9},{9,8},{10,11... | collective-permute-start | bytes 196616 | tf_op jit(solution)/shard_map/ppermute | solution.py:511
  36.6 1.2 %collective-permute-start.8 = (bf16[128,256]{1,0:T(8,128)(2,1)S(1)}, bf16[128,256]{1,0:T(8,128)(2,1)S(1)}, u32[]{:S(2)}, u32[]{:S(2)}) collective-permute-start(bf16[128,256]{1,0:T(8,128)(2,1)S(1)} %get-tuple-element.52), channel_id=1, source_target_pairs={{0,2},{1,3},{2,0},{3,1},{4,6},{5,7},{6,4},{7,5},{8,10},{9,11},{10,... | collective-permute-start | bytes 196616 | tf_op jit(solution)/shard_map/ppermute | solution.py:511
  37.8 1.4 %collective-permute-start.9 = (bf16[128,256]{1,0:T(8,128)(2,1)S(1)}, bf16[128,256]{1,0:T(8,128)(2,1)S(1)}, u32[]{:S(2)}, u32[]{:S(2)}) collective-permute-start(bf16[128,256]{1,0:T(8,128)(2,1)S(1)} %get-tuple-element.53), channel_id=1, source_target_pairs={{0,3},{1,2},{2,1},{3,0},{4,7},{5,6},{6,5},{7,4},{8,11},{9,10},{10,... | collective-permute-start | bytes 196616 | tf_op jit(solution)/shard_map/ppermute | solution.py:511
  39.2 2.5 %input_grad.1 = bf16[1,512,2048]{2,1,0:T(8,128)(2,1)} custom-call(bf16[512,128]{1,0:T(8,128)(2,1)S(1)} %get-tuple-element.47.grad_ref, bf16[2048,128]{1,0:T(8,128)(2,1)S(1)} %copy-done.1), custom_call_target="tpu_custom_call" | custom-call | flops 268435456 | bytes 3145728 | tf_op jit(solution)/shard_map/input_grad/pallas_call | solution.py:498
  41.7 0.0 collective-permute-done.7.r1_ref
  41.7 3.1 %collective-permute-done.8.r2_ref = bf16[128,256]{1,0:T(8,128)(2,1)S(1)} collective-permute-done((bf16[128,256]{1,0:T(8,128)(2,1)S(1)}, bf16[128,256]{1,0:T(8,128)(2,1)S(1)}, u32[]{:S(2)}, u32[]{:S(2)}) %collective-permute-start.8) | collective-permute-done | bytes 65568 | tf_op jit(solution)/shard_map/ppermute | solution.py:511
  44.8 0.0 collective-permute-done.9.r3_ref
  44.8 0.8 %final_sum.1 = f32[256,128]{1,0:T(8,128)} custom-call(f32[128,256]{1,0:T(8,128)S(1)} %get-tuple-element.50.own_ref, bf16[128,256]{1,0:T(8,128)(2,1)S(1)} %collective-permute-done.7.r1_ref, bf16[128,256]{1,0:T(8,128)(2,1)S(1)} %collective-permute-done.8.r2_ref, bf16[128,256]{1,0:T(8,128)(2,1)S(1)} %collective-permute-done.9.r3_ref), custom_call_target="tpu_custom_call" | custom-call | tf_op jit(solution)/shard_map/final_sum/pallas_call | solution.py:479
  (5 shorter events, 0.1 us)
Async XLA Ops:
  0.6 9.8 %copy-start.3 = (bf16[1,512,512]{2,1,0:T(8,128)(2,1)S(1)}, bf16[1,512,512]{2,1,0:T(8,128)(2,1)}, u32[]{:S(2)}) copy-start(bf16[1,512,512]{2,1,0:T(8,128)(2,1)} %g_ref.1) | copy-start | bytes 1572868
  0.6 9.8 %copy-start.2 = (bf16[1,512,512]{2,1,0:T(8,128)(2,1)S(1)}, bf16[1,512,512]{2,1,0:T(8,128)(2,1)}, u32[]{:S(2)}) copy-start(bf16[1,512,512]{2,1,0:T(8,128)(2,1)} %x_ref.1) | copy-start | bytes 1572868
  0.7 9.8 %copy-start.4 = (f32[8]{0:T(128)S(1)}, f32[8]{0:T(128)}, u32[]{:S(2)}) copy-start(f32[8]{0:T(128)} %skip_ref.1) | copy-start | bytes 100
  4.8 10.9 %collective-permute-start = (bf16[144,512]{1,0:T(8,128)(2,1)S(1)}, bf16[144,512]{1,0:T(8,128)(2,1)S(1)}, u32[]{:S(2)}, u32[]{:S(2)}) collective-permute-start(bf16[144,512]{1,0:T(8,128)(2,1)S(1)} %get-tuple-element.29), channel_id=1, source_target_pairs={{0,1},{1,0},{2,3},{3,2},{4,5},{5,4},{6,7},{7,6},{8,9},{9,8},{10,11... | collective-permute-start | bytes 442376 | tf_op jit(solution)/shard_map/ppermute | solution.py:511
  7.9 14.0 %collective-permute-start.1 = (bf16[144,512]{1,0:T(8,128)(2,1)S(1)}, bf16[144,512]{1,0:T(8,128)(2,1)S(1)}, u32[]{:S(2)}, u32[]{:S(2)}) collective-permute-start(bf16[144,512]{1,0:T(8,128)(2,1)S(1)} %get-tuple-element.30), channel_id=1, source_target_pairs={{0,2},{1,3},{2,0},{3,1},{4,6},{5,7},{6,4},{7,5},{8,10},{9,11},{10,... | collective-permute-start | bytes 442376 | tf_op jit(solution)/shard_map/ppermute | solution.py:511
  10.5 11.4 %collective-permute-start.2 = (bf16[144,512]{1,0:T(8,128)(2,1)S(1)}, bf16[144,512]{1,0:T(8,128)(2,1)S(1)}, u32[]{:S(2)}, u32[]{:S(2)}) collective-permute-start(bf16[144,512]{1,0:T(8,128)(2,1)S(1)} %get-tuple-element.31), channel_id=1, source_target_pairs={{0,3},{1,2},{2,1},{3,0},{4,7},{5,6},{6,5},{7,4},{8,11},{9,10},{10,... | collective-permute-start | bytes 442376 | tf_op jit(solution)/shard_map/ppermute | solution.py:511
  21.9 10.1 %copy-start = (bf16[1,512,2048]{2,1,0:T(8,128)(2,1)S(1)}, bf16[1,512,2048]{2,1,0:T(8,128)(2,1)}, u32[]{:S(2)}) copy-start(bf16[1,512,2048]{2,1,0:T(8,128)(2,1)} %tokens_ref.1) | copy-start | bytes 6291460
  24.1 15.1 %copy-start.1 = (bf16[2048,128]{1,0:T(8,128)(2,1)S(1)}, bf16[2048,128]{1,0:T(8,128)(2,1)}, u32[]{:S(2)}) copy-start(bf16[2048,128]{1,0:T(8,128)(2,1)} %w_ref.1) | copy-start | bytes 1572868
  24.1 6.1 %collective-permute-start.5 = (bf16[512,128]{1,0:T(8,128)(2,1)S(1)}, bf16[512,128]{1,0:T(8,128)(2,1)S(1)}, u32[]{:S(2)}, u32[]{:S(2)}) collective-permute-start(bf16[512,128]{1,0:T(8,128)(2,1)S(1)} %get-tuple-element.46.a0_ref), channel_id=1, source_target_pairs={{0,12},{4,8},{8,4},{12,0},{1,13},{5,9},{9,5},{13,1},{2,14},{6,10},... | collective-permute-start | bytes 393224 | tf_op jit(solution)/shard_map/ppermute | solution.py:511
  26.5 5.0 %collective-permute-start.4 = (bf16[512,128]{1,0:T(8,128)(2,1)S(1)}, bf16[512,128]{1,0:T(8,128)(2,1)S(1)}, u32[]{:S(2)}, u32[]{:S(2)}) collective-permute-start(bf16[512,128]{1,0:T(8,128)(2,1)S(1)} %get-tuple-element.46.a0_ref), channel_id=1, source_target_pairs={{0,8},{4,12},{8,0},{12,4},{1,9},{5,13},{9,1},{13,5},{2,10},{6,14},... | collective-permute-start | bytes 393224 | tf_op jit(solution)/shard_map/ppermute | solution.py:511
  27.0 5.0 %collective-permute-start.3 = (bf16[512,128]{1,0:T(8,128)(2,1)S(1)}, bf16[512,128]{1,0:T(8,128)(2,1)S(1)}, u32[]{:S(2)}, u32[]{:S(2)}) collective-permute-start(bf16[512,128]{1,0:T(8,128)(2,1)S(1)} %get-tuple-element.46.a0_ref), channel_id=1, source_target_pairs={{0,4},{4,0},{8,12},{12,8},{1,5},{5,1},{9,13},{13,9},{2,6},{6,2},{1... | collective-permute-start | bytes 393224 | tf_op jit(solution)/shard_map/ppermute | solution.py:511
  32.5 1.6 %collective-permute-start.6 = (bf16[4,128,256]{2,1,0:T(8,128)(2,1)S(1)}, bf16[4,128,256]{2,1,0:T(8,128)(2,1)S(1)}, u32[]{:S(2)}, u32[]{:S(2)}) collective-permute-start(bf16[4,128,256]{2,1,0:T(8,128)(2,1)S(1)} %get-tuple-element.49), channel_id=1, source_target_pairs={{0,16},{16,0},{1,17},{17,1},{2,18},{18,2},{3,19},{19,3},{4,20},{20... | collective-permute-start | bytes 786440 | tf_op jit(solution)/shard_map/ppermute | solution.py:511
  34.2 7.5 %collective-permute-start.7 = (bf16[128,256]{1,0:T(8,128)(2,1)S(1)}, bf16[128,256]{1,0:T(8,128)(2,1)S(1)}, u32[]{:S(2)}, u32[]{:S(2)}) collective-permute-start(bf16[128,256]{1,0:T(8,128)(2,1)S(1)} %get-tuple-element.51), channel_id=1, source_target_pairs={{0,1},{1,0},{2,3},{3,2},{4,5},{5,4},{6,7},{7,6},{8,9},{9,8},{10,11... | collective-permute-start | bytes 196616 | tf_op jit(solution)/shard_map/ppermute | solution.py:511
  36.6 8.2 %collective-permute-start.8 = (bf16[128,256]{1,0:T(8,128)(2,1)S(1)}, bf16[128,256]{1,0:T(8,128)(2,1)S(1)}, u32[]{:S(2)}, u32[]{:S(2)}) collective-permute-start(bf16[128,256]{1,0:T(8,128)(2,1)S(1)} %get-tuple-element.52), channel_id=1, source_target_pairs={{0,2},{1,3},{2,0},{3,1},{4,6},{5,7},{6,4},{7,5},{8,10},{9,11},{10,... | collective-permute-start | bytes 196616 | tf_op jit(solution)/shard_map/ppermute | solution.py:511
  37.8 7.0 %collective-permute-start.9 = (bf16[128,256]{1,0:T(8,128)(2,1)S(1)}, bf16[128,256]{1,0:T(8,128)(2,1)S(1)}, u32[]{:S(2)}, u32[]{:S(2)}) collective-permute-start(bf16[128,256]{1,0:T(8,128)(2,1)S(1)} %get-tuple-element.53), channel_id=1, source_target_pairs={{0,3},{1,2},{2,1},{3,0},{4,7},{5,6},{6,5},{7,4},{8,11},{9,10},{10,... | collective-permute-start | bytes 196616 | tf_op jit(solution)/shard_map/ppermute | solution.py:511

commit v3 on v2

--- a/solution.py
+++ b/solution.py
@@ -11,7 +11,7 @@
 BF16 = jnp.bfloat16
 VMEM_SPEC = pl.BlockSpec(memory_space=pltpu.VMEM)
 SMEM_SPEC = pl.BlockSpec(memory_space=pltpu.SMEM)
-EXTRA = 16
+EXTRA = 8
 
 
 def mm(a, b):
@@ -52,10 +52,10 @@
         pltpu.make_async_copy(dt_hbm.at[0], dt_ref, sems.at[0]),
         pltpu.make_async_copy(rate_hbm, rate_ref, sems.at[1]),
         pltpu.make_async_copy(bias_hbm, bias_ref, sems.at[2]),
-        pltpu.make_async_copy(w_hbm, w_ref, sems.at[3]),
-        pltpu.make_async_copy(tokens_hbm.at[0, :chunk], tok_ref.at[:chunk], sems.at[4]),
-        pltpu.make_async_copy(x_hbm.at[0], x_ref, sems.at[5]),
-        pltpu.make_async_copy(g_hbm.at[0], g_ref, sems.at[6]),
+        pltpu.make_async_copy(g_hbm.at[0], g_ref, sems.at[3]),
+        pltpu.make_async_copy(x_hbm.at[0], x_ref, sems.at[4]),
+        pltpu.make_async_copy(w_hbm, w_ref, sems.at[5]),
+        pltpu.make_async_copy(tokens_hbm.at[0, :chunk], tok_ref.at[:chunk], sems.at[6]),
         pltpu.make_async_copy(tokens_hbm.at[0, chunk:], tok_ref.at[chunk:], sems.at[7]),
     ]
     for c in copies:
@@ -106,39 +106,31 @@
     row8 = lax.broadcasted_iota(jnp.int32, (8, width), 0)
     coef_ref[...] = jnp.where(row8 == 0, first_decay, jnp.where(row8 == 1, second_decay, 0.0))
     high = decay.astype(BF16).astype(F32)
-    row16 = lax.broadcasted_iota(jnp.int32, (EXTRA, width), 0)
-    last = jnp.where(row16 == 0, high, jnp.where(row16 == 1, decay - high, 0.0)).astype(BF16)
-
+    row_e = lax.broadcasted_iota(jnp.int32, (EXTRA, width), 0)
+    last = jnp.where(row_e == 0, high, jnp.where(row_e == 1, decay - high, 0.0)).astype(BF16)
+
+    copies[3].wait()
+    copies[4].wait()
+    for q in range(CHUNKS):
+        at = slice(q * chunk, (q + 1) * chunk)
+        spread_decs = decs[:, at].T.astype(BF16)
+        for j, (ref, kind) in enumerate(((g_ref, 0), (g_ref, 1), (x_ref, 2), (x_ref, 3))):
+            to = slice(j * width, (j + 1) * width)
+            scaled_ref[at, to] = (ref[at].astype(F32) * mm(spread_decs, spread[:, to])).astype(BF16)
+    copies[5].wait()
     onward, backward = [], []
     for q in range(CHUNKS):
         at = slice(q * chunk, (q + 1) * chunk)
-        e = mm(decs[:, at].T.astype(BF16), spread)
-        if q == 0:
-            copies[3].wait()
-            copies[4].wait()
-        else:
-            copies[7].wait()
+        copies[6 + q].wait()
         projected = mm(tok_ref[at], w_ref[...])
         half = projected.shape[1] // 2
         bc_ref[at] = projected.astype(BF16)
         turned = pltpu.roll(projected, half, 1)
         cb_ref[at] = turned.astype(BF16)
         cb_t = turned.T.astype(BF16)
-        if q == 0:
-            copies[5].wait()
-            copies[6].wait()
-        x = x_ref[at].astype(F32)
-        g = g_ref[at].astype(F32)
-        g_up = (g * e[:, :width]).astype(BF16)
-        g_down = (g * e[:, width : 2 * width]).astype(BF16)
-        x_up = (x * e[:, 2 * width : 3 * width]).astype(BF16)
-        x_down = (x * e[:, 3 * width :]).astype(BF16)
-        scaled_ref[at, :width] = g_up
-        scaled_ref[at, width : 2 * width] = g_down
-        scaled_ref[at, 2 * width : 3 * width] = x_up
-        scaled_ref[at, 3 * width :] = x_down
-        onward.append(jnp.concatenate([mm(cb_t[:half], g_down), mm(cb_t[half:], x_down)], axis=0))
-        backward.append(jnp.concatenate([mm(cb_t[:half], g_up), mm(cb_t[half:], x_up)], axis=0))
+        parts = [scaled_ref[at, j * width : (j + 1) * width] for j in range(4)]
+        onward.append(jnp.concatenate([mm(cb_t[:half], parts[1]), mm(cb_t[half:], parts[3])], axis=0))
+        backward.append(jnp.concatenate([mm(cb_t[:half], parts[0]), mm(cb_t[half:], parts[2])], axis=0))
 
     near_ref[0] = onward[0]
     near_ref[1] = backward[1]
@@ -303,45 +295,71 @@
     )(x, g, bc, cb, rows, decs, spread, skip)
 
 
-def carry_kernel(
-    direct, r1_ref, r2_ref, r3_ref, near_ref, coef_ref, queries_ref, scaled_ref, y_ref, gv_ref, gbc_ref,
-    yo_ref, gvo_ref, group_ref, before_ref, after_ref,
+def combine_received(direct, refs, two_n):
+    if not direct:
+        return refs[0][:two_n].astype(F32), refs[1][:two_n].astype(F32)
+    here = lax.axis_index("seq")
+    width = refs[0].shape[1]
+    decays = [r[two_n : two_n + 1].astype(F32) + r[two_n + 1 : two_n + 2].astype(F32) for r in refs]
+    before = jnp.zeros((two_n, width), F32)
+    after = jnp.zeros((two_n, width), F32)
+    for k in (1, 2, 3):
+        there = here ^ k
+        low, high = jnp.minimum(here, there), jnp.maximum(here, there)
+        factor = jnp.ones((1, width), F32)
+        for m in (1, 2, 3):
+            if m != k:
+                mid = here ^ m
+                inside = jnp.logical_and(mid > low, mid < high)
+                factor = factor * jnp.where(inside, decays[m - 1], 1.0)
+        part = refs[k - 1][:two_n].astype(F32)
+        earlier = there < here
+        before = before + part * jnp.where(earlier, factor, 0.0)
+        after = after + part * jnp.where(earlier, 0.0, factor)
+    return before, after
+
+
+def group_kernel(
+    direct, r3_ref, r2_ref, r1_ref, near_ref, coef_ref, scaled_ref, gbc_ref, group_ref, before_ref, after_ref
 ):
+    length, two_n = group_ref.shape
+    width = coef_ref.shape[1]
+    chunk = length // CHUNKS
+    before, after = combine_received(direct, (r1_ref, r2_ref, r3_ref), two_n)
+    befores = [before.astype(BF16), (near_ref[0] + coef_ref[0:1] * before).astype(BF16)]
+    afters = [(near_ref[1] + coef_ref[1:2] * after).astype(BF16), after.astype(BF16)]
+    left = lax.broadcasted_iota(jnp.int32, (1, two_n), 1) < two_n // 2
+    for q in range(CHUNKS):
+        at = slice(q * chunk, (q + 1) * chunk)
+        before_ref[q] = befores[q]
+        after_ref[q] = afters[q]
+        both = jnp.concatenate([befores[q], afters[q]], axis=1)
+        from_g = mm_t(scaled_ref[at, : 2 * width], both)
+        from_x = mm_t(scaled_ref[at, 2 * width :], both)
+        group_ref[at] = (gbc_ref[at] + jnp.where(left, from_x, from_g)).astype(BF16)
+
+
+def group_sums(direct, r3, r2, r1, near, coef, scaled, gbc):
+    length, two_n = gbc.shape
+    width = coef.shape[1]
+    state = jax.ShapeDtypeStruct((CHUNKS, two_n, width), BF16)
+    return pl.pallas_call(
+        functools.partial(group_kernel, direct),
+        name="group_sums",
+        in_specs=[VMEM_SPEC] * 7,
+        out_specs=[VMEM_SPEC] * 3,
+        out_shape=[jax.ShapeDtypeStruct((length, two_n), BF16), state, state],
+        compiler_params=LIMIT,
+        cost_estimate=pl.CostEstimate(flops=8 * length * two_n * width, bytes_accessed=3 << 20, transcendentals=0),
+    )(r3, r2, r1, near, coef, scaled, gbc)
+
+
+def carry_kernel(before_ref, after_ref, queries_ref, y_ref, gv_ref, yo_ref, gvo_ref):
     step = pl.program_id(0)
     _, two_n, width = before_ref.shape
-    chunk = group_ref.shape[0]
+    chunk = yo_ref.shape[0]
     lanes = 128
     half = two_n // 2
-
-    @pl.when(step == 0)
-    def _():
-        if direct:
-            here = lax.axis_index("seq")
-            refs = (r1_ref, r2_ref, r3_ref)
-            decays = [r[two_n : two_n + 1].astype(F32) + r[two_n + 1 : two_n + 2].astype(F32) for r in refs]
-            before = jnp.zeros((two_n, width), F32)
-            after = jnp.zeros((two_n, width), F32)
-            for k in (1, 2, 3):
-                there = here ^ k
-                low, high = jnp.minimum(here, there), jnp.maximum(here, there)
-                factor = jnp.ones((1, width), F32)
-                for m in (1, 2, 3):
-                    if m != k:
-                        mid = here ^ m
-                        inside = jnp.logical_and(mid > low, mid < high)
-                        factor = factor * jnp.where(inside, decays[m - 1], 1.0)
-                part = refs[k - 1][:two_n].astype(F32)
-                earlier = there < here
-                before = before + part * jnp.where(earlier, factor, 0.0)
-                after = after + part * jnp.where(earlier, 0.0, factor)
-        else:
-            before = r1_ref[:two_n].astype(F32)
-            after = r2_ref[:two_n].astype(F32)
-        before_ref[0] = before.astype(BF16)
-        before_ref[1] = (near_ref[0] + coef_ref[0:1] * before).astype(BF16)
-        after_ref[0] = (near_ref[1] + coef_ref[1:2] * after).astype(BF16)
-        after_ref[1] = after.astype(BF16)
-
     before = before_ref[step]
     after = after_ref[step]
     first_half = lax.broadcasted_iota(jnp.int32, (1, lanes), 1) < lanes // 2
@@ -359,35 +377,24 @@
         wide2 = slice(2 * width + 2 * p * lanes, 2 * width + 2 * (p + 1) * lanes)
         yo_ref[:, at] = (y_ref[pl.ds(s0, chunk), at] + mm(queries_ref[pl.ds(s0, chunk), wide], main)).astype(BF16)
         gvo_ref[:, at] = (gv_ref[pl.ds(s0, chunk), at] + mm(queries_ref[pl.ds(s0, chunk), wide2], back)).astype(BF16)
-    both = jnp.concatenate([before, after], axis=1)
-    from_g = mm_t(scaled_ref[pl.ds(s0, chunk), : 2 * width], both)
-    from_x = mm_t(scaled_ref[pl.ds(s0, chunk), 2 * width :], both)
-    group_ref[...] = (gbc_ref[pl.ds(s0, chunk), :] + jnp.where(first_half, from_x, from_g)).astype(BF16)
-
-
-def add_carries(direct, r1, r2, r3, near, coef, queries, scaled, y, gv, gbc):
+
+
+def add_carries(before, after, queries, y, gv):
     length, width = y.shape
-    two_n = gbc.shape[1]
+    two_n = before.shape[1]
     chunk = length // CHUNKS
     part3 = pl.BlockSpec((None, chunk, width), lambda i: (0, i, 0))
-    return pl.pallas_call(
-        functools.partial(carry_kernel, direct),
+    out = jax.ShapeDtypeStruct((1, length, width), BF16)
+    return pl.pallas_call(
+        carry_kernel,
         name="add_carries",
         grid=(CHUNKS,),
-        in_specs=[VMEM_SPEC] * 10,
-        out_specs=[part3, part3, pl.BlockSpec((chunk, two_n), lambda i: (i, 0))],
-        out_shape=[
-            jax.ShapeDtypeStruct((1, length, width), BF16),
-            jax.ShapeDtypeStruct((1, length, width), BF16),
-            jax.ShapeDtypeStruct((length, two_n), BF16),
-        ],
-        scratch_shapes=[
-            pltpu.VMEM((CHUNKS, two_n, width), BF16),
-            pltpu.VMEM((CHUNKS, two_n, width), BF16),
-        ],
-        compiler_params=LIMIT,
-        cost_estimate=pl.CostEstimate(flops=16 * length * two_n * width, bytes_accessed=5 << 20, transcendentals=0),
-    )(r1, r2, r3, near, coef, queries, scaled, y, gv, gbc)
+        in_specs=[VMEM_SPEC] * 5,
+        out_specs=[part3, part3],
+        out_shape=[out, out],
+        compiler_params=LIMIT,
+        cost_estimate=pl.CostEstimate(flops=8 * length * two_n * width, bytes_accessed=5 << 20, transcendentals=0),
+    )(before, after, queries, y, gv)
 
 
 def scanned_generic(onward, backward, two_n):
@@ -408,44 +415,59 @@
     return pad(total(onward, False)), pad(total(backward, True))
 
 
-def weight_kernel(a0_ref, a1_ref, a2_ref, a3_ref, tokens_ref, grad_ref, send_ref, keep_ref):
+def away_kernel(a0_ref, a1_ref, a2_ref, a3_ref, tokens_ref, grad_ref, grad_t_ref, send_ref):
     total = a0_ref[...].astype(F32) + a1_ref[...].astype(F32) + a2_ref[...].astype(F32) + a3_ref[...].astype(F32)
     grad = total.astype(BF16)
     grad_ref[...] = grad
     grad_t = grad.astype(F32).T.astype(BF16)
+    grad_t_ref[...] = grad_t
+    here = lax.axis_index("dp")
+    n_seq, _, cols = send_ref.shape
+    for s in range(n_seq):
+        away = pl.multiple_of(((1 - here) * n_seq + s) * cols, cols)
+        send_ref[s] = mm(grad_t, tokens_ref[0, :, pl.ds(away, cols)]).astype(BF16)
+
+
+def home_kernel(grad_t_ref, tokens_ref, keep_ref):
     here = lax.axis_index("dp")
     n_seq, _, cols = keep_ref.shape
     for s in range(n_seq):
-        away = pl.multiple_of(((1 - here) * n_seq + s) * cols, cols)
-        send_ref[s] = mm(grad_t, tokens_ref[:, pl.ds(away, cols)]).astype(BF16)
-    for s in range(n_seq):
         home = pl.multiple_of((here * n_seq + s) * cols, cols)
-        keep_ref[s] = mm(grad_t, tokens_ref[:, pl.ds(home, cols)])
-
-
-def weight_parts(n_seq, groups, tokens):
+        keep_ref[s] = mm(grad_t_ref[...], tokens_ref[0, :, pl.ds(home, cols)])
+
+
+def weight_away(n_seq, groups, tokens):
     _, length, depth = tokens.shape
     two_n = groups[0].shape[1]
     cols = depth // (2 * n_seq)
     return pl.pallas_call(
-        weight_kernel,
-        name="weight_parts",
-        grid=(1,),
-        in_specs=[pl.BlockSpec((length, two_n), lambda i: (0, 0))] * 4
-        + [pl.BlockSpec((None, length, depth), lambda i: (0, 0, 0))],
-        out_specs=[
-            pl.BlockSpec((length, two_n), lambda i: (0, 0)),
-            pl.BlockSpec((n_seq, two_n, cols), lambda i: (0, 0, 0)),
-            pl.BlockSpec((n_seq, two_n, cols), lambda i: (0, 0, 0)),
-        ],
+        away_kernel,
+        name="weight_away",
+        in_specs=[VMEM_SPEC] * 5,
+        out_specs=[VMEM_SPEC] * 3,
         out_shape=[
             jax.ShapeDtypeStruct((length, two_n), BF16),
+            jax.ShapeDtypeStruct((two_n, length), BF16),
             jax.ShapeDtypeStruct((n_seq, two_n, cols), BF16),
-            jax.ShapeDtypeStruct((n_seq, two_n, cols), F32),
         ],
         compiler_params=LIMIT,
-        cost_estimate=pl.CostEstimate(flops=2 * length * two_n * depth, bytes_accessed=4 << 20, transcendentals=0),
+        cost_estimate=pl.CostEstimate(flops=length * two_n * depth, bytes_accessed=2 << 20, transcendentals=0),
     )(*groups, tokens)
+
+
+def weight_home(n_seq, grad_t, tokens):
+    _, length, depth = tokens.shape
+    two_n = grad_t.shape[0]
+    cols = depth // (2 * n_seq)
+    return pl.pallas_call(
+        home_kernel,
+        name="weight_home",
+        in_specs=[VMEM_SPEC] * 2,
+        out_specs=VMEM_SPEC,
+        out_shape=jax.ShapeDtypeStruct((n_seq, two_n, cols), F32),
+        compiler_params=LIMIT,
+        cost_estimate=pl.CostEstimate(flops=length * two_n * depth, bytes_accessed=2 << 20, transcendentals=0),
+    )(grad_t, tokens)
 
 
 def pair_kernel(keep_ref, got_ref, own_ref, s1_ref, s2_ref, s3_ref):
@@ -469,12 +491,12 @@
     )(keep, got)
 
 
-def final_kernel(scale, own_ref, r1_ref, r2_ref, r3_ref, out_ref):
+def final_kernel(scale, own_ref, r3_ref, r2_ref, r1_ref, out_ref):
     total = own_ref[...] + r1_ref[...].astype(F32) + r2_ref[...].astype(F32) + r3_ref[...].astype(F32)
     out_ref[...] = total.T * scale
 
 
-def final_sum(scale, own, r1, r2, r3):
+def final_sum(scale, own, r3, r2, r1):
     two_n, cols = own.shape
     return pl.pallas_call(
         functools.partial(final_kernel, scale),
@@ -483,7 +505,7 @@
         in_specs=[VMEM_SPEC] * 4,
         out_specs=VMEM_SPEC,
         out_shape=jax.ShapeDtypeStruct((cols, two_n), F32),
-    )(own, r1, r2, r3)
+    )(own, r3, r2, r1)
 
 
 def input_kernel(grad_ref, w_ref, out_ref):
@@ -520,24 +542,26 @@
     )
     direct = n_seq == 4
     if direct:
-        r1, r2, r3 = swap(pay1, "seq", 1), swap(pay2, "seq", 2), swap(pay3, "seq", 3)
+        r3, r2, r1 = swap(pay3, "seq", 3), swap(pay2, "seq", 2), swap(pay1, "seq", 1)
     else:
         r1, r2 = scanned_generic(pay1, pay2, two_n)
         r3 = r2
     y_local, gv_local, gbc_local, queries = inside_chunks(
         head_values, grad_y, bc, cb, rows, decs, spread, skip_gain
     )
-    y_out, grad_values, group = add_carries(
-        direct, r1, r2, r3, near, coef, queries, scaled, y_local, gv_local, gbc_local
-    )
+    group, before, after = group_sums(direct, r3, r2, r1, near, coef, scaled, gbc_local)
     total_tokens = n_dp * n_seq * length
     if direct and n_dp == 2 and n_head == 4:
         groups = [group] + [swap(group, "head", k) for k in (1, 2, 3)]
-        grad_bc, send, keep = weight_parts(n_seq, groups, layer_input)
+        y_out, grad_values = add_carries(before, after, queries, y_local, gv_local)
+        grad_bc, grad_t, send = weight_away(n_seq, groups, layer_input)
         got = swap(send, "dp", 1)
+        keep = weight_home(n_seq, grad_t, layer_input)
         own, s1, s2, s3 = pair_sum(keep, got)
-        grad_w_bc = final_sum(1.0 / total_tokens, own, swap(s1, "seq", 1), swap(s2, "seq", 2), swap(s3, "seq", 3))
+        t3, t2, t1 = swap(s3, "seq", 3), swap(s2, "seq", 2), swap(s1, "seq", 1)
+        grad_w_bc = final_sum(1.0 / total_tokens, own, t3, t2, t1)
     else:
+        y_out, grad_values = add_carries(before, after, queries, y_local, gv_local)
         grad_bc = lax.psum(group.astype(F32), "head").astype(BF16)
         part = jnp.einsum("td,tk->dk", layer_input[0], grad_bc, preferred_element_type=F32)
         grad_w_bc = lax.psum_scatter(part, ("dp", "seq"), scatter_dimension=0, tiled=True) / total_tokens

time: 45.7 us -> 42.5 us (0.930)
  waiting for transfers between devices: 15.3 us -> 12.2 us
    ppermute x10, waiting for transfers between devices: 15.3 us -> 12.2 us  [swap(): lax.ppermute(value, axis, [(i, i ^ k) for i in range(lax.axis_size(axis))])]
    pallas_call x2 -> x4, Pallas kernels: 2.72 us -> 3.18 us  [the longest x1 1.66 us: add_carries(): pl.pallas_call(carry_kernel, name='add_carries', grid=(CHUNKS,), in_specs...]
  transfers between devices with their start and end apart: 10 -> 10, of which waited for: 6 -> 6; matrix products, arithmetic and copies ran while one was open for 0% -> 0% of each run, Pallas kernels for 17% -> 23%
where the time goes in v3:
time: 42.5 us; the launch traced here: 42.3 us
  Pallas kernels  15.6 us (37%)
  starting transfers between devices  13.8 us (32%)
  waiting for transfers between devices  12.2 us (29%)
  between operations  0.73 us (2%)
    ppermute x10, starting transfers between devices, swap(): lax.ppermute(value, axis, [(i, i ^ k) for i in range(lax.axis_size(axis))])  13.8 us
    ppermute x10, waiting for transfers between devices, swap(): lax.ppermute(value, axis, [(i, i ^ k) for i in range(lax.axis_size(axis))])  12.2 us
    pallas_call x1, Pallas kernels, inside_chunks(): pl.pallas_call(local_kernel, name='inside_chunks', in_specs=[VMEM_SPEC] *...  5.16 us
    pallas_call x1, Pallas kernels, block_states(): pl.pallas_call(functools.partial(states_kernel, n_seq), name='block_state...  3.92 us
    pallas_call x1, Pallas kernels, input_grad(): pl.pallas_call(input_kernel, name='input_grad', grid=(steps,), in_specs=[...  2.49 us
    pallas_call x1, Pallas kernels, add_carries(): pl.pallas_call(carry_kernel, name='add_carries', grid=(CHUNKS,), in_specs...  1.66 us
  transfers between devices with their start and end apart: 10, of which 6 were waited for; matrix products, arithmetic and copies ran while one was open for 0% of the time, Pallas kernels for 23%

profile of v3, /device:TPU:0, one launch (start us, length us, event | category | flops | bytes accessed | tf_op | source)
XLA Modules:
  0.0 42.3 jit_solution(2434849336163931337)
XLA Ops:
  0.6 0.0 copy-start.3
  0.7 3.9 %block_states.1 = (bf16[512,128]{1,0:T(8,128)(2,1)S(1)}, bf16[512,128]{1,0:T(8,128)(2,1)S(1)}, f32[4,8,512]{2,1,0:T(8,128)S(1)}, bf16[64,512]{1,0:T(8,128)(2,1)S...) custom-call(bf16[1,512,2048]{2,1,0:T(8,128)(2,1)} %tokens_ref.3, ...), custom_call_target="tpu_custom_call" | custom-call | flops 268435456 | bytes 5242880 | tf_op jit(solution)/shard_map/block_states/pallas_call | solution.py:163
  4.6 5.1 %collective-permute-start = (bf16[136,512]{1,0:T(8,128)(2,1)S(1)}, bf16[136,512]{1,0:T(8,128)(2,1)S(1)}, u32[]{:S(2)}, u32[]{:S(2)}) collective-permute-start(bf16[136,512]{1,0:T(8,128)(2,1)S(1)} %get-tuple-element.31), channel_id=1, source_target_pairs={{0,3},{1,2},{2,1},{3,0},{4,7},{5,6},{6,5},{7,4},{8,11},{9,10},{10,... | collective-permute-start | bytes 417800 | tf_op jit(solution)/shard_map/ppermute | solution.py:533
  9.7 0.0 collective-permute-start.1
  9.7 0.6 %collective-permute-start.2 = (bf16[136,512]{1,0:T(8,128)(2,1)S(1)}, bf16[136,512]{1,0:T(8,128)(2,1)S(1)}, u32[]{:S(2)}, u32[]{:S(2)}) collective-permute-start(bf16[136,512]{1,0:T(8,128)(2,1)S(1)} %get-tuple-element.33), channel_id=1, source_target_pairs={{0,1},{1,0},{2,3},{3,2},{4,5},{5,4},{6,7},{7,6},{8,9},{9,8},{10,11... | collective-permute-start | bytes 417800 | tf_op jit(solution)/shard_map/ppermute | solution.py:533
  10.4 0.0 copy-done.3
  10.4 0.0 copy-done.4
  10.4 5.2 %inside_chunks.1 = (f32[512,512]{1,0:T(8,128)S(1)}, f32[512,512]{1,0:T(8,128)S(1)}, f32[512,128]{1,0:T(8,128)S(1)}, bf16[512,2048]{1,0:T(8,128)(2,1)S(1)}) custom-call(bf16[1,512,512]{2,1,0:T(8,128)(2,1)S(1)} %copy-done.2, bf16[1,512,512]{2,1,0:T(8,128)(2,1)S(1)} %copy-done.3, bf16[512,128]{1,0:T(8,128)(2,1)S(1)} %get-tuple-element.37.bc_ref, ...), custom_call_target="tpu_custom_call" | custom-call | flops 805306368 | bytes 4194304 | tf_op jit(solution)/shard_map/inside_chunks/pallas_call | solution.py:275
  15.5 0.0 copy-start
  15.6 0.0 collective-permute-done.r3_ref
  15.6 5.9 %collective-permute-done.1.r2_ref = bf16[136,512]{1,0:T(8,128)(2,1)S(1)} collective-permute-done((bf16[136,512]{1,0:T(8,128)(2,1)S(1)}, bf16[136,512]{1,0:T(8,128)(2,1)S(1)}, u32[]{:S(2)}, u32[]{:S(2)}) %collective-permute-start.1) | collective-permute-done | bytes 139296 | tf_op jit(solution)/shard_map/ppermute | solution.py:533
  21.5 0.0 collective-permute-done.2.r1_ref
  21.5 0.8 %group_sums.1 = (bf16[512,128]{1,0:T(8,128)(2,1)S(1)}, bf16[2,128,512]{2,1,0:T(8,128)(2,1)S(1)}, bf16[2,128,512]{2,1,0:T(8,128)(2,1)S(1)}) custom-call(bf16[136,512]{1,0:T(8,128)(2,1)S(1)} %collective-permute-done.r3_ref, bf16[136,512]{1,0:T(8,128)(2,1)S(1)} %collective-permute-done.1.r2_ref, bf16[136,512]{1,0:T(8,128)(2,1)S(1)} %collective-permute-done.2.r1_ref, ...), custom_call_target="tpu_custom_call" | custom-call | flops 268435456 | bytes 3145728 | tf_op jit(solution)/shard_map/group_sums/pallas_call | solution.py:346
  22.3 2.5 %collective-permute-start.5 = (bf16[512,128]{1,0:T(8,128)(2,1)S(1)}, bf16[512,128]{1,0:T(8,128)(2,1)S(1)}, u32[]{:S(2)}, u32[]{:S(2)}) collective-permute-start(bf16[512,128]{1,0:T(8,128)(2,1)S(1)} %get-tuple-element.50.a0_ref), channel_id=1, source_target_pairs={{0,12},{4,8},{8,4},{12,0},{1,13},{5,9},{9,5},{13,1},{2,14},{6,10},... | collective-permute-start | bytes 393224 | tf_op jit(solution)/shard_map/ppermute | solution.py:533
  24.8 0.5 %collective-permute-start.4 = (bf16[512,128]{1,0:T(8,128)(2,1)S(1)}, bf16[512,128]{1,0:T(8,128)(2,1)S(1)}, u32[]{:S(2)}, u32[]{:S(2)}) collective-permute-start(bf16[512,128]{1,0:T(8,128)(2,1)S(1)} %get-tuple-element.50.a0_ref), channel_id=1, source_target_pairs={{0,8},{4,12},{8,0},{12,4},{1,9},{5,13},{9,1},{13,5},{2,10},{6,14},... | collective-permute-start | bytes 393224 | tf_op jit(solution)/shard_map/ppermute | solution.py:533
  25.3 0.5 %collective-permute-start.3 = (bf16[512,128]{1,0:T(8,128)(2,1)S(1)}, bf16[512,128]{1,0:T(8,128)(2,1)S(1)}, u32[]{:S(2)}, u32[]{:S(2)}) collective-permute-start(bf16[512,128]{1,0:T(8,128)(2,1)S(1)} %get-tuple-element.50.a0_ref), channel_id=1, source_target_pairs={{0,4},{4,0},{8,12},{12,8},{1,5},{5,1},{9,13},{13,9},{2,6},{6,2},{1... | collective-permute-start | bytes 393224 | tf_op jit(solution)/shard_map/ppermute | solution.py:533
  25.9 3.2 %collective-permute-done.5.a3_ref = bf16[512,128]{1,0:T(8,128)(2,1)S(1)} collective-permute-done((bf16[512,128]{1,0:T(8,128)(2,1)S(1)}, bf16[512,128]{1,0:T(8,128)(2,1)S(1)}, u32[]{:S(2)}, u32[]{:S(2)}) %collective-permute-start.5) | collective-permute-done | bytes 131104 | tf_op jit(solution)/shard_map/ppermute | solution.py:533
  29.1 1.5 %collective-permute-done.4.a2_ref = bf16[512,128]{1,0:T(8,128)(2,1)S(1)} collective-permute-done((bf16[512,128]{1,0:T(8,128)(2,1)S(1)}, bf16[512,128]{1,0:T(8,128)(2,1)S(1)}, u32[]{:S(2)}, u32[]{:S(2)}) %collective-permute-start.4) | collective-permute-done | bytes 131104 | tf_op jit(solution)/shard_map/ppermute | solution.py:533
  30.6 0.1 collective-permute-done.3.a1_ref
  30.7 0.4 weight_away.1
  31.1 0.1 collective-permute-start.6
  31.2 0.3 weight_home.1.keep_ref
  31.5 1.2 %collective-permute-done.6.got_ref = bf16[4,128,256]{2,1,0:T(8,128)(2,1)S(1)} collective-permute-done((bf16[4,128,256]{2,1,0:T(8,128)(2,1)S(1)}, bf16[4,128,256]{2,1,0:T(8,128)(2,1)S(1)}, u32[]{:S(2)}, u32[]{:S(2)}) %collective-permute-start.6) | collective-permute-done | bytes 262176 | tf_op jit(solution)/shard_map/ppermute | solution.py:533
  32.8 2.4 %collective-permute-start.7 = (bf16[128,256]{1,0:T(8,128)(2,1)S(1)}, bf16[128,256]{1,0:T(8,128)(2,1)S(1)}, u32[]{:S(2)}, u32[]{:S(2)}) collective-permute-start(bf16[128,256]{1,0:T(8,128)(2,1)S(1)} %get-tuple-element.55), channel_id=1, source_target_pairs={{0,3},{1,2},{2,1},{3,0},{4,7},{5,6},{6,5},{7,4},{8,11},{9,10},{10,... | collective-permute-start | bytes 196616 | tf_op jit(solution)/shard_map/ppermute | solution.py:533
  35.1 0.0 collective-permute-start.8
  35.1 2.1 %collective-permute-start.9 = (bf16[128,256]{1,0:T(8,128)(2,1)S(1)}, bf16[128,256]{1,0:T(8,128)(2,1)S(1)}, u32[]{:S(2)}, u32[]{:S(2)}) collective-permute-start(bf16[128,256]{1,0:T(8,128)(2,1)S(1)} %get-tuple-element.57), channel_id=1, source_target_pairs={{0,1},{1,0},{2,3},{3,2},{4,5},{5,4},{6,7},{7,6},{8,9},{9,8},{10,11... | collective-permute-start | bytes 196616 | tf_op jit(solution)/shard_map/ppermute | solution.py:533
  37.2 1.7 %add_carries.1 = (bf16[1,512,512]{2,1,0:T(8,128)(2,1)}, bf16[1,512,512]{2,1,0:T(8,128)(2,1)}) custom-call(bf16[2,128,512]{2,1,0:T(8,128)(2,1)S(1)} %get-tuple-element.43.before_ref, bf16[2,128,512]{2,1,0:T(8,128)(2,1)S(1)} %get-tuple-element.44.after_ref, bf16[512,2048]{1,0:T(8,128)(2,1)S(1)} %get-tuple-element.45.queries_ref, ...), custom_call_target="tpu_custom_call" | custom-call | flops 268435456 | bytes 5242880 | tf_op jit(solution)/shard_map/add_carries/pallas_call | solution.py:388
  38.9 2.5 %input_grad.1 = bf16[1,512,2048]{2,1,0:T(8,128)(2,1)} custom-call(bf16[512,128]{1,0:T(8,128)(2,1)S(1)} %get-tuple-element.51.grad_ref, bf16[2048,128]{1,0:T(8,128)(2,1)S(1)} %copy-done.1), custom_call_target="tpu_custom_call" | custom-call | flops 268435456 | bytes 3145728 | tf_op jit(solution)/shard_map/input_grad/pallas_call | solution.py:520
  41.4 0.0 collective-permute-done.7.r3_ref
  41.4 0.2 collective-permute-done.8.r2_ref
  41.6 0.0 collective-permute-done.9.r1_ref
  41.6 0.8 %final_sum.1 = f32[256,128]{1,0:T(8,128)} custom-call(f32[128,256]{1,0:T(8,128)S(1)} %get-tuple-element.54.own_ref, bf16[128,256]{1,0:T(8,128)(2,1)S(1)} %collective-permute-done.7.r3_ref, bf16[128,256]{1,0:T(8,128)(2,1)S(1)} %collective-permute-done.8.r2_ref, bf16[128,256]{1,0:T(8,128)(2,1)S(1)} %collective-permute-done.9.r1_ref), custom_call_target="tpu_custom_call" | custom-call | tf_op jit(solution)/shard_map/final_sum/pallas_call | solution.py:501
  (7 shorter events, 0.1 us)
Async XLA Ops:
  0.6 9.7 %copy-start.3 = (bf16[1,512,512]{2,1,0:T(8,128)(2,1)S(1)}, bf16[1,512,512]{2,1,0:T(8,128)(2,1)}, u32[]{:S(2)}) copy-start(bf16[1,512,512]{2,1,0:T(8,128)(2,1)} %g_ref.1) | copy-start | bytes 1572868
  0.6 9.7 %copy-start.2 = (bf16[1,512,512]{2,1,0:T(8,128)(2,1)S(1)}, bf16[1,512,512]{2,1,0:T(8,128)(2,1)}, u32[]{:S(2)}) copy-start(bf16[1,512,512]{2,1,0:T(8,128)(2,1)} %x_ref.1) | copy-start | bytes 1572868
  0.7 9.7 %copy-start.4 = (f32[8]{0:T(128)S(1)}, f32[8]{0:T(128)}, u32[]{:S(2)}) copy-start(f32[8]{0:T(128)} %skip_ref.1) | copy-start | bytes 100
  4.6 11.0 %collective-permute-start = (bf16[136,512]{1,0:T(8,128)(2,1)S(1)}, bf16[136,512]{1,0:T(8,128)(2,1)S(1)}, u32[]{:S(2)}, u32[]{:S(2)}) collective-permute-start(bf16[136,512]{1,0:T(8,128)(2,1)S(1)} %get-tuple-element.31), channel_id=1, source_target_pairs={{0,3},{1,2},{2,1},{3,0},{4,7},{5,6},{6,5},{7,4},{8,11},{9,10},{10,... | collective-permute-start | bytes 417800 | tf_op jit(solution)/shard_map/ppermute | solution.py:533
  9.7 11.8 %collective-permute-start.1 = (bf16[136,512]{1,0:T(8,128)(2,1)S(1)}, bf16[136,512]{1,0:T(8,128)(2,1)S(1)}, u32[]{:S(2)}, u32[]{:S(2)}) collective-permute-start(bf16[136,512]{1,0:T(8,128)(2,1)S(1)} %get-tuple-element.32), channel_id=1, source_target_pairs={{0,2},{1,3},{2,0},{3,1},{4,6},{5,7},{6,4},{7,5},{8,10},{9,11},{10,... | collective-permute-start | bytes 417800 | tf_op jit(solution)/shard_map/ppermute | solution.py:533
  9.7 11.8 %collective-permute-start.2 = (bf16[136,512]{1,0:T(8,128)(2,1)S(1)}, bf16[136,512]{1,0:T(8,128)(2,1)S(1)}, u32[]{:S(2)}, u32[]{:S(2)}) collective-permute-start(bf16[136,512]{1,0:T(8,128)(2,1)S(1)} %get-tuple-element.33), channel_id=1, source_target_pairs={{0,1},{1,0},{2,3},{3,2},{4,5},{5,4},{6,7},{7,6},{8,9},{9,8},{10,11... | collective-permute-start | bytes 417800 | tf_op jit(solution)/shard_map/ppermute | solution.py:533
  15.5 15.2 %copy-start = (bf16[1,512,2048]{2,1,0:T(8,128)(2,1)S(1)}, bf16[1,512,2048]{2,1,0:T(8,128)(2,1)}, u32[]{:S(2)}) copy-start(bf16[1,512,2048]{2,1,0:T(8,128)(2,1)} %tokens_ref.3) | copy-start | bytes 6291460
  22.3 6.8 %collective-permute-start.5 = (bf16[512,128]{1,0:T(8,128)(2,1)S(1)}, bf16[512,128]{1,0:T(8,128)(2,1)S(1)}, u32[]{:S(2)}, u32[]{:S(2)}) collective-permute-start(bf16[512,128]{1,0:T(8,128)(2,1)S(1)} %get-tuple-element.50.a0_ref), channel_id=1, source_target_pairs={{0,12},{4,8},{8,4},{12,0},{1,13},{5,9},{9,5},{13,1},{2,14},{6,10},... | collective-permute-start | bytes 393224 | tf_op jit(solution)/shard_map/ppermute | solution.py:533
  24.8 5.8 %collective-permute-start.4 = (bf16[512,128]{1,0:T(8,128)(2,1)S(1)}, bf16[512,128]{1,0:T(8,128)(2,1)S(1)}, u32[]{:S(2)}, u32[]{:S(2)}) collective-permute-start(bf16[512,128]{1,0:T(8,128)(2,1)S(1)} %get-tuple-element.50.a0_ref), channel_id=1, source_target_pairs={{0,8},{4,12},{8,0},{12,4},{1,9},{5,13},{9,1},{13,5},{2,10},{6,14},... | collective-permute-start | bytes 393224 | tf_op jit(solution)/shard_map/ppermute | solution.py:533
  25.3 5.4 %collective-permute-start.3 = (bf16[512,128]{1,0:T(8,128)(2,1)S(1)}, bf16[512,128]{1,0:T(8,128)(2,1)S(1)}, u32[]{:S(2)}, u32[]{:S(2)}) collective-permute-start(bf16[512,128]{1,0:T(8,128)(2,1)S(1)} %get-tuple-element.50.a0_ref), channel_id=1, source_target_pairs={{0,4},{4,0},{8,12},{12,8},{1,5},{5,1},{9,13},{13,9},{2,6},{6,2},{1... | collective-permute-start | bytes 393224 | tf_op jit(solution)/shard_map/ppermute | solution.py:533
  31.1 1.6 %collective-permute-start.6 = (bf16[4,128,256]{2,1,0:T(8,128)(2,1)S(1)}, bf16[4,128,256]{2,1,0:T(8,128)(2,1)S(1)}, u32[]{:S(2)}, u32[]{:S(2)}) collective-permute-start(bf16[4,128,256]{2,1,0:T(8,128)(2,1)S(1)} %get-tuple-element.53), channel_id=1, source_target_pairs={{0,16},{16,0},{1,17},{17,1},{2,18},{18,2},{3,19},{19,3},{4,20},{20... | collective-permute-start | bytes 786440 | tf_op jit(solution)/shard_map/ppermute | solution.py:533
  32.8 8.6 %collective-permute-start.7 = (bf16[128,256]{1,0:T(8,128)(2,1)S(1)}, bf16[128,256]{1,0:T(8,128)(2,1)S(1)}, u32[]{:S(2)}, u32[]{:S(2)}) collective-permute-start(bf16[128,256]{1,0:T(8,128)(2,1)S(1)} %get-tuple-element.55), channel_id=1, source_target_pairs={{0,3},{1,2},{2,1},{3,0},{4,7},{5,6},{6,5},{7,4},{8,11},{9,10},{10,... | collective-permute-start | bytes 196616 | tf_op jit(solution)/shard_map/ppermute | solution.py:533
  35.1 6.4 %collective-permute-start.8 = (bf16[128,256]{1,0:T(8,128)(2,1)S(1)}, bf16[128,256]{1,0:T(8,128)(2,1)S(1)}, u32[]{:S(2)}, u32[]{:S(2)}) collective-permute-start(bf16[128,256]{1,0:T(8,128)(2,1)S(1)} %get-tuple-element.56), channel_id=1, source_target_pairs={{0,2},{1,3},{2,0},{3,1},{4,6},{5,7},{6,4},{7,5},{8,10},{9,11},{10,... | collective-permute-start | bytes 196616 | tf_op jit(solution)/shard_map/ppermute | solution.py:533
  35.1 6.4 %collective-permute-start.9 = (bf16[128,256]{1,0:T(8,128)(2,1)S(1)}, bf16[128,256]{1,0:T(8,128)(2,1)S(1)}, u32[]{:S(2)}, u32[]{:S(2)}) collective-permute-start(bf16[128,256]{1,0:T(8,128)(2,1)S(1)} %get-tuple-element.57), channel_id=1, source_target_pairs={{0,1},{1,0},{2,3},{3,2},{4,5},{5,4},{6,7},{7,6},{8,9},{9,8},{10,11... | collective-permute-start | bytes 196616 | tf_op jit(solution)/shard_map/ppermute | solution.py:533
  37.2 1.7 %copy-start.1 = (bf16[2048,128]{1,0:T(8,128)(2,1)S(1)}, bf16[2048,128]{1,0:T(8,128)(2,1)}, u32[]{:S(2)}) copy-start(bf16[2048,128]{1,0:T(8,128)(2,1)} %w_ref.1) | copy-start | bytes 1572868

commit v4 on v3

--- a/solution.py
+++ b/solution.py
@@ -11,7 +11,10 @@
 BF16 = jnp.bfloat16
 VMEM_SPEC = pl.BlockSpec(memory_space=pltpu.VMEM)
 SMEM_SPEC = pl.BlockSpec(memory_space=pltpu.SMEM)
-EXTRA = 8
+LANES = 128
+ORDER_A = (3, 2, 1)
+ORDER_B = (3, 2, 1)
+ORDER_C = (3, 2, 1)
 
 
 def mm(a, b):
@@ -38,6 +41,24 @@
     kind_ok = (row >> log2(2 * heads)) == (col >> log2(width))
     head_ok = (row & (heads - 1)) == ((col & (width - 1)) >> log2(width // heads))
     return jnp.where(kind_ok & head_ok, 1.0, 0.0).astype(BF16)
+
+
+def pack(ref, state, decay):
+    rows, width = state.shape
+    blocks = width // LANES
+    high = decay.astype(BF16).astype(F32)
+    for p in range(blocks):
+        ref[p * rows : (p + 1) * rows] = state[:, p * LANES : (p + 1) * LANES].astype(BF16)
+    parts = [v[:, p * LANES : (p + 1) * LANES] for v in (high, decay - high) for p in range(blocks)]
+    ref[blocks * rows :] = jnp.concatenate(parts, axis=0).astype(BF16)
+
+
+def unpack(payload, rows):
+    blocks = payload.shape[0] // (rows + 2)
+    state = jnp.concatenate([payload[p * rows : (p + 1) * rows] for p in range(blocks)], axis=1).astype(F32)
+    tail = payload[blocks * rows :].astype(F32)
+    decay = jnp.concatenate([tail[p : p + 1] + tail[blocks + p : blocks + p + 1] for p in range(blocks)], axis=1)
+    return state, decay
 
 
 def states_kernel(
@@ -105,10 +126,6 @@
     second_decay = to_lanes(jnp.exp(final - middle))
     row8 = lax.broadcasted_iota(jnp.int32, (8, width), 0)
     coef_ref[...] = jnp.where(row8 == 0, first_decay, jnp.where(row8 == 1, second_decay, 0.0))
-    high = decay.astype(BF16).astype(F32)
-    row_e = lax.broadcasted_iota(jnp.int32, (EXTRA, width), 0)
-    last = jnp.where(row_e == 0, high, jnp.where(row_e == 1, decay - high, 0.0)).astype(BF16)
-
     copies[3].wait()
     copies[4].wait()
     for q in range(CHUNKS):
@@ -134,24 +151,24 @@
 
     near_ref[0] = onward[0]
     near_ref[1] = backward[1]
-    next_total = (onward[0] * second_decay + onward[1]).astype(BF16)
-    prior_total = (backward[0] + first_decay * backward[1]).astype(BF16)
-    rows = next_total.shape[0]
-    for k, ref in ((1, pay1_ref), (2, pay2_ref), (3, pay3_ref)):
-        ref[rows:] = last
-        if n_seq == 4:
-            here = lax.axis_index("seq")
+    next_total = onward[0] * second_decay + onward[1]
+    prior_total = backward[0] + first_decay * backward[1]
+    if n_seq == 4:
+        here = lax.axis_index("seq")
+        for k, ref in ((1, pay1_ref), (2, pay2_ref), (3, pay3_ref)):
             up = (here ^ k) > here
 
             @pl.when(up)
             def _():
-                ref[:rows] = next_total
+                pack(ref, next_total, decay)
 
             @pl.when(jnp.logical_not(up))
             def _():
-                ref[:rows] = prior_total
-        else:
-            ref[:rows] = next_total if k == 1 else prior_total
+                pack(ref, prior_total, decay)
+    else:
+        pack(pay1_ref, next_total, decay)
+        pack(pay2_ref, prior_total, decay)
+        pack(pay3_ref, prior_total, decay)
 
 
 def block_states(n_seq, tokens, x, g, dt, w, rate, bias):
@@ -159,7 +176,7 @@
     width = x.shape[2]
     heads = dt.shape[1]
     two_n = w.shape[1]
-    pay = jax.ShapeDtypeStruct((two_n + EXTRA, width), BF16)
+    pay = jax.ShapeDtypeStruct((width // LANES * (two_n + 2), LANES), BF16)
     return pl.pallas_call(
         functools.partial(states_kernel, n_seq),
         name="block_states",
@@ -297,10 +314,10 @@
 
 def combine_received(direct, refs, two_n):
     if not direct:
-        return refs[0][:two_n].astype(F32), refs[1][:two_n].astype(F32)
+        return refs[0][...], refs[1][...]
     here = lax.axis_index("seq")
-    width = refs[0].shape[1]
-    decays = [r[two_n : two_n + 1].astype(F32) + r[two_n + 1 : two_n + 2].astype(F32) for r in refs]
+    states, decays = zip(*[unpack(r[...], two_n) for r in refs])
+    width = states[0].shape[1]
     before = jnp.zeros((two_n, width), F32)
     after = jnp.zeros((two_n, width), F32)
     for k in (1, 2, 3):
@@ -312,20 +329,22 @@
                 mid = here ^ m
                 inside = jnp.logical_and(mid > low, mid < high)
                 factor = factor * jnp.where(inside, decays[m - 1], 1.0)
-        part = refs[k - 1][:two_n].astype(F32)
+        part = states[k - 1]
         earlier = there < here
         before = before + part * jnp.where(earlier, factor, 0.0)
         after = after + part * jnp.where(earlier, 0.0, factor)
     return before, after
 
 
-def group_kernel(
-    direct, r3_ref, r2_ref, r1_ref, near_ref, coef_ref, scaled_ref, gbc_ref, group_ref, before_ref, after_ref
-):
+def group_kernel(direct, count, *refs):
+    received = refs[:count]
+    near_ref, coef_ref, scaled_ref, gbc_ref, group_ref, before_ref, after_ref = refs[count:]
+    if direct:
+        received = [received[ORDER_A.index(k)] for k in (1, 2, 3)]
     length, two_n = group_ref.shape
     width = coef_ref.shape[1]
     chunk = length // CHUNKS
-    before, after = combine_received(direct, (r1_ref, r2_ref, r3_ref), two_n)
+    before, after = combine_received(direct, received, two_n)
     befores = [before.astype(BF16), (near_ref[0] + coef_ref[0:1] * before).astype(BF16)]
     afters = [(near_ref[1] + coef_ref[1:2] * after).astype(BF16), after.astype(BF16)]
     left = lax.broadcasted_iota(jnp.int32, (1, two_n), 1) < two_n // 2
@@ -339,19 +358,19 @@
         group_ref[at] = (gbc_ref[at] + jnp.where(left, from_x, from_g)).astype(BF16)
 
 
-def group_sums(direct, r3, r2, r1, near, coef, scaled, gbc):
+def group_sums(direct, received, near, coef, scaled, gbc):
     length, two_n = gbc.shape
     width = coef.shape[1]
     state = jax.ShapeDtypeStruct((CHUNKS, two_n, width), BF16)
     return pl.pallas_call(
-        functools.partial(group_kernel, direct),
+        functools.partial(group_kernel, direct, len(received)),
         name="group_sums",
-        in_specs=[VMEM_SPEC] * 7,
+        in_specs=[VMEM_SPEC] * (4 + len(received)),
         out_specs=[VMEM_SPEC] * 3,
         out_shape=[jax.ShapeDtypeStruct((length, two_n), BF16), state, state],
         compiler_params=LIMIT,
         cost_estimate=pl.CostEstimate(flops=8 * length * two_n * width, bytes_accessed=3 << 20, transcendentals=0),
-    )(r3, r2, r1, near, coef, scaled, gbc)
+    )(*received, near, coef, scaled, gbc)
 
 
 def carry_kernel(before_ref, after_ref, queries_ref, y_ref, gv_ref, yo_ref, gvo_ref):
@@ -405,14 +424,13 @@
 
         def step(k, before):
             at = size - 1 - k if reverse else k
-            one = every[at].astype(F32)
-            new = before * (one[two_n : two_n + 1] + one[two_n + 1 : two_n + 2]) + one[:two_n]
+            state, decay = unpack(every[at], two_n)
+            new = before * decay + state
             return jnp.where(at > here if reverse else at < here, new, before)
 
-        return lax.fori_loop(0, size, step, jnp.zeros((two_n, payload.shape[1]), F32))
-
-    pad = lambda v: jnp.pad(v.astype(BF16), ((0, EXTRA), (0, 0)))
-    return pad(total(onward, False)), pad(total(backward, True))
+        return lax.fori_loop(0, size, step, jnp.zeros((two_n, LANES * (payload.shape[0] // (two_n + 2))), F32))
+
+    return total(onward, False), total(backward, True)
 
 
 def away_kernel(a0_ref, a1_ref, a2_ref, a3_ref, tokens_ref, grad_ref, grad_t_ref, send_ref):
@@ -542,24 +560,25 @@
     )
     direct = n_seq == 4
     if direct:
-        r3, r2, r1 = swap(pay3, "seq", 3), swap(pay2, "seq", 2), swap(pay1, "seq", 1)
+        received = [swap((pay1, pay2, pay3)[k - 1], "seq", k) for k in ORDER_A]
     else:
-        r1, r2 = scanned_generic(pay1, pay2, two_n)
-        r3 = r2
+        received = scanned_generic(pay1, pay2, two_n)
     y_local, gv_local, gbc_local, queries = inside_chunks(
         head_values, grad_y, bc, cb, rows, decs, spread, skip_gain
     )
-    group, before, after = group_sums(direct, r3, r2, r1, near, coef, scaled, gbc_local)
+    group, before, after = group_sums(direct, received, near, coef, scaled, gbc_local)
     total_tokens = n_dp * n_seq * length
     if direct and n_dp == 2 and n_head == 4:
-        groups = [group] + [swap(group, "head", k) for k in (1, 2, 3)]
+        others = [swap(group, "head", k) for k in ORDER_B[::-1]]
         y_out, grad_values = add_carries(before, after, queries, y_local, gv_local)
+        *others, y_out = lax.optimization_barrier((*others, y_out))
+        groups = [group, *others]
         grad_bc, grad_t, send = weight_away(n_seq, groups, layer_input)
         got = swap(send, "dp", 1)
         keep = weight_home(n_seq, grad_t, layer_input)
         own, s1, s2, s3 = pair_sum(keep, got)
-        t3, t2, t1 = swap(s3, "seq", 3), swap(s2, "seq", 2), swap(s1, "seq", 1)
-        grad_w_bc = final_sum(1.0 / total_tokens, own, t3, t2, t1)
+        sums = [swap((s1, s2, s3)[k - 1], "seq", k) for k in ORDER_C]
+        grad_w_bc = final_sum(1.0 / total_tokens, own, *sums)
     else:
         y_out, grad_values = add_carries(before, after, queries, y_local, gv_local)
         grad_bc = lax.psum(group.astype(F32), "head").astype(BF16)

time: 42.5 us -> 41.9 us (0.986)
  waiting for transfers between devices: 12.2 us -> 11.6 us
    ppermute x10, waiting for transfers between devices: 12.2 us -> 11.6 us  [swap(): lax.ppermute(value, axis, [(i, i ^ k) for i in range(lax.axis_size(axis))])]
where the time goes in v4:
time: 41.9 us; the launch traced here: 41.8 us
  Pallas kernels  15.6 us (37%)
  starting transfers between devices  13.8 us (33%)
  waiting for transfers between devices  11.6 us (28%)
  between operations  0.73 us (2%)
    ppermute x10, starting transfers between devices, swap(): lax.ppermute(value, axis, [(i, i ^ k) for i in range(lax.axis_size(axis))])  13.8 us
    ppermute x10, waiting for transfers between devices, swap(): lax.ppermute(value, axis, [(i, i ^ k) for i in range(lax.axis_size(axis))])  11.6 us
    pallas_call x1, Pallas kernels, inside_chunks(): pl.pallas_call(local_kernel, name='inside_chunks', in_specs=[VMEM_SPEC] *...  5.17 us
    pallas_call x1, Pallas kernels, block_states(): pl.pallas_call(functools.partial(states_kernel, n_seq), name='block_state...  3.94 us
    pallas_call x1, Pallas kernels, input_grad(): pl.pallas_call(input_kernel, name='input_grad', grid=(steps,), in_specs=[...  2.49 us
    pallas_call x1, Pallas kernels, add_carries(): pl.pallas_call(carry_kernel, name='add_carries', grid=(CHUNKS,), in_specs...  1.68 us
  transfers between devices with their start and end apart: 10, of which 6 were waited for; matrix products, arithmetic and copies ran while one was open for 0% of the time, Pallas kernels for 23%

profile of v4, /device:TPU:0, one launch (start us, length us, event | category | flops | bytes accessed | tf_op | source)
XLA Modules:
  0.0 41.8 jit_solution(12732944694235198090)
XLA Ops:
  0.6 0.0 copy-start.3
  0.6 0.0 copy-start.2
  0.7 3.9 %block_states.1 = (bf16[512,128]{1,0:T(8,128)(2,1)S(1)}, bf16[512,128]{1,0:T(8,128)(2,1)S(1)}, f32[4,8,512]{2,1,0:T(8,128)S(1)}, bf16[64,512]{1,0:T(8,128)(2,1)S...) custom-call(bf16[1,512,2048]{2,1,0:T(8,128)(2,1)} %tokens_ref.3, ...), custom_call_target="tpu_custom_call" | custom-call | flops 268435456 | bytes 5242880 | tf_op jit(solution)/shard_map/block_states/pallas_call | solution.py:180
  4.6 5.1 %collective-permute-start = (bf16[520,128]{1,0:T(8,128)(2,1)S(1)}, bf16[520,128]{1,0:T(8,128)(2,1)S(1)}, u32[]{:S(2)}, u32[]{:S(2)}) collective-permute-start(bf16[520,128]{1,0:T(8,128)(2,1)S(1)} %get-tuple-element.35), channel_id=1, source_target_pairs={{0,3},{1,2},{2,1},{3,0},{4,7},{5,6},{6,5},{7,4},{8,11},{9,10},{10,... | collective-permute-start | bytes 399368 | tf_op jit(solution)/shard_map/ppermute | solution.py:551
  9.7 0.0 collective-permute-start.1
  9.7 0.6 %collective-permute-start.2 = (bf16[520,128]{1,0:T(8,128)(2,1)S(1)}, bf16[520,128]{1,0:T(8,128)(2,1)S(1)}, u32[]{:S(2)}, u32[]{:S(2)}) collective-permute-start(bf16[520,128]{1,0:T(8,128)(2,1)S(1)} %get-tuple-element.37), channel_id=1, source_target_pairs={{0,1},{1,0},{2,3},{3,2},{4,5},{5,4},{6,7},{7,6},{8,9},{9,8},{10,11... | collective-permute-start | bytes 399368 | tf_op jit(solution)/shard_map/ppermute | solution.py:551
  10.4 0.0 copy-done.3
  10.4 5.2 %inside_chunks.1 = (f32[512,512]{1,0:T(8,128)S(1)}, f32[512,512]{1,0:T(8,128)S(1)}, f32[512,128]{1,0:T(8,128)S(1)}, bf16[512,2048]{1,0:T(8,128)(2,1)S(1)}) custom-call(bf16[1,512,512]{2,1,0:T(8,128)(2,1)S(1)} %copy-done.2, bf16[1,512,512]{2,1,0:T(8,128)(2,1)S(1)} %copy-done.3, bf16[512,128]{1,0:T(8,128)(2,1)S(1)} %get-tuple-element.41.bc_ref, ...), custom_call_target="tpu_custom_call" | custom-call | flops 805306368 | bytes 4194304 | tf_op jit(solution)/shard_map/inside_chunks/pallas_call | solution.py:292
  15.6 0.0 collective-permute-done.refs_0_
  15.6 5.4 %collective-permute-done.1.refs_1_ = bf16[520,128]{1,0:T(8,128)(2,1)S(1)} collective-permute-done((bf16[520,128]{1,0:T(8,128)(2,1)S(1)}, bf16[520,128]{1,0:T(8,128)(2,1)S(1)}, u32[]{:S(2)}, u32[]{:S(2)}) %collective-permute-start.1) | collective-permute-done | bytes 133152 | tf_op jit(solution)/shard_map/ppermute | solution.py:551
  21.0 0.0 collective-permute-done.2.refs_2_
  21.0 0.8 %group_sums.1 = (bf16[512,128]{1,0:T(8,128)(2,1)S(1)}, bf16[2,128,512]{2,1,0:T(8,128)(2,1)S(1)}, bf16[2,128,512]{2,1,0:T(8,128)(2,1)S(1)}) custom-call(bf16[520,128]{1,0:T(8,128)(2,1)S(1)} %collective-permute-done.refs_0_, bf16[520,128]{1,0:T(8,128)(2,1)S(1)} %collective-permute-done.1.refs_1_, bf16[520,128]{1,0:T(8,128)(2,1)S(1)} %collective-permute-done.2.refs_2_, ...), custom_call_target="tpu_custom_call" | custom-call | flops 268435456 | bytes 3145728 | tf_op jit(solution)/shard_map/group_sums/pallas_call | solution.py:365
  21.8 2.5 %collective-permute-start.5 = (bf16[512,128]{1,0:T(8,128)(2,1)S(1)}, bf16[512,128]{1,0:T(8,128)(2,1)S(1)}, u32[]{:S(2)}, u32[]{:S(2)}) collective-permute-start(bf16[512,128]{1,0:T(8,128)(2,1)S(1)} %get-tuple-element.47.a0_ref), channel_id=1, source_target_pairs={{0,12},{4,8},{8,4},{12,0},{1,13},{5,9},{9,5},{13,1},{2,14},{6,10},... | collective-permute-start | bytes 393224 | tf_op jit(solution)/shard_map/ppermute | solution.py:551
  24.3 0.5 %collective-permute-start.4 = (bf16[512,128]{1,0:T(8,128)(2,1)S(1)}, bf16[512,128]{1,0:T(8,128)(2,1)S(1)}, u32[]{:S(2)}, u32[]{:S(2)}) collective-permute-start(bf16[512,128]{1,0:T(8,128)(2,1)S(1)} %get-tuple-element.47.a0_ref), channel_id=1, source_target_pairs={{0,8},{4,12},{8,0},{12,4},{1,9},{5,13},{9,1},{13,5},{2,10},{6,14},... | collective-permute-start | bytes 393224 | tf_op jit(solution)/shard_map/ppermute | solution.py:551
  24.8 0.5 %collective-permute-start.3 = (bf16[512,128]{1,0:T(8,128)(2,1)S(1)}, bf16[512,128]{1,0:T(8,128)(2,1)S(1)}, u32[]{:S(2)}, u32[]{:S(2)}) collective-permute-start(bf16[512,128]{1,0:T(8,128)(2,1)S(1)} %get-tuple-element.47.a0_ref), channel_id=1, source_target_pairs={{0,4},{4,0},{8,12},{12,8},{1,5},{5,1},{9,13},{13,9},{2,6},{6,2},{1... | collective-permute-start | bytes 393224 | tf_op jit(solution)/shard_map/ppermute | solution.py:551
  25.3 1.7 %add_carries.1 = (bf16[1,512,512]{2,1,0:T(8,128)(2,1)}, bf16[1,512,512]{2,1,0:T(8,128)(2,1)}) custom-call(bf16[2,128,512]{2,1,0:T(8,128)(2,1)S(1)} %get-tuple-element.48.before_ref, bf16[2,128,512]{2,1,0:T(8,128)(2,1)S(1)} %get-tuple-element.49.after_ref, bf16[512,2048]{1,0:T(8,128)(2,1)S(1)} %get-tuple-element.50.queries_ref, ...), custom_call_target="tpu_custom_call" | custom-call | flops 268435456 | bytes 5242880 | tf_op jit(solution)/shard_map/add_carries/pallas_call | solution.py:407
  27.0 1.5 %collective-permute-done.5.a3_ref = bf16[512,128]{1,0:T(8,128)(2,1)S(1)} collective-permute-done((bf16[512,128]{1,0:T(8,128)(2,1)S(1)}, bf16[512,128]{1,0:T(8,128)(2,1)S(1)}, u32[]{:S(2)}, u32[]{:S(2)}) %collective-permute-start.5) | collective-permute-done | bytes 131104 | tf_op jit(solution)/shard_map/ppermute | solution.py:551
  28.5 1.5 %collective-permute-done.4.a2_ref = bf16[512,128]{1,0:T(8,128)(2,1)S(1)} collective-permute-done((bf16[512,128]{1,0:T(8,128)(2,1)S(1)}, bf16[512,128]{1,0:T(8,128)(2,1)S(1)}, u32[]{:S(2)}, u32[]{:S(2)}) %collective-permute-start.4) | collective-permute-done | bytes 131104 | tf_op jit(solution)/shard_map/ppermute | solution.py:551
  30.1 0.1 collective-permute-done.3.a1_ref
  30.2 0.4 weight_away.1
  30.6 0.0 copy-start.1
  30.6 0.1 collective-permute-start.6
  30.6 0.3 weight_home.1.keep_ref
  31.0 1.2 %collective-permute-done.6.got_ref = bf16[4,128,256]{2,1,0:T(8,128)(2,1)S(1)} collective-permute-done((bf16[4,128,256]{2,1,0:T(8,128)(2,1)S(1)}, bf16[4,128,256]{2,1,0:T(8,128)(2,1)S(1)}, u32[]{:S(2)}, u32[]{:S(2)}) %collective-permute-start.6) | collective-permute-done | bytes 262176 | tf_op jit(solution)/shard_map/ppermute | solution.py:551
  32.2 2.4 %collective-permute-start.7 = (bf16[128,256]{1,0:T(8,128)(2,1)S(1)}, bf16[128,256]{1,0:T(8,128)(2,1)S(1)}, u32[]{:S(2)}, u32[]{:S(2)}) collective-permute-start(bf16[128,256]{1,0:T(8,128)(2,1)S(1)} %get-tuple-element.63), channel_id=1, source_target_pairs={{0,3},{1,2},{2,1},{3,0},{4,7},{5,6},{6,5},{7,4},{8,11},{9,10},{10,... | collective-permute-start | bytes 196616 | tf_op jit(solution)/shard_map/ppermute | solution.py:551
  34.6 0.0 collective-permute-start.8
  34.6 2.1 %collective-permute-start.9 = (bf16[128,256]{1,0:T(8,128)(2,1)S(1)}, bf16[128,256]{1,0:T(8,128)(2,1)S(1)}, u32[]{:S(2)}, u32[]{:S(2)}) collective-permute-start(bf16[128,256]{1,0:T(8,128)(2,1)S(1)} %get-tuple-element.65), channel_id=1, source_target_pairs={{0,1},{1,0},{2,3},{3,2},{4,5},{5,4},{6,7},{7,6},{8,9},{9,8},{10,11... | collective-permute-start | bytes 196616 | tf_op jit(solution)/shard_map/ppermute | solution.py:551
  36.7 2.5 %input_grad.1 = bf16[1,512,2048]{2,1,0:T(8,128)(2,1)} custom-call(bf16[512,128]{1,0:T(8,128)(2,1)S(1)} %get-tuple-element.59.grad_ref, bf16[2048,128]{1,0:T(8,128)(2,1)S(1)} %copy-done.1), custom_call_target="tpu_custom_call" | custom-call | flops 268435456 | bytes 3145728 | tf_op jit(solution)/shard_map/input_grad/pallas_call | solution.py:538
  39.2 0.0 collective-permute-done.7.r3_ref
  39.2 1.9 %collective-permute-done.8.r2_ref = bf16[128,256]{1,0:T(8,128)(2,1)S(1)} collective-permute-done((bf16[128,256]{1,0:T(8,128)(2,1)S(1)}, bf16[128,256]{1,0:T(8,128)(2,1)S(1)}, u32[]{:S(2)}, u32[]{:S(2)}) %collective-permute-start.8) | collective-permute-done | bytes 65568 | tf_op jit(solution)/shard_map/ppermute | solution.py:551
  41.0 0.0 collective-permute-done.9.r1_ref
  41.0 0.8 %final_sum.1 = f32[256,128]{1,0:T(8,128)} custom-call(f32[128,256]{1,0:T(8,128)S(1)} %get-tuple-element.62.own_ref, bf16[128,256]{1,0:T(8,128)(2,1)S(1)} %collective-permute-done.7.r3_ref, bf16[128,256]{1,0:T(8,128)(2,1)S(1)} %collective-permute-done.8.r2_ref, bf16[128,256]{1,0:T(8,128)(2,1)S(1)} %collective-permute-done.9.r1_ref), custom_call_target="tpu_custom_call" | custom-call | tf_op jit(solution)/shard_map/final_sum/pallas_call | solution.py:519
  (7 shorter events, 0.1 us)
Async XLA Ops:
  0.6 9.7 %copy-start.3 = (bf16[1,512,512]{2,1,0:T(8,128)(2,1)S(1)}, bf16[1,512,512]{2,1,0:T(8,128)(2,1)}, u32[]{:S(2)}) copy-start(bf16[1,512,512]{2,1,0:T(8,128)(2,1)} %g_ref.1) | copy-start | bytes 1572868
  0.6 9.7 %copy-start.2 = (bf16[1,512,512]{2,1,0:T(8,128)(2,1)S(1)}, bf16[1,512,512]{2,1,0:T(8,128)(2,1)}, u32[]{:S(2)}) copy-start(bf16[1,512,512]{2,1,0:T(8,128)(2,1)} %x_ref.1) | copy-start | bytes 1572868
  0.7 9.7 %copy-start.4 = (f32[8]{0:T(128)S(1)}, f32[8]{0:T(128)}, u32[]{:S(2)}) copy-start(f32[8]{0:T(128)} %skip_ref.1) | copy-start | bytes 100
  4.6 11.0 %collective-permute-start = (bf16[520,128]{1,0:T(8,128)(2,1)S(1)}, bf16[520,128]{1,0:T(8,128)(2,1)S(1)}, u32[]{:S(2)}, u32[]{:S(2)}) collective-permute-start(bf16[520,128]{1,0:T(8,128)(2,1)S(1)} %get-tuple-element.35), channel_id=1, source_target_pairs={{0,3},{1,2},{2,1},{3,0},{4,7},{5,6},{6,5},{7,4},{8,11},{9,10},{10,... | collective-permute-start | bytes 399368 | tf_op jit(solution)/shard_map/ppermute | solution.py:551
  9.7 11.2 %collective-permute-start.1 = (bf16[520,128]{1,0:T(8,128)(2,1)S(1)}, bf16[520,128]{1,0:T(8,128)(2,1)S(1)}, u32[]{:S(2)}, u32[]{:S(2)}) collective-permute-start(bf16[520,128]{1,0:T(8,128)(2,1)S(1)} %get-tuple-element.36), channel_id=1, source_target_pairs={{0,2},{1,3},{2,0},{3,1},{4,6},{5,7},{6,4},{7,5},{8,10},{9,11},{10,... | collective-permute-start | bytes 399368 | tf_op jit(solution)/shard_map/ppermute | solution.py:551
  9.7 11.2 %collective-permute-start.2 = (bf16[520,128]{1,0:T(8,128)(2,1)S(1)}, bf16[520,128]{1,0:T(8,128)(2,1)S(1)}, u32[]{:S(2)}, u32[]{:S(2)}) collective-permute-start(bf16[520,128]{1,0:T(8,128)(2,1)S(1)} %get-tuple-element.37), channel_id=1, source_target_pairs={{0,1},{1,0},{2,3},{3,2},{4,5},{5,4},{6,7},{7,6},{8,9},{9,8},{10,11... | collective-permute-start | bytes 399368 | tf_op jit(solution)/shard_map/ppermute | solution.py:551
  21.8 6.8 %collective-permute-start.5 = (bf16[512,128]{1,0:T(8,128)(2,1)S(1)}, bf16[512,128]{1,0:T(8,128)(2,1)S(1)}, u32[]{:S(2)}, u32[]{:S(2)}) collective-permute-start(bf16[512,128]{1,0:T(8,128)(2,1)S(1)} %get-tuple-element.47.a0_ref), channel_id=1, source_target_pairs={{0,12},{4,8},{8,4},{12,0},{1,13},{5,9},{9,5},{13,1},{2,14},{6,10},... | collective-permute-start | bytes 393224 | tf_op jit(solution)/shard_map/ppermute | solution.py:551
  24.3 5.8 %collective-permute-start.4 = (bf16[512,128]{1,0:T(8,128)(2,1)S(1)}, bf16[512,128]{1,0:T(8,128)(2,1)S(1)}, u32[]{:S(2)}, u32[]{:S(2)}) collective-permute-start(bf16[512,128]{1,0:T(8,128)(2,1)S(1)} %get-tuple-element.47.a0_ref), channel_id=1, source_target_pairs={{0,8},{4,12},{8,0},{12,4},{1,9},{5,13},{9,1},{13,5},{2,10},{6,14},... | collective-permute-start | bytes 393224 | tf_op jit(solution)/shard_map/ppermute | solution.py:551
  24.8 5.4 %collective-permute-start.3 = (bf16[512,128]{1,0:T(8,128)(2,1)S(1)}, bf16[512,128]{1,0:T(8,128)(2,1)S(1)}, u32[]{:S(2)}, u32[]{:S(2)}) collective-permute-start(bf16[512,128]{1,0:T(8,128)(2,1)S(1)} %get-tuple-element.47.a0_ref), channel_id=1, source_target_pairs={{0,4},{4,0},{8,12},{12,8},{1,5},{5,1},{9,13},{13,9},{2,6},{6,2},{1... | collective-permute-start | bytes 393224 | tf_op jit(solution)/shard_map/ppermute | solution.py:551
  25.3 4.9 %copy-start = (bf16[1,512,2048]{2,1,0:T(8,128)(2,1)S(1)}, bf16[1,512,2048]{2,1,0:T(8,128)(2,1)}, u32[]{:S(2)}) copy-start(bf16[1,512,2048]{2,1,0:T(8,128)(2,1)} %tokens_ref.3) | copy-start | bytes 6291460
  30.6 6.1 %copy-start.1 = (bf16[2048,128]{1,0:T(8,128)(2,1)S(1)}, bf16[2048,128]{1,0:T(8,128)(2,1)}, u32[]{:S(2)}) copy-start(bf16[2048,128]{1,0:T(8,128)(2,1)} %w_ref.1) | copy-start | bytes 1572868
  30.6 1.6 %collective-permute-start.6 = (bf16[4,128,256]{2,1,0:T(8,128)(2,1)S(1)}, bf16[4,128,256]{2,1,0:T(8,128)(2,1)S(1)}, u32[]{:S(2)}, u32[]{:S(2)}) collective-permute-start(bf16[4,128,256]{2,1,0:T(8,128)(2,1)S(1)} %get-tuple-element.61), channel_id=1, source_target_pairs={{0,16},{16,0},{1,17},{17,1},{2,18},{18,2},{3,19},{19,3},{4,20},{20... | collective-permute-start | bytes 786440 | tf_op jit(solution)/shard_map/ppermute | solution.py:551
  32.2 7.0 %collective-permute-start.7 = (bf16[128,256]{1,0:T(8,128)(2,1)S(1)}, bf16[128,256]{1,0:T(8,128)(2,1)S(1)}, u32[]{:S(2)}, u32[]{:S(2)}) collective-permute-start(bf16[128,256]{1,0:T(8,128)(2,1)S(1)} %get-tuple-element.63), channel_id=1, source_target_pairs={{0,3},{1,2},{2,1},{3,0},{4,7},{5,6},{6,5},{7,4},{8,11},{9,10},{10,... | collective-permute-start | bytes 196616 | tf_op jit(solution)/shard_map/ppermute | solution.py:551
  34.6 6.4 %collective-permute-start.8 = (bf16[128,256]{1,0:T(8,128)(2,1)S(1)}, bf16[128,256]{1,0:T(8,128)(2,1)S(1)}, u32[]{:S(2)}, u32[]{:S(2)}) collective-permute-start(bf16[128,256]{1,0:T(8,128)(2,1)S(1)} %get-tuple-element.64), channel_id=1, source_target_pairs={{0,2},{1,3},{2,0},{3,1},{4,6},{5,7},{6,4},{7,5},{8,10},{9,11},{10,... | collective-permute-start | bytes 196616 | tf_op jit(solution)/shard_map/ppermute | solution.py:551
  34.6 6.4 %collective-permute-start.9 = (bf16[128,256]{1,0:T(8,128)(2,1)S(1)}, bf16[128,256]{1,0:T(8,128)(2,1)S(1)}, u32[]{:S(2)}, u32[]{:S(2)}) collective-permute-start(bf16[128,256]{1,0:T(8,128)(2,1)S(1)} %get-tuple-element.65), channel_id=1, source_target_pairs={{0,1},{1,0},{2,3},{3,2},{4,5},{5,4},{6,7},{7,6},{8,9},{9,8},{10,11... | collective-permute-start | bytes 196616 | tf_op jit(solution)/shard_map/ppermute | solution.py:551

commit v5 on v4

--- a/solution.py
+++ b/solution.py
@@ -12,7 +12,7 @@
 VMEM_SPEC = pl.BlockSpec(memory_space=pltpu.VMEM)
 SMEM_SPEC = pl.BlockSpec(memory_space=pltpu.SMEM)
 LANES = 128
-ORDER_A = (3, 2, 1)
+ORDER_A = (2, 1, 3)
 ORDER_B = (3, 2, 1)
 ORDER_C = (3, 2, 1)
 

time: 41.9 us -> 41.5 us (level)
  waiting for transfers between devices: 11.6 us -> 9.76 us
  starting transfers between devices: 13.8 us -> 15.3 us
    ppermute x10, waiting for transfers between devices: 11.6 us -> 9.76 us  [swap(): lax.ppermute(value, axis, [(i, i ^ k) for i in range(lax.axis_size(axis))])]
    ppermute x10, starting transfers between devices: 13.8 us -> 15.3 us  [swap(): lax.ppermute(value, axis, [(i, i ^ k) for i in range(lax.axis_size(axis))])]
  transfers between devices with their start and end apart: 10 -> 10, of which waited for: 6 -> 8; matrix products, arithmetic and copies ran while one was open for 0% -> 0% of each run, Pallas kernels for 23% -> 23%
where the time goes in v5:
time: 41.5 us; the launch traced here: 41.4 us
  Pallas kernels  15.6 us (38%)
  starting transfers between devices  15.3 us (37%)
  waiting for transfers between devices  9.76 us (24%)
  between operations  0.74 us (2%)
    ppermute x10, starting transfers between devices, swap(): lax.ppermute(value, axis, [(i, i ^ k) for i in range(lax.axis_size(axis))])  15.3 us
    ppermute x10, waiting for transfers between devices, swap(): lax.ppermute(value, axis, [(i, i ^ k) for i in range(lax.axis_size(axis))])  9.76 us
    pallas_call x1, Pallas kernels, inside_chunks(): pl.pallas_call(local_kernel, name='inside_chunks', in_specs=[VMEM_SPEC] *...  5.17 us
    pallas_call x1, Pallas kernels, block_states(): pl.pallas_call(functools.partial(states_kernel, n_seq), name='block_state...  3.94 us
    pallas_call x1, Pallas kernels, input_grad(): pl.pallas_call(input_kernel, name='input_grad', grid=(steps,), in_specs=[...  2.49 us
    pallas_call x1, Pallas kernels, add_carries(): pl.pallas_call(carry_kernel, name='add_carries', grid=(CHUNKS,), in_specs...  1.68 us
  transfers between devices with their start and end apart: 10, of which 8 were waited for; matrix products, arithmetic and copies ran while one was open for 0% of the time, Pallas kernels for 23%

profile of v5, /device:TPU:0, one launch (start us, length us, event | category | flops | bytes accessed | tf_op | source)
XLA Modules:
  0.0 41.4 jit_solution(6748197086544282419)
XLA Ops:
  0.6 0.0 copy-start.3
  0.6 0.0 copy-start.2
  0.7 0.0 copy-start.4
  0.7 3.9 %block_states.1 = (bf16[512,128]{1,0:T(8,128)(2,1)S(1)}, bf16[512,128]{1,0:T(8,128)(2,1)S(1)}, f32[4,8,512]{2,1,0:T(8,128)S(1)}, bf16[64,512]{1,0:T(8,128)(2,1)S...) custom-call(bf16[1,512,2048]{2,1,0:T(8,128)(2,1)} %tokens_ref.3, ...), custom_call_target="tpu_custom_call" | custom-call | flops 268435456 | bytes 5242880 | tf_op jit(solution)/shard_map/block_states/pallas_call | solution.py:180
  4.6 4.1 %collective-permute-start = (bf16[520,128]{1,0:T(8,128)(2,1)S(1)}, bf16[520,128]{1,0:T(8,128)(2,1)S(1)}, u32[]{:S(2)}, u32[]{:S(2)}) collective-permute-start(bf16[520,128]{1,0:T(8,128)(2,1)S(1)} %get-tuple-element.35), channel_id=1, source_target_pairs={{0,2},{1,3},{2,0},{3,1},{4,6},{5,7},{6,4},{7,5},{8,10},{9,11},{10,... | collective-permute-start | bytes 399368 | tf_op jit(solution)/shard_map/ppermute | solution.py:551
  8.7 1.6 %collective-permute-start.1 = (bf16[520,128]{1,0:T(8,128)(2,1)S(1)}, bf16[520,128]{1,0:T(8,128)(2,1)S(1)}, u32[]{:S(2)}, u32[]{:S(2)}) collective-permute-start(bf16[520,128]{1,0:T(8,128)(2,1)S(1)} %get-tuple-element.36), channel_id=1, source_target_pairs={{0,1},{1,0},{2,3},{3,2},{4,5},{5,4},{6,7},{7,6},{8,9},{9,8},{10,11... | collective-permute-start | bytes 399368 | tf_op jit(solution)/shard_map/ppermute | solution.py:551
  10.3 0.0 collective-permute-start.2
  10.3 5.2 %inside_chunks.1 = (f32[512,512]{1,0:T(8,128)S(1)}, f32[512,512]{1,0:T(8,128)S(1)}, f32[512,128]{1,0:T(8,128)S(1)}, bf16[512,2048]{1,0:T(8,128)(2,1)S(1)}) custom-call(bf16[1,512,512]{2,1,0:T(8,128)(2,1)S(1)} %copy-done.2, bf16[1,512,512]{2,1,0:T(8,128)(2,1)S(1)} %copy-done.3, bf16[512,128]{1,0:T(8,128)(2,1)S(1)} %get-tuple-element.41.bc_ref, ...), custom_call_target="tpu_custom_call" | custom-call | flops 805306368 | bytes 4194304 | tf_op jit(solution)/shard_map/inside_chunks/pallas_call | solution.py:292
  15.5 1.3 %collective-permute-done.refs_0_ = bf16[520,128]{1,0:T(8,128)(2,1)S(1)} collective-permute-done((bf16[520,128]{1,0:T(8,128)(2,1)S(1)}, bf16[520,128]{1,0:T(8,128)(2,1)S(1)}, u32[]{:S(2)}, u32[]{:S(2)}) %collective-permute-start) | collective-permute-done | bytes 133152 | tf_op jit(solution)/shard_map/ppermute | solution.py:551
  16.8 0.0 collective-permute-done.1.refs_1_
  16.8 2.4 %collective-permute-done.2.refs_2_ = bf16[520,128]{1,0:T(8,128)(2,1)S(1)} collective-permute-done((bf16[520,128]{1,0:T(8,128)(2,1)S(1)}, bf16[520,128]{1,0:T(8,128)(2,1)S(1)}, u32[]{:S(2)}, u32[]{:S(2)}) %collective-permute-start.2) | collective-permute-done | bytes 133152 | tf_op jit(solution)/shard_map/ppermute | solution.py:551
  19.2 0.8 %group_sums.1 = (bf16[512,128]{1,0:T(8,128)(2,1)S(1)}, bf16[2,128,512]{2,1,0:T(8,128)(2,1)S(1)}, bf16[2,128,512]{2,1,0:T(8,128)(2,1)S(1)}) custom-call(bf16[520,128]{1,0:T(8,128)(2,1)S(1)} %collective-permute-done.refs_0_, bf16[520,128]{1,0:T(8,128)(2,1)S(1)} %collective-permute-done.1.refs_1_, bf16[520,128]{1,0:T(8,128)(2,1)S(1)} %collective-permute-done.2.refs_2_, ...), custom_call_target="tpu_custom_call" | custom-call | flops 268435456 | bytes 3145728 | tf_op jit(solution)/shard_map/group_sums/pallas_call | solution.py:365
  20.0 2.5 %collective-permute-start.5 = (bf16[512,128]{1,0:T(8,128)(2,1)S(1)}, bf16[512,128]{1,0:T(8,128)(2,1)S(1)}, u32[]{:S(2)}, u32[]{:S(2)}) collective-permute-start(bf16[512,128]{1,0:T(8,128)(2,1)S(1)} %get-tuple-element.47.a0_ref), channel_id=1, source_target_pairs={{0,12},{4,8},{8,4},{12,0},{1,13},{5,9},{9,5},{13,1},{2,14},{6,10},... | collective-permute-start | bytes 393224 | tf_op jit(solution)/shard_map/ppermute | solution.py:551
  22.5 0.5 %collective-permute-start.4 = (bf16[512,128]{1,0:T(8,128)(2,1)S(1)}, bf16[512,128]{1,0:T(8,128)(2,1)S(1)}, u32[]{:S(2)}, u32[]{:S(2)}) collective-permute-start(bf16[512,128]{1,0:T(8,128)(2,1)S(1)} %get-tuple-element.47.a0_ref), channel_id=1, source_target_pairs={{0,8},{4,12},{8,0},{12,4},{1,9},{5,13},{9,1},{13,5},{2,10},{6,14},... | collective-permute-start | bytes 393224 | tf_op jit(solution)/shard_map/ppermute | solution.py:551
  23.0 0.5 %collective-permute-start.3 = (bf16[512,128]{1,0:T(8,128)(2,1)S(1)}, bf16[512,128]{1,0:T(8,128)(2,1)S(1)}, u32[]{:S(2)}, u32[]{:S(2)}) collective-permute-start(bf16[512,128]{1,0:T(8,128)(2,1)S(1)} %get-tuple-element.47.a0_ref), channel_id=1, source_target_pairs={{0,4},{4,0},{8,12},{12,8},{1,5},{5,1},{9,13},{13,9},{2,6},{6,2},{1... | collective-permute-start | bytes 393224 | tf_op jit(solution)/shard_map/ppermute | solution.py:551
  23.5 1.7 %add_carries.1 = (bf16[1,512,512]{2,1,0:T(8,128)(2,1)}, bf16[1,512,512]{2,1,0:T(8,128)(2,1)}) custom-call(bf16[2,128,512]{2,1,0:T(8,128)(2,1)S(1)} %get-tuple-element.48.before_ref, bf16[2,128,512]{2,1,0:T(8,128)(2,1)S(1)} %get-tuple-element.49.after_ref, bf16[512,2048]{1,0:T(8,128)(2,1)S(1)} %get-tuple-element.50.queries_ref, ...), custom_call_target="tpu_custom_call" | custom-call | flops 268435456 | bytes 5242880 | tf_op jit(solution)/shard_map/add_carries/pallas_call | solution.py:407
  25.2 1.8 %collective-permute-done.5.a3_ref = bf16[512,128]{1,0:T(8,128)(2,1)S(1)} collective-permute-done((bf16[512,128]{1,0:T(8,128)(2,1)S(1)}, bf16[512,128]{1,0:T(8,128)(2,1)S(1)}, u32[]{:S(2)}, u32[]{:S(2)}) %collective-permute-start.5) | collective-permute-done | bytes 131104 | tf_op jit(solution)/shard_map/ppermute | solution.py:551
  27.0 1.0 %collective-permute-done.4.a2_ref = bf16[512,128]{1,0:T(8,128)(2,1)S(1)} collective-permute-done((bf16[512,128]{1,0:T(8,128)(2,1)S(1)}, bf16[512,128]{1,0:T(8,128)(2,1)S(1)}, u32[]{:S(2)}, u32[]{:S(2)}) %collective-permute-start.4) | collective-permute-done | bytes 131104 | tf_op jit(solution)/shard_map/ppermute | solution.py:551
  28.0 0.1 collective-permute-done.3.a1_ref
  28.1 0.4 weight_away.1
  28.5 0.0 copy-start.1
  28.5 0.1 collective-permute-start.6
  28.6 0.3 weight_home.1.keep_ref
  28.9 1.2 %collective-permute-done.6.got_ref = bf16[4,128,256]{2,1,0:T(8,128)(2,1)S(1)} collective-permute-done((bf16[4,128,256]{2,1,0:T(8,128)(2,1)S(1)}, bf16[4,128,256]{2,1,0:T(8,128)(2,1)S(1)}, u32[]{:S(2)}, u32[]{:S(2)}) %collective-permute-start.6) | collective-permute-done | bytes 262176 | tf_op jit(solution)/shard_map/ppermute | solution.py:551
  30.2 2.5 %collective-permute-start.7 = (bf16[128,256]{1,0:T(8,128)(2,1)S(1)}, bf16[128,256]{1,0:T(8,128)(2,1)S(1)}, u32[]{:S(2)}, u32[]{:S(2)}) collective-permute-start(bf16[128,256]{1,0:T(8,128)(2,1)S(1)} %get-tuple-element.63), channel_id=1, source_target_pairs={{0,3},{1,2},{2,1},{3,0},{4,7},{5,6},{6,5},{7,4},{8,11},{9,10},{10,... | collective-permute-start | bytes 196616 | tf_op jit(solution)/shard_map/ppermute | solution.py:551
  32.6 3.1 %collective-permute-start.8 = (bf16[128,256]{1,0:T(8,128)(2,1)S(1)}, bf16[128,256]{1,0:T(8,128)(2,1)S(1)}, u32[]{:S(2)}, u32[]{:S(2)}) collective-permute-start(bf16[128,256]{1,0:T(8,128)(2,1)S(1)} %get-tuple-element.64), channel_id=1, source_target_pairs={{0,2},{1,3},{2,0},{3,1},{4,6},{5,7},{6,4},{7,5},{8,10},{9,11},{10,... | collective-permute-start | bytes 196616 | tf_op jit(solution)/shard_map/ppermute | solution.py:551
  35.7 0.5 %collective-permute-start.9 = (bf16[128,256]{1,0:T(8,128)(2,1)S(1)}, bf16[128,256]{1,0:T(8,128)(2,1)S(1)}, u32[]{:S(2)}, u32[]{:S(2)}) collective-permute-start(bf16[128,256]{1,0:T(8,128)(2,1)S(1)} %get-tuple-element.65), channel_id=1, source_target_pairs={{0,1},{1,0},{2,3},{3,2},{4,5},{5,4},{6,7},{7,6},{8,9},{9,8},{10,11... | collective-permute-start | bytes 196616 | tf_op jit(solution)/shard_map/ppermute | solution.py:551
  36.2 2.5 %input_grad.1 = bf16[1,512,2048]{2,1,0:T(8,128)(2,1)} custom-call(bf16[512,128]{1,0:T(8,128)(2,1)S(1)} %get-tuple-element.59.grad_ref, bf16[2048,128]{1,0:T(8,128)(2,1)S(1)} %copy-done.1), custom_call_target="tpu_custom_call" | custom-call | flops 268435456 | bytes 3145728 | tf_op jit(solution)/shard_map/input_grad/pallas_call | solution.py:538
  38.7 0.0 collective-permute-done.7.r3_ref
  38.7 1.5 %collective-permute-done.8.r2_ref = bf16[128,256]{1,0:T(8,128)(2,1)S(1)} collective-permute-done((bf16[128,256]{1,0:T(8,128)(2,1)S(1)}, bf16[128,256]{1,0:T(8,128)(2,1)S(1)}, u32[]{:S(2)}, u32[]{:S(2)}) %collective-permute-start.8) | collective-permute-done | bytes 65568 | tf_op jit(solution)/shard_map/ppermute | solution.py:551
  40.2 0.4 %collective-permute-done.9.r1_ref = bf16[128,256]{1,0:T(8,128)(2,1)S(1)} collective-permute-done((bf16[128,256]{1,0:T(8,128)(2,1)S(1)}, bf16[128,256]{1,0:T(8,128)(2,1)S(1)}, u32[]{:S(2)}, u32[]{:S(2)}) %collective-permute-start.9) | collective-permute-done | bytes 65568 | tf_op jit(solution)/shard_map/ppermute | solution.py:551
  40.6 0.8 %final_sum.1 = f32[256,128]{1,0:T(8,128)} custom-call(f32[128,256]{1,0:T(8,128)S(1)} %get-tuple-element.62.own_ref, bf16[128,256]{1,0:T(8,128)(2,1)S(1)} %collective-permute-done.7.r3_ref, bf16[128,256]{1,0:T(8,128)(2,1)S(1)} %collective-permute-done.8.r2_ref, bf16[128,256]{1,0:T(8,128)(2,1)S(1)} %collective-permute-done.9.r1_ref), custom_call_target="tpu_custom_call" | custom-call | tf_op jit(solution)/shard_map/final_sum/pallas_call | solution.py:519
  (7 shorter events, 0.1 us)
Async XLA Ops:
  0.6 9.7 %copy-start.3 = (bf16[1,512,512]{2,1,0:T(8,128)(2,1)S(1)}, bf16[1,512,512]{2,1,0:T(8,128)(2,1)}, u32[]{:S(2)}) copy-start(bf16[1,512,512]{2,1,0:T(8,128)(2,1)} %g_ref.1) | copy-start | bytes 1572868
  0.6 9.7 %copy-start.2 = (bf16[1,512,512]{2,1,0:T(8,128)(2,1)S(1)}, bf16[1,512,512]{2,1,0:T(8,128)(2,1)}, u32[]{:S(2)}) copy-start(bf16[1,512,512]{2,1,0:T(8,128)(2,1)} %x_ref.1) | copy-start | bytes 1572868
  0.7 9.7 %copy-start.4 = (f32[8]{0:T(128)S(1)}, f32[8]{0:T(128)}, u32[]{:S(2)}) copy-start(f32[8]{0:T(128)} %skip_ref.1) | copy-start | bytes 100
  4.6 12.2 %collective-permute-start = (bf16[520,128]{1,0:T(8,128)(2,1)S(1)}, bf16[520,128]{1,0:T(8,128)(2,1)S(1)}, u32[]{:S(2)}, u32[]{:S(2)}) collective-permute-start(bf16[520,128]{1,0:T(8,128)(2,1)S(1)} %get-tuple-element.35), channel_id=1, source_target_pairs={{0,2},{1,3},{2,0},{3,1},{4,6},{5,7},{6,4},{7,5},{8,10},{9,11},{10,... | collective-permute-start | bytes 399368 | tf_op jit(solution)/shard_map/ppermute | solution.py:551
  8.7 8.1 %collective-permute-start.1 = (bf16[520,128]{1,0:T(8,128)(2,1)S(1)}, bf16[520,128]{1,0:T(8,128)(2,1)S(1)}, u32[]{:S(2)}, u32[]{:S(2)}) collective-permute-start(bf16[520,128]{1,0:T(8,128)(2,1)S(1)} %get-tuple-element.36), channel_id=1, source_target_pairs={{0,1},{1,0},{2,3},{3,2},{4,5},{5,4},{6,7},{7,6},{8,9},{9,8},{10,11... | collective-permute-start | bytes 399368 | tf_op jit(solution)/shard_map/ppermute | solution.py:551
  10.3 8.9 %collective-permute-start.2 = (bf16[520,128]{1,0:T(8,128)(2,1)S(1)}, bf16[520,128]{1,0:T(8,128)(2,1)S(1)}, u32[]{:S(2)}, u32[]{:S(2)}) collective-permute-start(bf16[520,128]{1,0:T(8,128)(2,1)S(1)} %get-tuple-element.37), channel_id=1, source_target_pairs={{0,3},{1,2},{2,1},{3,0},{4,7},{5,6},{6,5},{7,4},{8,11},{9,10},{10,... | collective-permute-start | bytes 399368 | tf_op jit(solution)/shard_map/ppermute | solution.py:551
  20.0 7.1 %collective-permute-start.5 = (bf16[512,128]{1,0:T(8,128)(2,1)S(1)}, bf16[512,128]{1,0:T(8,128)(2,1)S(1)}, u32[]{:S(2)}, u32[]{:S(2)}) collective-permute-start(bf16[512,128]{1,0:T(8,128)(2,1)S(1)} %get-tuple-element.47.a0_ref), channel_id=1, source_target_pairs={{0,12},{4,8},{8,4},{12,0},{1,13},{5,9},{9,5},{13,1},{2,14},{6,10},... | collective-permute-start | bytes 393224 | tf_op jit(solution)/shard_map/ppermute | solution.py:551
  22.5 5.6 %collective-permute-start.4 = (bf16[512,128]{1,0:T(8,128)(2,1)S(1)}, bf16[512,128]{1,0:T(8,128)(2,1)S(1)}, u32[]{:S(2)}, u32[]{:S(2)}) collective-permute-start(bf16[512,128]{1,0:T(8,128)(2,1)S(1)} %get-tuple-element.47.a0_ref), channel_id=1, source_target_pairs={{0,8},{4,12},{8,0},{12,4},{1,9},{5,13},{9,1},{13,5},{2,10},{6,14},... | collective-permute-start | bytes 393224 | tf_op jit(solution)/shard_map/ppermute | solution.py:551
  23.0 5.1 %collective-permute-start.3 = (bf16[512,128]{1,0:T(8,128)(2,1)S(1)}, bf16[512,128]{1,0:T(8,128)(2,1)S(1)}, u32[]{:S(2)}, u32[]{:S(2)}) collective-permute-start(bf16[512,128]{1,0:T(8,128)(2,1)S(1)} %get-tuple-element.47.a0_ref), channel_id=1, source_target_pairs={{0,4},{4,0},{8,12},{12,8},{1,5},{5,1},{9,13},{13,9},{2,6},{6,2},{1... | collective-permute-start | bytes 393224 | tf_op jit(solution)/shard_map/ppermute | solution.py:551
  23.5 4.6 %copy-start = (bf16[1,512,2048]{2,1,0:T(8,128)(2,1)S(1)}, bf16[1,512,2048]{2,1,0:T(8,128)(2,1)}, u32[]{:S(2)}) copy-start(bf16[1,512,2048]{2,1,0:T(8,128)(2,1)} %tokens_ref.3) | copy-start | bytes 6291460
  28.5 7.7 %copy-start.1 = (bf16[2048,128]{1,0:T(8,128)(2,1)S(1)}, bf16[2048,128]{1,0:T(8,128)(2,1)}, u32[]{:S(2)}) copy-start(bf16[2048,128]{1,0:T(8,128)(2,1)} %w_ref.1) | copy-start | bytes 1572868
  28.5 1.6 %collective-permute-start.6 = (bf16[4,128,256]{2,1,0:T(8,128)(2,1)S(1)}, bf16[4,128,256]{2,1,0:T(8,128)(2,1)S(1)}, u32[]{:S(2)}, u32[]{:S(2)}) collective-permute-start(bf16[4,128,256]{2,1,0:T(8,128)(2,1)S(1)} %get-tuple-element.61), channel_id=1, source_target_pairs={{0,16},{16,0},{1,17},{17,1},{2,18},{18,2},{3,19},{19,3},{4,20},{20... | collective-permute-start | bytes 786440 | tf_op jit(solution)/shard_map/ppermute | solution.py:551
  30.2 8.5 %collective-permute-start.7 = (bf16[128,256]{1,0:T(8,128)(2,1)S(1)}, bf16[128,256]{1,0:T(8,128)(2,1)S(1)}, u32[]{:S(2)}, u32[]{:S(2)}) collective-permute-start(bf16[128,256]{1,0:T(8,128)(2,1)S(1)} %get-tuple-element.63), channel_id=1, source_target_pairs={{0,3},{1,2},{2,1},{3,0},{4,7},{5,6},{6,5},{7,4},{8,11},{9,10},{10,... | collective-permute-start | bytes 196616 | tf_op jit(solution)/shard_map/ppermute | solution.py:551
  32.6 7.6 %collective-permute-start.8 = (bf16[128,256]{1,0:T(8,128)(2,1)S(1)}, bf16[128,256]{1,0:T(8,128)(2,1)S(1)}, u32[]{:S(2)}, u32[]{:S(2)}) collective-permute-start(bf16[128,256]{1,0:T(8,128)(2,1)S(1)} %get-tuple-element.64), channel_id=1, source_target_pairs={{0,2},{1,3},{2,0},{3,1},{4,6},{5,7},{6,4},{7,5},{8,10},{9,11},{10,... | collective-permute-start | bytes 196616 | tf_op jit(solution)/shard_map/ppermute | solution.py:551
  35.7 4.9 %collective-permute-start.9 = (bf16[128,256]{1,0:T(8,128)(2,1)S(1)}, bf16[128,256]{1,0:T(8,128)(2,1)S(1)}, u32[]{:S(2)}, u32[]{:S(2)}) collective-permute-start(bf16[128,256]{1,0:T(8,128)(2,1)S(1)} %get-tuple-element.65), channel_id=1, source_target_pairs={{0,1},{1,0},{2,3},{3,2},{4,5},{5,4},{6,7},{7,6},{8,9},{9,8},{10,11... | collective-permute-start | bytes 196616 | tf_op jit(solution)/shard_map/ppermute | solution.py:551

commit v6 on v5

--- a/solution.py
+++ b/solution.py
@@ -64,7 +64,7 @@
 def states_kernel(
     n_seq, tokens_hbm, x_hbm, g_hbm, dt_hbm, w_hbm, rate_hbm, bias_hbm,
     bc_ref, cb_ref, rows_ref, decs_ref, spread_ref, scaled_ref, near_ref, coef_ref, pay1_ref, pay2_ref, pay3_ref,
-    tok_ref, x_ref, g_ref, dt_ref, w_ref, rate_ref, bias_ref, sems,
+    x_ref, g_ref, tok_ref, w_ref, dt_ref, rate_ref, bias_ref, sems,
 ):
     heads, length = dt_ref.shape
     chunk = length // CHUNKS
@@ -181,7 +181,7 @@
         functools.partial(states_kernel, n_seq),
         name="block_states",
         in_specs=[HBM_SPEC] * 7,
-        out_specs=[VMEM_SPEC] * 11,
+        out_specs=[VMEM_SPEC] * 15,
         out_shape=[
             jax.ShapeDtypeStruct((length, two_n), BF16),
             jax.ShapeDtypeStruct((length, two_n), BF16),
@@ -194,13 +194,13 @@
             pay,
             pay,
             pay,
+            jax.ShapeDtypeStruct((length, width), BF16),
+            jax.ShapeDtypeStruct((length, width), BF16),
+            jax.ShapeDtypeStruct((length, depth), BF16),
+            jax.ShapeDtypeStruct((depth, two_n), BF16),
         ],
         scratch_shapes=[
-            pltpu.VMEM((length, depth), BF16),
-            pltpu.VMEM((length, width), BF16),
-            pltpu.VMEM((length, width), BF16),
             pltpu.VMEM((heads, length), F32),
-            pltpu.VMEM((depth, two_n), BF16),
             pltpu.SMEM((heads,), F32),
             pltpu.SMEM((heads,), F32),
             pltpu.SemaphoreType.DMA((8,)),
@@ -214,7 +214,7 @@
     x_ref, g_ref, bc_ref, cb_ref, rows_ref, decs_ref, spread_ref, skip_ref,
     y_ref, gv_ref, gbc_ref, queries_ref, gvt_ref, gbt_ref, gc_ref,
 ):
-    length, width = x_ref.shape[1:]
+    length, width = x_ref.shape
     lanes = 128
     n_pair = width // lanes
     chunk = length // CHUNKS
@@ -238,9 +238,9 @@
             total = None
             for p in range(n_pair):
                 at = slice(p * lanes, (p + 1) * lanes)
-                xp = x_ref[0, pl.ds(s0, chunk), at]
+                xp = x_ref[pl.ds(s0, chunk), at]
                 x1, x2 = jnp.where(first_half, xp, zero), jnp.where(first_half, zero, xp)
-                g_t = g_ref[0, pl.ds(t0, tile), at]
+                g_t = g_ref[pl.ds(t0, tile), at]
                 gt = g_t.astype(F32).T.astype(BF16)
                 cols = rows_ref[p, :, pl.ds(t0, tile)].T
                 mains = []
@@ -256,14 +256,14 @@
                     total = term if total is None else total + term
                 sk = jnp.where(first_half, skip_ref[2 * p], skip_ref[2 * p + 1])
                 y = mm(mains[0], x1) + mm(mains[1], x2)
-                y_ref[pl.ds(t0, tile), at] = y + sk * x_ref[0, pl.ds(t0, tile), at].astype(F32)
+                y_ref[pl.ds(t0, tile), at] = y + sk * x_ref[pl.ds(t0, tile), at].astype(F32)
                 gvt = mm(jnp.where(upper, gt, zero), mains[0]) + mm(jnp.where(upper, zero, gt), mains[1])
                 if tb == 0:
                     gvt_ref[p] = gvt
                 elif tb < chunk // tile - 1:
                     gvt_ref[p] += gvt
                 else:
-                    gs = g_ref[0, pl.ds(s0, chunk), at].astype(F32)
+                    gs = g_ref[pl.ds(s0, chunk), at].astype(F32)
                     gv_ref[pl.ds(s0, chunk), at] = (gvt_ref[p] + gvt).T + sk * gs
             total = total.astype(BF16)
             gc_ref[tb * tile : (tb + 1) * tile] = mm(total, cb_ref[pl.ds(s0, chunk), :])
@@ -286,7 +286,7 @@
 
 
 def inside_chunks(x, g, bc, cb, rows, decs, spread, skip):
-    _, length, width = x.shape
+    length, width = x.shape
     n_pair = width // 128
     chunk = length // CHUNKS
     return pl.pallas_call(
@@ -443,7 +443,7 @@
     n_seq, _, cols = send_ref.shape
     for s in range(n_seq):
         away = pl.multiple_of(((1 - here) * n_seq + s) * cols, cols)
-        send_ref[s] = mm(grad_t, tokens_ref[0, :, pl.ds(away, cols)]).astype(BF16)
+        send_ref[s] = mm(grad_t, tokens_ref[:, pl.ds(away, cols)]).astype(BF16)
 
 
 def home_kernel(grad_t_ref, tokens_ref, keep_ref):
@@ -451,11 +451,11 @@
     n_seq, _, cols = keep_ref.shape
     for s in range(n_seq):
         home = pl.multiple_of((here * n_seq + s) * cols, cols)
-        keep_ref[s] = mm(grad_t_ref[...], tokens_ref[0, :, pl.ds(home, cols)])
+        keep_ref[s] = mm(grad_t_ref[...], tokens_ref[:, pl.ds(home, cols)])
 
 
 def weight_away(n_seq, groups, tokens):
-    _, length, depth = tokens.shape
+    length, depth = tokens.shape
     two_n = groups[0].shape[1]
     cols = depth // (2 * n_seq)
     return pl.pallas_call(
@@ -474,7 +474,7 @@
 
 
 def weight_home(n_seq, grad_t, tokens):
-    _, length, depth = tokens.shape
+    length, depth = tokens.shape
     two_n = grad_t.shape[0]
     cols = depth // (2 * n_seq)
     return pl.pallas_call(
@@ -555,7 +555,7 @@
     n_seq, n_head, n_dp = lax.axis_size("seq"), lax.axis_size("head"), lax.axis_size("dp")
     length = layer_input.shape[1]
     two_n = w_bc.shape[1]
-    bc, cb, rows, decs, spread, scaled, near, coef, pay1, pay2, pay3 = block_states(
+    bc, cb, rows, decs, spread, scaled, near, coef, pay1, pay2, pay3, x, g, tokens, w = block_states(
         n_seq, layer_input, head_values, grad_y, dt_raw, w_bc, decay_rate, dt_bias
     )
     direct = n_seq == 4
@@ -564,7 +564,7 @@
     else:
         received = scanned_generic(pay1, pay2, two_n)
     y_local, gv_local, gbc_local, queries = inside_chunks(
-        head_values, grad_y, bc, cb, rows, decs, spread, skip_gain
+        x, g, bc, cb, rows, decs, spread, skip_gain
     )
     group, before, after = group_sums(direct, received, near, coef, scaled, gbc_local)
     total_tokens = n_dp * n_seq * length
@@ -573,18 +573,18 @@
         y_out, grad_values = add_carries(before, after, queries, y_local, gv_local)
         *others, y_out = lax.optimization_barrier((*others, y_out))
         groups = [group, *others]
-        grad_bc, grad_t, send = weight_away(n_seq, groups, layer_input)
+        grad_bc, grad_t, send = weight_away(n_seq, groups, tokens)
         got = swap(send, "dp", 1)
-        keep = weight_home(n_seq, grad_t, layer_input)
+        keep = weight_home(n_seq, grad_t, tokens)
         own, s1, s2, s3 = pair_sum(keep, got)
         sums = [swap((s1, s2, s3)[k - 1], "seq", k) for k in ORDER_C]
         grad_w_bc = final_sum(1.0 / total_tokens, own, *sums)
     else:
         y_out, grad_values = add_carries(before, after, queries, y_local, gv_local)
         grad_bc = lax.psum(group.astype(F32), "head").astype(BF16)
-        part = jnp.einsum("td,tk->dk", layer_input[0], grad_bc, preferred_element_type=F32)
+        part = jnp.einsum("td,tk->dk", tokens, grad_bc, preferred_element_type=F32)
         grad_w_bc = lax.psum_scatter(part, ("dp", "seq"), scatter_dimension=0, tiled=True) / total_tokens
-    grad_input = input_grad(grad_bc, w_bc)
+    grad_input = input_grad(grad_bc, w)
     return y_out, grad_values, grad_input, grad_w_bc
 
 

time: 41.5 us -> 41.5 us (level)
  no operation moved by 1% of the time
where the time goes in v6:
time: 41.5 us; the launch traced here: 41.4 us
  Pallas kernels  15.5 us (37%)
  starting transfers between devices  15.3 us (37%)
  waiting for transfers between devices  9.86 us (24%)
  between operations  0.7 us (2%)
    ppermute x10, starting transfers between devices, swap(): lax.ppermute(value, axis, [(i, i ^ k) for i in range(lax.axis_size(axis))])  15.3 us
    ppermute x10, waiting for transfers between devices, swap(): lax.ppermute(value, axis, [(i, i ^ k) for i in range(lax.axis_size(axis))])  9.86 us
    pallas_call x1, Pallas kernels, inside_chunks(): pl.pallas_call(local_kernel, name='inside_chunks', in_specs=[VMEM_SPEC] *...  5.11 us
    pallas_call x1, Pallas kernels, block_states(): pl.pallas_call(functools.partial(states_kernel, n_seq), name='block_state...  3.94 us
    pallas_call x1, Pallas kernels, input_grad(): pl.pallas_call(input_kernel, name='input_grad', grid=(steps,), in_specs=[...  2.49 us
    pallas_call x1, Pallas kernels, add_carries(): pl.pallas_call(carry_kernel, name='add_carries', grid=(CHUNKS,), in_specs...  1.66 us
  transfers between devices with their start and end apart: 10, of which 8 were waited for; matrix products, arithmetic and copies ran while one was open for 0% of the time, Pallas kernels for 23%

profile of v6, /device:TPU:0, one launch (start us, length us, event | category | flops | bytes accessed | tf_op | source)
XLA Modules:
  0.0 41.4 jit_solution(7493310664138475005)
XLA Ops:
  0.6 0.0 copy-start
  0.6 3.9 %block_states.1 = (bf16[512,128]{1,0:T(8,128)(2,1)S(1)}, bf16[512,128]{1,0:T(8,128)(2,1)S(1)}, f32[4,8,512]{2,1,0:T(8,128)S(1)}, bf16[64,512]{1,0:T(8,128)(2,1)S...) custom-call(bf16[1,512,2048]{2,1,0:T(8,128)(2,1)} %tokens_hbm.1, ...), custom_call_target="tpu_custom_call" | custom-call | flops 268435456 | bytes 5242880 | tf_op jit(solution)/shard_map/block_states/pallas_call | solution.py:180
  4.6 4.1 %collective-permute-start = (bf16[520,128]{1,0:T(8,128)(2,1)S(1)}, bf16[520,128]{1,0:T(8,128)(2,1)S(1)}, u32[]{:S(2)}, u32[]{:S(2)}) collective-permute-start(bf16[520,128]{1,0:T(8,128)(2,1)S(1)} %get-tuple-element.39), channel_id=1, source_target_pairs={{0,2},{1,3},{2,0},{3,1},{4,6},{5,7},{6,4},{7,5},{8,10},{9,11},{10,... | collective-permute-start | bytes 399368 | tf_op jit(solution)/shard_map/ppermute | solution.py:551
  8.7 1.6 %collective-permute-start.1 = (bf16[520,128]{1,0:T(8,128)(2,1)S(1)}, bf16[520,128]{1,0:T(8,128)(2,1)S(1)}, u32[]{:S(2)}, u32[]{:S(2)}) collective-permute-start(bf16[520,128]{1,0:T(8,128)(2,1)S(1)} %get-tuple-element.40), channel_id=1, source_target_pairs={{0,1},{1,0},{2,3},{3,2},{4,5},{5,4},{6,7},{7,6},{8,9},{9,8},{10,11... | collective-permute-start | bytes 399368 | tf_op jit(solution)/shard_map/ppermute | solution.py:551
  10.3 0.0 collective-permute-start.2
  10.3 0.0 copy-done
  10.3 5.1 %inside_chunks.1 = (f32[512,512]{1,0:T(8,128)S(1)}, f32[512,512]{1,0:T(8,128)S(1)}, f32[512,128]{1,0:T(8,128)S(1)}, bf16[512,2048]{1,0:T(8,128)(2,1)S(1)}) custom-call(bf16[512,512]{1,0:T(8,128)(2,1)S(1)} %get-tuple-element.45.x_ref, bf16[512,512]{1,0:T(8,128)(2,1)S(1)} %get-tuple-element.46.g_ref, bf16[512,128]{1,0:T(8,128)(2,1)S(1)} %get-tuple-element.47.bc_ref, ...), custom_call_target="tpu_custom_call" | custom-call | flops 805306368 | bytes 4194304 | tf_op jit(solution)/shard_map/inside_chunks/pallas_call | solution.py:292
  15.4 1.4 %collective-permute-done.refs_0_ = bf16[520,128]{1,0:T(8,128)(2,1)S(1)} collective-permute-done((bf16[520,128]{1,0:T(8,128)(2,1)S(1)}, bf16[520,128]{1,0:T(8,128)(2,1)S(1)}, u32[]{:S(2)}, u32[]{:S(2)}) %collective-permute-start) | collective-permute-done | bytes 133152 | tf_op jit(solution)/shard_map/ppermute | solution.py:551
  16.8 0.0 collective-permute-done.1.refs_1_
  16.8 2.4 %collective-permute-done.2.refs_2_ = bf16[520,128]{1,0:T(8,128)(2,1)S(1)} collective-permute-done((bf16[520,128]{1,0:T(8,128)(2,1)S(1)}, bf16[520,128]{1,0:T(8,128)(2,1)S(1)}, u32[]{:S(2)}, u32[]{:S(2)}) %collective-permute-start.2) | collective-permute-done | bytes 133152 | tf_op jit(solution)/shard_map/ppermute | solution.py:551
  19.1 0.8 %group_sums.1 = (bf16[512,128]{1,0:T(8,128)(2,1)S(1)}, bf16[2,128,512]{2,1,0:T(8,128)(2,1)S(1)}, bf16[2,128,512]{2,1,0:T(8,128)(2,1)S(1)}) custom-call(bf16[520,128]{1,0:T(8,128)(2,1)S(1)} %collective-permute-done.refs_0_, bf16[520,128]{1,0:T(8,128)(2,1)S(1)} %collective-permute-done.1.refs_1_, bf16[520,128]{1,0:T(8,128)(2,1)S(1)} %collective-permute-done.2.refs_2_, ...), custom_call_target="tpu_custom_call" | custom-call | flops 268435456 | bytes 3145728 | tf_op jit(solution)/shard_map/group_sums/pallas_call | solution.py:365
  19.9 2.5 %collective-permute-start.5 = (bf16[512,128]{1,0:T(8,128)(2,1)S(1)}, bf16[512,128]{1,0:T(8,128)(2,1)S(1)}, u32[]{:S(2)}, u32[]{:S(2)}) collective-permute-start(bf16[512,128]{1,0:T(8,128)(2,1)S(1)} %get-tuple-element.53.a0_ref), channel_id=1, source_target_pairs={{0,12},{4,8},{8,4},{12,0},{1,13},{5,9},{9,5},{13,1},{2,14},{6,10},... | collective-permute-start | bytes 393224 | tf_op jit(solution)/shard_map/ppermute | solution.py:551
  22.5 0.5 %collective-permute-start.4 = (bf16[512,128]{1,0:T(8,128)(2,1)S(1)}, bf16[512,128]{1,0:T(8,128)(2,1)S(1)}, u32[]{:S(2)}, u32[]{:S(2)}) collective-permute-start(bf16[512,128]{1,0:T(8,128)(2,1)S(1)} %get-tuple-element.53.a0_ref), channel_id=1, source_target_pairs={{0,8},{4,12},{8,0},{12,4},{1,9},{5,13},{9,1},{13,5},{2,10},{6,14},... | collective-permute-start | bytes 393224 | tf_op jit(solution)/shard_map/ppermute | solution.py:551
  23.0 0.5 %collective-permute-start.3 = (bf16[512,128]{1,0:T(8,128)(2,1)S(1)}, bf16[512,128]{1,0:T(8,128)(2,1)S(1)}, u32[]{:S(2)}, u32[]{:S(2)}) collective-permute-start(bf16[512,128]{1,0:T(8,128)(2,1)S(1)} %get-tuple-element.53.a0_ref), channel_id=1, source_target_pairs={{0,4},{4,0},{8,12},{12,8},{1,5},{5,1},{9,13},{13,9},{2,6},{6,2},{1... | collective-permute-start | bytes 393224 | tf_op jit(solution)/shard_map/ppermute | solution.py:551
  23.5 1.7 %add_carries.1 = (bf16[1,512,512]{2,1,0:T(8,128)(2,1)}, bf16[1,512,512]{2,1,0:T(8,128)(2,1)}) custom-call(bf16[2,128,512]{2,1,0:T(8,128)(2,1)S(1)} %get-tuple-element.54.before_ref, bf16[2,128,512]{2,1,0:T(8,128)(2,1)S(1)} %get-tuple-element.55.after_ref, bf16[512,2048]{1,0:T(8,128)(2,1)S(1)} %get-tuple-element.56.queries_ref, ...), custom_call_target="tpu_custom_call" | custom-call | flops 268435456 | bytes 5242880 | tf_op jit(solution)/shard_map/add_carries/pallas_call | solution.py:407
  25.2 1.8 %collective-permute-done.5.a3_ref = bf16[512,128]{1,0:T(8,128)(2,1)S(1)} collective-permute-done((bf16[512,128]{1,0:T(8,128)(2,1)S(1)}, bf16[512,128]{1,0:T(8,128)(2,1)S(1)}, u32[]{:S(2)}, u32[]{:S(2)}) %collective-permute-start.5) | collective-permute-done | bytes 131104 | tf_op jit(solution)/shard_map/ppermute | solution.py:551
  27.0 1.0 %collective-permute-done.4.a2_ref = bf16[512,128]{1,0:T(8,128)(2,1)S(1)} collective-permute-done((bf16[512,128]{1,0:T(8,128)(2,1)S(1)}, bf16[512,128]{1,0:T(8,128)(2,1)S(1)}, u32[]{:S(2)}, u32[]{:S(2)}) %collective-permute-start.4) | collective-permute-done | bytes 131104 | tf_op jit(solution)/shard_map/ppermute | solution.py:551
  28.0 0.1 collective-permute-done.3.a1_ref
  28.1 0.4 weight_away.1
  28.5 0.1 collective-permute-start.6
  28.6 0.3 weight_home.1.keep_ref
  28.9 1.2 %collective-permute-done.6.got_ref = bf16[4,128,256]{2,1,0:T(8,128)(2,1)S(1)} collective-permute-done((bf16[4,128,256]{2,1,0:T(8,128)(2,1)S(1)}, bf16[4,128,256]{2,1,0:T(8,128)(2,1)S(1)}, u32[]{:S(2)}, u32[]{:S(2)}) %collective-permute-start.6) | collective-permute-done | bytes 262176 | tf_op jit(solution)/shard_map/ppermute | solution.py:551
  30.1 2.5 %collective-permute-start.7 = (bf16[128,256]{1,0:T(8,128)(2,1)S(1)}, bf16[128,256]{1,0:T(8,128)(2,1)S(1)}, u32[]{:S(2)}, u32[]{:S(2)}) collective-permute-start(bf16[128,256]{1,0:T(8,128)(2,1)S(1)} %get-tuple-element.71), channel_id=1, source_target_pairs={{0,3},{1,2},{2,1},{3,0},{4,7},{5,6},{6,5},{7,4},{8,11},{9,10},{10,... | collective-permute-start | bytes 196616 | tf_op jit(solution)/shard_map/ppermute | solution.py:551
  32.6 3.1 %collective-permute-start.8 = (bf16[128,256]{1,0:T(8,128)(2,1)S(1)}, bf16[128,256]{1,0:T(8,128)(2,1)S(1)}, u32[]{:S(2)}, u32[]{:S(2)}) collective-permute-start(bf16[128,256]{1,0:T(8,128)(2,1)S(1)} %get-tuple-element.72), channel_id=1, source_target_pairs={{0,2},{1,3},{2,0},{3,1},{4,6},{5,7},{6,4},{7,5},{8,10},{9,11},{10,... | collective-permute-start | bytes 196616 | tf_op jit(solution)/shard_map/ppermute | solution.py:551
  35.7 0.5 %collective-permute-start.9 = (bf16[128,256]{1,0:T(8,128)(2,1)S(1)}, bf16[128,256]{1,0:T(8,128)(2,1)S(1)}, u32[]{:S(2)}, u32[]{:S(2)}) collective-permute-start(bf16[128,256]{1,0:T(8,128)(2,1)S(1)} %get-tuple-element.73), channel_id=1, source_target_pairs={{0,1},{1,0},{2,3},{3,2},{4,5},{5,4},{6,7},{7,6},{8,9},{9,8},{10,11... | collective-permute-start | bytes 196616 | tf_op jit(solution)/shard_map/ppermute | solution.py:551
  36.1 2.5 %input_grad.1 = bf16[1,512,2048]{2,1,0:T(8,128)(2,1)} custom-call(bf16[512,128]{1,0:T(8,128)(2,1)S(1)} %get-tuple-element.66.grad_ref, bf16[2048,128]{1,0:T(8,128)(2,1)S(1)} %get-tuple-element.67.w_ref), custom_call_target="tpu_custom_call" | custom-call | flops 268435456 | bytes 3145728 | tf_op jit(solution)/shard_map/input_grad/pallas_call | solution.py:538
  38.6 0.0 collective-permute-done.7.r3_ref
  38.6 1.5 %collective-permute-done.8.r2_ref = bf16[128,256]{1,0:T(8,128)(2,1)S(1)} collective-permute-done((bf16[128,256]{1,0:T(8,128)(2,1)S(1)}, bf16[128,256]{1,0:T(8,128)(2,1)S(1)}, u32[]{:S(2)}, u32[]{:S(2)}) %collective-permute-start.8) | collective-permute-done | bytes 65568 | tf_op jit(solution)/shard_map/ppermute | solution.py:551
  40.2 0.4 %collective-permute-done.9.r1_ref = bf16[128,256]{1,0:T(8,128)(2,1)S(1)} collective-permute-done((bf16[128,256]{1,0:T(8,128)(2,1)S(1)}, bf16[128,256]{1,0:T(8,128)(2,1)S(1)}, u32[]{:S(2)}, u32[]{:S(2)}) %collective-permute-start.9) | collective-permute-done | bytes 65568 | tf_op jit(solution)/shard_map/ppermute | solution.py:551
  40.6 0.8 %final_sum.1 = f32[256,128]{1,0:T(8,128)} custom-call(f32[128,256]{1,0:T(8,128)S(1)} %get-tuple-element.70.own_ref, bf16[128,256]{1,0:T(8,128)(2,1)S(1)} %collective-permute-done.7.r3_ref, bf16[128,256]{1,0:T(8,128)(2,1)S(1)} %collective-permute-done.8.r2_ref, bf16[128,256]{1,0:T(8,128)(2,1)S(1)} %collective-permute-done.9.r1_ref), custom_call_target="tpu_custom_call" | custom-call | tf_op jit(solution)/shard_map/final_sum/pallas_call | solution.py:519
  (1 shorter events, 0.0 us)
Async XLA Ops:
  0.6 9.6 %copy-start = (f32[8]{0:T(128)S(1)}, f32[8]{0:T(128)}, u32[]{:S(2)}) copy-start(f32[8]{0:T(128)} %skip_ref.1) | copy-start | bytes 100
  4.6 12.2 %collective-permute-start = (bf16[520,128]{1,0:T(8,128)(2,1)S(1)}, bf16[520,128]{1,0:T(8,128)(2,1)S(1)}, u32[]{:S(2)}, u32[]{:S(2)}) collective-permute-start(bf16[520,128]{1,0:T(8,128)(2,1)S(1)} %get-tuple-element.39), channel_id=1, source_target_pairs={{0,2},{1,3},{2,0},{3,1},{4,6},{5,7},{6,4},{7,5},{8,10},{9,11},{10,... | collective-permute-start | bytes 399368 | tf_op jit(solution)/shard_map/ppermute | solution.py:551
  8.7 8.1 %collective-permute-start.1 = (bf16[520,128]{1,0:T(8,128)(2,1)S(1)}, bf16[520,128]{1,0:T(8,128)(2,1)S(1)}, u32[]{:S(2)}, u32[]{:S(2)}) collective-permute-start(bf16[520,128]{1,0:T(8,128)(2,1)S(1)} %get-tuple-element.40), channel_id=1, source_target_pairs={{0,1},{1,0},{2,3},{3,2},{4,5},{5,4},{6,7},{7,6},{8,9},{9,8},{10,11... | collective-permute-start | bytes 399368 | tf_op jit(solution)/shard_map/ppermute | solution.py:551
  10.3 8.9 %collective-permute-start.2 = (bf16[520,128]{1,0:T(8,128)(2,1)S(1)}, bf16[520,128]{1,0:T(8,128)(2,1)S(1)}, u32[]{:S(2)}, u32[]{:S(2)}) collective-permute-start(bf16[520,128]{1,0:T(8,128)(2,1)S(1)} %get-tuple-element.41), channel_id=1, source_target_pairs={{0,3},{1,2},{2,1},{3,0},{4,7},{5,6},{6,5},{7,4},{8,11},{9,10},{10,... | collective-permute-start | bytes 399368 | tf_op jit(solution)/shard_map/ppermute | solution.py:551
  19.9 7.0 %collective-permute-start.5 = (bf16[512,128]{1,0:T(8,128)(2,1)S(1)}, bf16[512,128]{1,0:T(8,128)(2,1)S(1)}, u32[]{:S(2)}, u32[]{:S(2)}) collective-permute-start(bf16[512,128]{1,0:T(8,128)(2,1)S(1)} %get-tuple-element.53.a0_ref), channel_id=1, source_target_pairs={{0,12},{4,8},{8,4},{12,0},{1,13},{5,9},{9,5},{13,1},{2,14},{6,10},... | collective-permute-start | bytes 393224 | tf_op jit(solution)/shard_map/ppermute | solution.py:551
  22.5 5.6 %collective-permute-start.4 = (bf16[512,128]{1,0:T(8,128)(2,1)S(1)}, bf16[512,128]{1,0:T(8,128)(2,1)S(1)}, u32[]{:S(2)}, u32[]{:S(2)}) collective-permute-start(bf16[512,128]{1,0:T(8,128)(2,1)S(1)} %get-tuple-element.53.a0_ref), channel_id=1, source_target_pairs={{0,8},{4,12},{8,0},{12,4},{1,9},{5,13},{9,1},{13,5},{2,10},{6,14},... | collective-permute-start | bytes 393224 | tf_op jit(solution)/shard_map/ppermute | solution.py:551
  23.0 5.1 %collective-permute-start.3 = (bf16[512,128]{1,0:T(8,128)(2,1)S(1)}, bf16[512,128]{1,0:T(8,128)(2,1)S(1)}, u32[]{:S(2)}, u32[]{:S(2)}) collective-permute-start(bf16[512,128]{1,0:T(8,128)(2,1)S(1)} %get-tuple-element.53.a0_ref), channel_id=1, source_target_pairs={{0,4},{4,0},{8,12},{12,8},{1,5},{5,1},{9,13},{13,9},{2,6},{6,2},{1... | collective-permute-start | bytes 393224 | tf_op jit(solution)/shard_map/ppermute | solution.py:551
  28.5 1.6 %collective-permute-start.6 = (bf16[4,128,256]{2,1,0:T(8,128)(2,1)S(1)}, bf16[4,128,256]{2,1,0:T(8,128)(2,1)S(1)}, u32[]{:S(2)}, u32[]{:S(2)}) collective-permute-start(bf16[4,128,256]{2,1,0:T(8,128)(2,1)S(1)} %get-tuple-element.69), channel_id=1, source_target_pairs={{0,16},{16,0},{1,17},{17,1},{2,18},{18,2},{3,19},{19,3},{4,20},{20... | collective-permute-start | bytes 786440 | tf_op jit(solution)/shard_map/ppermute | solution.py:551
  30.1 8.5 %collective-permute-start.7 = (bf16[128,256]{1,0:T(8,128)(2,1)S(1)}, bf16[128,256]{1,0:T(8,128)(2,1)S(1)}, u32[]{:S(2)}, u32[]{:S(2)}) collective-permute-start(bf16[128,256]{1,0:T(8,128)(2,1)S(1)} %get-tuple-element.71), channel_id=1, source_target_pairs={{0,3},{1,2},{2,1},{3,0},{4,7},{5,6},{6,5},{7,4},{8,11},{9,10},{10,... | collective-permute-start | bytes 196616 | tf_op jit(solution)/shard_map/ppermute | solution.py:551
  32.6 7.6 %collective-permute-start.8 = (bf16[128,256]{1,0:T(8,128)(2,1)S(1)}, bf16[128,256]{1,0:T(8,128)(2,1)S(1)}, u32[]{:S(2)}, u32[]{:S(2)}) collective-permute-start(bf16[128,256]{1,0:T(8,128)(2,1)S(1)} %get-tuple-element.72), channel_id=1, source_target_pairs={{0,2},{1,3},{2,0},{3,1},{4,6},{5,7},{6,4},{7,5},{8,10},{9,11},{10,... | collective-permute-start | bytes 196616 | tf_op jit(solution)/shard_map/ppermute | solution.py:551
  35.7 4.9 %collective-permute-start.9 = (bf16[128,256]{1,0:T(8,128)(2,1)S(1)}, bf16[128,256]{1,0:T(8,128)(2,1)S(1)}, u32[]{:S(2)}, u32[]{:S(2)}) collective-permute-start(bf16[128,256]{1,0:T(8,128)(2,1)S(1)} %get-tuple-element.73), channel_id=1, source_target_pairs={{0,1},{1,0},{2,3},{3,2},{4,5},{5,4},{6,7},{7,6},{8,9},{9,8},{10,11... | collective-permute-start | bytes 196616 | tf_op jit(solution)/shard_map/ppermute | solution.py:551

commit v7 on v6

--- a/solution.py
+++ b/solution.py
@@ -59,6 +59,10 @@
     tail = payload[blocks * rows :].astype(F32)
     decay = jnp.concatenate([tail[p : p + 1] + tail[blocks + p : blocks + p + 1] for p in range(blocks)], axis=1)
     return state, decay
+
+
+def mm_rows(a, b):
+    return lax.dot_general(a, b, (((0,), (0,)), ((), ())), preferred_element_type=F32)
 
 
 def states_kernel(
@@ -130,10 +134,10 @@
     copies[4].wait()
     for q in range(CHUNKS):
         at = slice(q * chunk, (q + 1) * chunk)
-        spread_decs = decs[:, at].T.astype(BF16)
+        chunk_decs = decs[:, at].astype(BF16)
         for j, (ref, kind) in enumerate(((g_ref, 0), (g_ref, 1), (x_ref, 2), (x_ref, 3))):
             to = slice(j * width, (j + 1) * width)
-            scaled_ref[at, to] = (ref[at].astype(F32) * mm(spread_decs, spread[:, to])).astype(BF16)
+            scaled_ref[at, to] = (ref[at].astype(F32) * mm_rows(chunk_decs, spread[:, to])).astype(BF16)
     copies[5].wait()
     onward, backward = [], []
     for q in range(CHUNKS):
@@ -144,7 +148,7 @@
         bc_ref[at] = projected.astype(BF16)
         turned = pltpu.roll(projected, half, 1)
         cb_ref[at] = turned.astype(BF16)
-        cb_t = turned.T.astype(BF16)
+        cb_t = turned.astype(BF16).T
         parts = [scaled_ref[at, j * width : (j + 1) * width] for j in range(4)]
         onward.append(jnp.concatenate([mm(cb_t[:half], parts[1]), mm(cb_t[half:], parts[3])], axis=0))
         backward.append(jnp.concatenate([mm(cb_t[:half], parts[0]), mm(cb_t[half:], parts[2])], axis=0))

time: 41.5 us -> 41.5 us (level)
  no operation moved by 1% of the time
where the time goes in v7:
time: 41.5 us; the launch traced here: 41.3 us
  Pallas kernels  15.5 us (37%)
  starting transfers between devices  15.3 us (37%)
  waiting for transfers between devices  9.87 us (24%)
  between operations  0.7 us (2%)
    ppermute x10, starting transfers between devices, swap(): lax.ppermute(value, axis, [(i, i ^ k) for i in range(lax.axis_size(axis))])  15.3 us
    ppermute x10, waiting for transfers between devices, swap(): lax.ppermute(value, axis, [(i, i ^ k) for i in range(lax.axis_size(axis))])  9.87 us
    pallas_call x1, Pallas kernels, inside_chunks(): pl.pallas_call(local_kernel, name='inside_chunks', in_specs=[VMEM_SPEC] *...  5.11 us
    pallas_call x1, Pallas kernels, block_states(): pl.pallas_call(functools.partial(states_kernel, n_seq), name='block_state...  3.92 us
    pallas_call x1, Pallas kernels, input_grad(): pl.pallas_call(input_kernel, name='input_grad', grid=(steps,), in_specs=[...  2.49 us
    pallas_call x1, Pallas kernels, add_carries(): pl.pallas_call(carry_kernel, name='add_carries', grid=(CHUNKS,), in_specs...  1.66 us
  transfers between devices with their start and end apart: 10, of which 8 were waited for; matrix products, arithmetic and copies ran while one was open for 0% of the time, Pallas kernels for 23%

profile of v7, /device:TPU:0, one launch (start us, length us, event | category | flops | bytes accessed | tf_op | source)
XLA Modules:
  0.0 41.3 jit_solution(13819680112028998843)
XLA Ops:
  0.6 0.0 copy-start
  0.6 3.9 %block_states.1 = (bf16[512,128]{1,0:T(8,128)(2,1)S(1)}, bf16[512,128]{1,0:T(8,128)(2,1)S(1)}, f32[4,8,512]{2,1,0:T(8,128)S(1)}, bf16[64,512]{1,0:T(8,128)(2,1)S...) custom-call(bf16[1,512,2048]{2,1,0:T(8,128)(2,1)} %tokens_hbm.1, ...), custom_call_target="tpu_custom_call" | custom-call | flops 268435456 | bytes 5242880 | tf_op jit(solution)/shard_map/block_states/pallas_call | solution.py:184
  4.6 4.1 %collective-permute-start = (bf16[520,128]{1,0:T(8,128)(2,1)S(1)}, bf16[520,128]{1,0:T(8,128)(2,1)S(1)}, u32[]{:S(2)}, u32[]{:S(2)}) collective-permute-start(bf16[520,128]{1,0:T(8,128)(2,1)S(1)} %get-tuple-element.39), channel_id=1, source_target_pairs={{0,2},{1,3},{2,0},{3,1},{4,6},{5,7},{6,4},{7,5},{8,10},{9,11},{10,... | collective-permute-start | bytes 399368 | tf_op jit(solution)/shard_map/ppermute | solution.py:555
  8.7 1.6 %collective-permute-start.1 = (bf16[520,128]{1,0:T(8,128)(2,1)S(1)}, bf16[520,128]{1,0:T(8,128)(2,1)S(1)}, u32[]{:S(2)}, u32[]{:S(2)}) collective-permute-start(bf16[520,128]{1,0:T(8,128)(2,1)S(1)} %get-tuple-element.40), channel_id=1, source_target_pairs={{0,1},{1,0},{2,3},{3,2},{4,5},{5,4},{6,7},{7,6},{8,9},{9,8},{10,11... | collective-permute-start | bytes 399368 | tf_op jit(solution)/shard_map/ppermute | solution.py:555
  10.2 0.0 collective-permute-start.2
  10.3 0.0 copy-done
  10.3 5.1 %inside_chunks.1 = (f32[512,512]{1,0:T(8,128)S(1)}, f32[512,512]{1,0:T(8,128)S(1)}, f32[512,128]{1,0:T(8,128)S(1)}, bf16[512,2048]{1,0:T(8,128)(2,1)S(1)}) custom-call(bf16[512,512]{1,0:T(8,128)(2,1)S(1)} %get-tuple-element.45.x_ref, bf16[512,512]{1,0:T(8,128)(2,1)S(1)} %get-tuple-element.46.g_ref, bf16[512,128]{1,0:T(8,128)(2,1)S(1)} %get-tuple-element.47.bc_ref, ...), custom_call_target="tpu_custom_call" | custom-call | flops 805306368 | bytes 4194304 | tf_op jit(solution)/shard_map/inside_chunks/pallas_call | solution.py:296
  15.4 1.4 %collective-permute-done.refs_0_ = bf16[520,128]{1,0:T(8,128)(2,1)S(1)} collective-permute-done((bf16[520,128]{1,0:T(8,128)(2,1)S(1)}, bf16[520,128]{1,0:T(8,128)(2,1)S(1)}, u32[]{:S(2)}, u32[]{:S(2)}) %collective-permute-start) | collective-permute-done | bytes 133152 | tf_op jit(solution)/shard_map/ppermute | solution.py:555
  16.7 0.0 collective-permute-done.1.refs_1_
  16.7 2.4 %collective-permute-done.2.refs_2_ = bf16[520,128]{1,0:T(8,128)(2,1)S(1)} collective-permute-done((bf16[520,128]{1,0:T(8,128)(2,1)S(1)}, bf16[520,128]{1,0:T(8,128)(2,1)S(1)}, u32[]{:S(2)}, u32[]{:S(2)}) %collective-permute-start.2) | collective-permute-done | bytes 133152 | tf_op jit(solution)/shard_map/ppermute | solution.py:555
  19.1 0.8 %group_sums.1 = (bf16[512,128]{1,0:T(8,128)(2,1)S(1)}, bf16[2,128,512]{2,1,0:T(8,128)(2,1)S(1)}, bf16[2,128,512]{2,1,0:T(8,128)(2,1)S(1)}) custom-call(bf16[520,128]{1,0:T(8,128)(2,1)S(1)} %collective-permute-done.refs_0_, bf16[520,128]{1,0:T(8,128)(2,1)S(1)} %collective-permute-done.1.refs_1_, bf16[520,128]{1,0:T(8,128)(2,1)S(1)} %collective-permute-done.2.refs_2_, ...), custom_call_target="tpu_custom_call" | custom-call | flops 268435456 | bytes 3145728 | tf_op jit(solution)/shard_map/group_sums/pallas_call | solution.py:369
  19.9 2.5 %collective-permute-start.5 = (bf16[512,128]{1,0:T(8,128)(2,1)S(1)}, bf16[512,128]{1,0:T(8,128)(2,1)S(1)}, u32[]{:S(2)}, u32[]{:S(2)}) collective-permute-start(bf16[512,128]{1,0:T(8,128)(2,1)S(1)} %get-tuple-element.53.a0_ref), channel_id=1, source_target_pairs={{0,12},{4,8},{8,4},{12,0},{1,13},{5,9},{9,5},{13,1},{2,14},{6,10},... | collective-permute-start | bytes 393224 | tf_op jit(solution)/shard_map/ppermute | solution.py:555
  22.4 0.5 %collective-permute-start.4 = (bf16[512,128]{1,0:T(8,128)(2,1)S(1)}, bf16[512,128]{1,0:T(8,128)(2,1)S(1)}, u32[]{:S(2)}, u32[]{:S(2)}) collective-permute-start(bf16[512,128]{1,0:T(8,128)(2,1)S(1)} %get-tuple-element.53.a0_ref), channel_id=1, source_target_pairs={{0,8},{4,12},{8,0},{12,4},{1,9},{5,13},{9,1},{13,5},{2,10},{6,14},... | collective-permute-start | bytes 393224 | tf_op jit(solution)/shard_map/ppermute | solution.py:555
  22.9 0.5 %collective-permute-start.3 = (bf16[512,128]{1,0:T(8,128)(2,1)S(1)}, bf16[512,128]{1,0:T(8,128)(2,1)S(1)}, u32[]{:S(2)}, u32[]{:S(2)}) collective-permute-start(bf16[512,128]{1,0:T(8,128)(2,1)S(1)} %get-tuple-element.53.a0_ref), channel_id=1, source_target_pairs={{0,4},{4,0},{8,12},{12,8},{1,5},{5,1},{9,13},{13,9},{2,6},{6,2},{1... | collective-permute-start | bytes 393224 | tf_op jit(solution)/shard_map/ppermute | solution.py:555
  23.5 1.7 %add_carries.1 = (bf16[1,512,512]{2,1,0:T(8,128)(2,1)}, bf16[1,512,512]{2,1,0:T(8,128)(2,1)}) custom-call(bf16[2,128,512]{2,1,0:T(8,128)(2,1)S(1)} %get-tuple-element.54.before_ref, bf16[2,128,512]{2,1,0:T(8,128)(2,1)S(1)} %get-tuple-element.55.after_ref, bf16[512,2048]{1,0:T(8,128)(2,1)S(1)} %get-tuple-element.56.queries_ref, ...), custom_call_target="tpu_custom_call" | custom-call | flops 268435456 | bytes 5242880 | tf_op jit(solution)/shard_map/add_carries/pallas_call | solution.py:411
  25.1 1.8 %collective-permute-done.5.a3_ref = bf16[512,128]{1,0:T(8,128)(2,1)S(1)} collective-permute-done((bf16[512,128]{1,0:T(8,128)(2,1)S(1)}, bf16[512,128]{1,0:T(8,128)(2,1)S(1)}, u32[]{:S(2)}, u32[]{:S(2)}) %collective-permute-start.5) | collective-permute-done | bytes 131104 | tf_op jit(solution)/shard_map/ppermute | solution.py:555
  27.0 1.0 %collective-permute-done.4.a2_ref = bf16[512,128]{1,0:T(8,128)(2,1)S(1)} collective-permute-done((bf16[512,128]{1,0:T(8,128)(2,1)S(1)}, bf16[512,128]{1,0:T(8,128)(2,1)S(1)}, u32[]{:S(2)}, u32[]{:S(2)}) %collective-permute-start.4) | collective-permute-done | bytes 131104 | tf_op jit(solution)/shard_map/ppermute | solution.py:555
  28.0 0.1 collective-permute-done.3.a1_ref
  28.1 0.4 weight_away.1
  28.5 0.1 collective-permute-start.6
  28.5 0.3 weight_home.1.keep_ref
  28.9 1.2 %collective-permute-done.6.got_ref = bf16[4,128,256]{2,1,0:T(8,128)(2,1)S(1)} collective-permute-done((bf16[4,128,256]{2,1,0:T(8,128)(2,1)S(1)}, bf16[4,128,256]{2,1,0:T(8,128)(2,1)S(1)}, u32[]{:S(2)}, u32[]{:S(2)}) %collective-permute-start.6) | collective-permute-done | bytes 262176 | tf_op jit(solution)/shard_map/ppermute | solution.py:555
  30.1 2.4 %collective-permute-start.7 = (bf16[128,256]{1,0:T(8,128)(2,1)S(1)}, bf16[128,256]{1,0:T(8,128)(2,1)S(1)}, u32[]{:S(2)}, u32[]{:S(2)}) collective-permute-start(bf16[128,256]{1,0:T(8,128)(2,1)S(1)} %get-tuple-element.71), channel_id=1, source_target_pairs={{0,3},{1,2},{2,1},{3,0},{4,7},{5,6},{6,5},{7,4},{8,11},{9,10},{10,... | collective-permute-start | bytes 196616 | tf_op jit(solution)/shard_map/ppermute | solution.py:555
  32.6 3.1 %collective-permute-start.8 = (bf16[128,256]{1,0:T(8,128)(2,1)S(1)}, bf16[128,256]{1,0:T(8,128)(2,1)S(1)}, u32[]{:S(2)}, u32[]{:S(2)}) collective-permute-start(bf16[128,256]{1,0:T(8,128)(2,1)S(1)} %get-tuple-element.72), channel_id=1, source_target_pairs={{0,2},{1,3},{2,0},{3,1},{4,6},{5,7},{6,4},{7,5},{8,10},{9,11},{10,... | collective-permute-start | bytes 196616 | tf_op jit(solution)/shard_map/ppermute | solution.py:555
  35.6 0.5 %collective-permute-start.9 = (bf16[128,256]{1,0:T(8,128)(2,1)S(1)}, bf16[128,256]{1,0:T(8,128)(2,1)S(1)}, u32[]{:S(2)}, u32[]{:S(2)}) collective-permute-start(bf16[128,256]{1,0:T(8,128)(2,1)S(1)} %get-tuple-element.73), channel_id=1, source_target_pairs={{0,1},{1,0},{2,3},{3,2},{4,5},{5,4},{6,7},{7,6},{8,9},{9,8},{10,11... | collective-permute-start | bytes 196616 | tf_op jit(solution)/shard_map/ppermute | solution.py:555
  36.1 2.5 %input_grad.1 = bf16[1,512,2048]{2,1,0:T(8,128)(2,1)} custom-call(bf16[512,128]{1,0:T(8,128)(2,1)S(1)} %get-tuple-element.66.grad_ref, bf16[2048,128]{1,0:T(8,128)(2,1)S(1)} %get-tuple-element.67.w_ref), custom_call_target="tpu_custom_call" | custom-call | flops 268435456 | bytes 3145728 | tf_op jit(solution)/shard_map/input_grad/pallas_call | solution.py:542
  38.6 0.0 collective-permute-done.7.r3_ref
  38.6 1.5 %collective-permute-done.8.r2_ref = bf16[128,256]{1,0:T(8,128)(2,1)S(1)} collective-permute-done((bf16[128,256]{1,0:T(8,128)(2,1)S(1)}, bf16[128,256]{1,0:T(8,128)(2,1)S(1)}, u32[]{:S(2)}, u32[]{:S(2)}) %collective-permute-start.8) | collective-permute-done | bytes 65568 | tf_op jit(solution)/shard_map/ppermute | solution.py:555
  40.2 0.4 %collective-permute-done.9.r1_ref = bf16[128,256]{1,0:T(8,128)(2,1)S(1)} collective-permute-done((bf16[128,256]{1,0:T(8,128)(2,1)S(1)}, bf16[128,256]{1,0:T(8,128)(2,1)S(1)}, u32[]{:S(2)}, u32[]{:S(2)}) %collective-permute-start.9) | collective-permute-done | bytes 65568 | tf_op jit(solution)/shard_map/ppermute | solution.py:555
  40.6 0.8 %final_sum.1 = f32[256,128]{1,0:T(8,128)} custom-call(f32[128,256]{1,0:T(8,128)S(1)} %get-tuple-element.70.own_ref, bf16[128,256]{1,0:T(8,128)(2,1)S(1)} %collective-permute-done.7.r3_ref, bf16[128,256]{1,0:T(8,128)(2,1)S(1)} %collective-permute-done.8.r2_ref, bf16[128,256]{1,0:T(8,128)(2,1)S(1)} %collective-permute-done.9.r1_ref), custom_call_target="tpu_custom_call" | custom-call | tf_op jit(solution)/shard_map/final_sum/pallas_call | solution.py:523
  (1 shorter events, 0.0 us)
Async XLA Ops:
  0.6 9.6 %copy-start = (f32[8]{0:T(128)S(1)}, f32[8]{0:T(128)}, u32[]{:S(2)}) copy-start(f32[8]{0:T(128)} %skip_ref.1) | copy-start | bytes 100
  4.6 12.2 %collective-permute-start = (bf16[520,128]{1,0:T(8,128)(2,1)S(1)}, bf16[520,128]{1,0:T(8,128)(2,1)S(1)}, u32[]{:S(2)}, u32[]{:S(2)}) collective-permute-start(bf16[520,128]{1,0:T(8,128)(2,1)S(1)} %get-tuple-element.39), channel_id=1, source_target_pairs={{0,2},{1,3},{2,0},{3,1},{4,6},{5,7},{6,4},{7,5},{8,10},{9,11},{10,... | collective-permute-start | bytes 399368 | tf_op jit(solution)/shard_map/ppermute | solution.py:555
  8.7 8.1 %collective-permute-start.1 = (bf16[520,128]{1,0:T(8,128)(2,1)S(1)}, bf16[520,128]{1,0:T(8,128)(2,1)S(1)}, u32[]{:S(2)}, u32[]{:S(2)}) collective-permute-start(bf16[520,128]{1,0:T(8,128)(2,1)S(1)} %get-tuple-element.40), channel_id=1, source_target_pairs={{0,1},{1,0},{2,3},{3,2},{4,5},{5,4},{6,7},{7,6},{8,9},{9,8},{10,11... | collective-permute-start | bytes 399368 | tf_op jit(solution)/shard_map/ppermute | solution.py:555
  10.2 8.9 %collective-permute-start.2 = (bf16[520,128]{1,0:T(8,128)(2,1)S(1)}, bf16[520,128]{1,0:T(8,128)(2,1)S(1)}, u32[]{:S(2)}, u32[]{:S(2)}) collective-permute-start(bf16[520,128]{1,0:T(8,128)(2,1)S(1)} %get-tuple-element.41), channel_id=1, source_target_pairs={{0,3},{1,2},{2,1},{3,0},{4,7},{5,6},{6,5},{7,4},{8,11},{9,10},{10,... | collective-permute-start | bytes 399368 | tf_op jit(solution)/shard_map/ppermute | solution.py:555
  19.9 7.0 %collective-permute-start.5 = (bf16[512,128]{1,0:T(8,128)(2,1)S(1)}, bf16[512,128]{1,0:T(8,128)(2,1)S(1)}, u32[]{:S(2)}, u32[]{:S(2)}) collective-permute-start(bf16[512,128]{1,0:T(8,128)(2,1)S(1)} %get-tuple-element.53.a0_ref), channel_id=1, source_target_pairs={{0,12},{4,8},{8,4},{12,0},{1,13},{5,9},{9,5},{13,1},{2,14},{6,10},... | collective-permute-start | bytes 393224 | tf_op jit(solution)/shard_map/ppermute | solution.py:555
  22.4 5.6 %collective-permute-start.4 = (bf16[512,128]{1,0:T(8,128)(2,1)S(1)}, bf16[512,128]{1,0:T(8,128)(2,1)S(1)}, u32[]{:S(2)}, u32[]{:S(2)}) collective-permute-start(bf16[512,128]{1,0:T(8,128)(2,1)S(1)} %get-tuple-element.53.a0_ref), channel_id=1, source_target_pairs={{0,8},{4,12},{8,0},{12,4},{1,9},{5,13},{9,1},{13,5},{2,10},{6,14},... | collective-permute-start | bytes 393224 | tf_op jit(solution)/shard_map/ppermute | solution.py:555
  22.9 5.1 %collective-permute-start.3 = (bf16[512,128]{1,0:T(8,128)(2,1)S(1)}, bf16[512,128]{1,0:T(8,128)(2,1)S(1)}, u32[]{:S(2)}, u32[]{:S(2)}) collective-permute-start(bf16[512,128]{1,0:T(8,128)(2,1)S(1)} %get-tuple-element.53.a0_ref), channel_id=1, source_target_pairs={{0,4},{4,0},{8,12},{12,8},{1,5},{5,1},{9,13},{13,9},{2,6},{6,2},{1... | collective-permute-start | bytes 393224 | tf_op jit(solution)/shard_map/ppermute | solution.py:555
  28.5 1.6 %collective-permute-start.6 = (bf16[4,128,256]{2,1,0:T(8,128)(2,1)S(1)}, bf16[4,128,256]{2,1,0:T(8,128)(2,1)S(1)}, u32[]{:S(2)}, u32[]{:S(2)}) collective-permute-start(bf16[4,128,256]{2,1,0:T(8,128)(2,1)S(1)} %get-tuple-element.69), channel_id=1, source_target_pairs={{0,16},{16,0},{1,17},{17,1},{2,18},{18,2},{3,19},{19,3},{4,20},{20... | collective-permute-start | bytes 786440 | tf_op jit(solution)/shard_map/ppermute | solution.py:555
  30.1 8.5 %collective-permute-start.7 = (bf16[128,256]{1,0:T(8,128)(2,1)S(1)}, bf16[128,256]{1,0:T(8,128)(2,1)S(1)}, u32[]{:S(2)}, u32[]{:S(2)}) collective-permute-start(bf16[128,256]{1,0:T(8,128)(2,1)S(1)} %get-tuple-element.71), channel_id=1, source_target_pairs={{0,3},{1,2},{2,1},{3,0},{4,7},{5,6},{6,5},{7,4},{8,11},{9,10},{10,... | collective-permute-start | bytes 196616 | tf_op jit(solution)/shard_map/ppermute | solution.py:555
  32.6 7.6 %collective-permute-start.8 = (bf16[128,256]{1,0:T(8,128)(2,1)S(1)}, bf16[128,256]{1,0:T(8,128)(2,1)S(1)}, u32[]{:S(2)}, u32[]{:S(2)}) collective-permute-start(bf16[128,256]{1,0:T(8,128)(2,1)S(1)} %get-tuple-element.72), channel_id=1, source_target_pairs={{0,2},{1,3},{2,0},{3,1},{4,6},{5,7},{6,4},{7,5},{8,10},{9,11},{10,... | collective-permute-start | bytes 196616 | tf_op jit(solution)/shard_map/ppermute | solution.py:555
  35.6 4.9 %collective-permute-start.9 = (bf16[128,256]{1,0:T(8,128)(2,1)S(1)}, bf16[128,256]{1,0:T(8,128)(2,1)S(1)}, u32[]{:S(2)}, u32[]{:S(2)}) collective-permute-start(bf16[128,256]{1,0:T(8,128)(2,1)S(1)} %get-tuple-element.73), channel_id=1, source_target_pairs={{0,1},{1,0},{2,3},{3,2},{4,5},{5,4},{6,7},{7,6},{8,9},{9,8},{10,11... | collective-permute-start | bytes 196616 | tf_op jit(solution)/shard_map/ppermute | solution.py:555
